TPU v7x, 32 devices: a whole 2x2x4 slice. The times are simulated.
32 devices in a mesh: group: 4 (over y, x), leaf: 8 (over z, core).
Axes of the slice: x: 2, y: 2, z: 4, core: 2. Of those that a mesh axis runs over, the one named last changes fastest.
Arguments:
- points: bfloat16 [65536, 64], P(('group', 'leaf')), may hold values from -1.1953125 to 1.1953125
- ordering: int32 [32, 2048], P(('group', 'leaf')), may hold values from 0 to 2047, each once within a row
- iterate: float32 [65536, 128], P(('group', 'leaf')), may hold values from -6 to 6
- target: float32 [65536, 128], P(('group', 'leaf')), may hold values from -18 to 18
- step_size: float32 [128], replicated, may hold values from 0.1 to 0.5
- leaf_basis: bfloat16 [65536, 256], P(('group', 'leaf')), may hold values from -0.125 to 0.125
- transfer: bfloat16 [32, 256, 256], P(('group', 'leaf')), may hold values from -0.375 to 0.375
- leaf_skeleton: bfloat16 [32, 256, 64], P(('group', 'leaf')), may hold values from -0.8984375 to 0.8984375
- cluster_skeleton: bfloat16 [4, 256, 64], P('group'), may hold values from -1.1953125 to 1.1953125
- near_table: int32 [32, 8], P(('group', 'leaf')), may hold values from 0 to 1, as said below
- far_table: int32 [32, 8], P(('group', 'leaf')), may hold values from 0 to 1, as said below
- cluster_far: int32 [4, 4], P('group'), may hold values from 0 to 1, as said below
Outputs:
- updated: float32 [65536, 128], P(('group', 'leaf'))
Inputs may be any that keep to these rules, and one draw needn't show every extreme that they name: `near_table`: entries 0 or 1; each leaf's own place is 1; a 1 stands only at places at most 3 away from the leaf's own place; each row has at most 7 ones, and some row exactly 7. `far_table`: entries 0 or 1, never 1 where near_table is 1. `cluster_far`: entries 0 or 1, zero on the diagonal. `ordering`: each row is a permutation.
All inputs are finite; a program needn't handle non-finite values.
Results may differ from a plain program's by a relative error of at most 0.0044.
Values may be sent and summed in bfloat16 or wider, within the bound.
No kernel may reach another device: no remote copies, remote signals or barrier semaphores. Data moves between devices by JAX's collectives and lax.ppermute only.
A program may use at most 128 MiB of HBM per device.

v0:
```python
import math

import jax
import jax.numpy as jnp
from jax import lax
from jax.experimental import pallas as pl
from jax.experimental.pallas import tpu as pltpu
from jax.sharding import PartitionSpec as P


LANES = 128
COLS = 256
ROWS = 1024
FLAG_ROWS = 16
SHIFT = 66.0
LOG2E = math.log2(math.e)
VMEM = pltpu.VMEM
SMEM = pltpu.SMEM
HBM = pltpu.HBM
F32 = jnp.float32
BF16 = jnp.bfloat16


def contract(left, right, dims):
    return lax.dot_general(left, right, (dims, ((), ())), preferred_element_type=F32)


def matmul(left, right):
    return contract(left, right, ((1,), (0,)))


def call(kernel, outs, ins, scratch=(), flops=0, limit=16, aliases=None):
    single = not isinstance(outs, (list, tuple))
    shapes = [outs] if single else list(outs)
    results = pl.pallas_call(
        kernel,
        out_shape=shapes,
        in_specs=[pl.BlockSpec(memory_space=space) for _, space in ins],
        out_specs=[pl.BlockSpec(memory_space=VMEM)] * len(shapes),
        scratch_shapes=list(scratch),
        input_output_aliases=aliases or {},
        compiler_params=pltpu.CompilerParams(vmem_limit_bytes=limit << 20),
        cost_estimate=pl.CostEstimate(
            flops=int(flops), bytes_accessed=sum(a.size * a.dtype.itemsize for a, _ in ins), transcendentals=0
        ),
    )(*[a for a, _ in ins])
    return results[0] if single else results


def shaped(*shape, dtype=BF16):
    return jax.ShapeDtypeStruct(shape, dtype)


class Plan:
    def __init__(self, points, iterate):
        self.n, self.dim = points.shape
        self.rhs = iterate.shape[1]
        self.half = self.n // 2
        self.blocks = self.half // LANES
        self.flags = self.half + self.blocks * self.dim
        self.rows = self.flags + FLAG_ROWS
        self.tile_flops = 2 * self.n * self.n * 512

    def pay(self):
        return shaped(2, self.rows, self.rhs)

    def acc(self):
        return shaped(2, self.n, self.rhs, dtype=F32)

    def left(self):
        return shaped(2, self.n, self.dim)

    def offset_scratch(self):
        return [VMEM((8, self.half), F32)]


def three_parts(value):
    high = value.astype(BF16).astype(F32)
    rest = value - high
    middle = rest.astype(BF16).astype(F32)
    return high, middle, rest - middle


def extended(doubled, left):
    dim, width = doubled.shape
    wide = doubled.astype(F32)
    parts = three_parts(-0.25 * jnp.sum(wide * wide, axis=0, keepdims=True))
    row = lax.broadcasted_iota(jnp.int32, (LANES - dim, width), 0)
    ones, first = (0, 3) if left else (3, 0)
    below = jnp.where((row >= ones) & (row < ones + 3), 1.0, 0.0)
    for k, part in enumerate(parts):
        below = jnp.where(row == first + k, part, below)
    return jnp.concatenate([0.5 * wide if left else wide, below], axis=0)


def small_left(doubled):
    width = doubled.shape[1]
    return jnp.concatenate(
        [extended(doubled[:, k : k + LANES], True).T.astype(BF16) for k in range(0, width, LANES)], axis=0
    )


def doubled_of(ref):
    return (2.0 * ref[0].astype(F32)).astype(BF16)


def left_block(doubled):
    twice = jnp.concatenate([doubled, doubled], axis=0).astype(F32)
    return (0.5 * twice.T)[:, 0 : doubled.shape[0]].astype(BF16)


def doubled_block(plan, ref, b):
    return ref[plan.half + b * plan.dim : plan.half + (b + 1) * plan.dim, :]


def fill_left(plan, out_ref, ref, h):
    for b in range(plan.blocks):
        first = h * plan.half + b * LANES
        out_ref[first : first + LANES, :] = left_block(doubled_block(plan, ref, b))


def norms(doubled):
    wide = doubled.astype(F32)
    return (0.25 * LOG2E) * jnp.sum(wide * wide, axis=0, keepdims=True)


def fill_offset(plan, offset_ref, ref):
    for b in range(plan.blocks):
        offset_ref[0:1, b * LANES : (b + 1) * LANES] = -norms(doubled_block(plan, ref, b)) - SHIFT


def half_tile(plan, acc_ref, left_ref, source_ref, offset_ref):
    for r in range(0, plan.n, ROWS):
        left = left_ref[r : r + ROWS, :]
        total = acc_ref[r : r + ROWS, :]
        for c in range(0, plan.half, COLS):
            cols = slice(c, c + COLS)
            right = jnp.concatenate(
                [doubled_block(plan, source_ref, b) for b in range(c // LANES, (c + COLS) // LANES)], axis=1
            )
            power = matmul(left, right) * LOG2E + offset_ref[0:1, cols]
            total = total + matmul(jnp.exp2(power).astype(BF16), source_ref[cols, :])
        acc_ref[r : r + ROWS, :] = total


def pick(row, place):
    lane = lax.broadcasted_iota(jnp.int32, row.shape, 1)
    return jnp.sum(jnp.where(lane == place, row, 0.0)) > 0


def listed(row_ref, place):
    size = row_ref.shape[1]
    inside = (place >= 0) & (place < size)
    return inside & (row_ref[0, jnp.clip(place, 0, size - 1)] > 0)


def skeleton_rows(rank, dim):
    return (rank // LANES) * dim


def prepare(plan, near_row, iterate, points_t, basis, transfer, leaf_t, cluster_t):
    size = near_row.shape[1]
    n, half, dim = plan.n, plan.half, plan.dim
    rank = basis.shape[1]

    inputs = [points_t, iterate, near_row, leaf_t, cluster_t, basis, transfer]

    def kernel(*refs):
        count = len(inputs)
        sources, (pay_ref, down_ref, up_ref) = refs[:count], refs[count : count + 3]
        points_ref, iterate_ref, near_ref, leaf_ref, cluster_ref, basis_ref, transfer_ref, sems = refs[count + 3 :]
        copies = [
            pltpu.make_async_copy(source, into, sems.at[k])
            for k, (source, into) in enumerate(zip(sources, refs[count + 3 : -1]))
        ]
        for copy in copies:
            copy.start()
        copies[0].wait()
        for h in range(2):
            for b in range(plan.blocks):
                first = h * half + b * LANES
                pay_ref[h, half + b * dim : half + (b + 1) * dim, :] = (
                    2.0 * points_ref[:, first : first + LANES].astype(F32)
                ).astype(BF16)
        copies[1].wait()
        for h in range(2):
            pay_ref[h, 0:half, :] = iterate_ref[h * half : (h + 1) * half, :].astype(BF16)
        for copy in copies[2:]:
            copy.wait()
        lane = lax.broadcasted_iota(jnp.int32, (FLAG_ROWS, LANES), 1)
        row = jnp.zeros((FLAG_ROWS, LANES), F32)
        for k in range(size):
            row = jnp.where(lane == k, near_ref[0, k].astype(F32), row)
        for h in range(2):
            pay_ref[h, plan.flags :, :] = row.astype(BF16)

        def skeleton(ref, out_ref):
            doubled = doubled_of(ref)
            for b in range(rank // LANES):
                out_ref[rank + b * dim : rank + (b + 1) * dim, :] = doubled[:, b * LANES : (b + 1) * LANES]

        skeleton(leaf_ref, down_ref)
        skeleton(cluster_ref, up_ref)
        total = jnp.zeros((rank, plan.rhs), F32)
        for h in range(2):
            total = total + contract(
                basis_ref[h * half : (h + 1) * half, :], pay_ref[h, 0:half, :], ((0,), (0,))
            )
        coef = total.astype(BF16)
        down_ref[0:rank, :] = coef
        up_ref[0:rank, :] = contract(transfer_ref[0], coef, ((0,), (0,))).astype(BF16)

    rows = rank + skeleton_rows(rank, dim)
    return call(
        kernel,
        [plan.pay(), shaped(rows, plan.rhs), shaped(rows, plan.rhs)],
        [(value, HBM) for value in inputs],
        scratch=[(SMEM if value is near_row else VMEM)(value.shape, value.dtype) for value in inputs]
        + [pltpu.SemaphoreType.DMA((len(inputs),))],
        flops=2 * n * rank * plan.rhs,
    )


def own_tile(plan, pay):
    def kernel(pay_ref, acc_ref, left_ref, offset_ref):
        acc_ref[...] = jnp.zeros_like(acc_ref)
        for h in range(2):
            fill_left(plan, left_ref, pay_ref.at[h], h)

        @pl.loop(0, 2)
        def _(h):
            fill_offset(plan, offset_ref, pay_ref.at[h])
            half_tile(plan, acc_ref.at[0], left_ref, pay_ref.at[h], offset_ref)

    return call(
        kernel,
        plan.acc(),
        [(pay, VMEM)],
        scratch=[VMEM(plan.left().shape[1:], BF16)] + plan.offset_scratch(),
        flops=plan.tile_flops,
    )


def pair_tiles(plan, near_row, pay, partner, acc):
    def kernel(near_ref, pay_ref, partner_ref, acc_in, acc_ref, left_ref, row_ref, offset_ref):
        place = lax.axis_index("leaf")
        core = lax.rem(place, 2)
        for h in range(2):
            fill_left(plan, left_ref.at[0], pay_ref.at[h], h)
            fill_left(plan, left_ref.at[1], partner_ref.at[h], h)
        row = partner_ref[0, plan.flags :, :].astype(F32)
        row_ref[...] = row

        @pl.when(listed(near_ref, place + 1 - 2 * core))
        def _():
            fill_offset(plan, offset_ref, partner_ref.at[core])
            half_tile(plan, acc_ref.at[0], left_ref.at[0], partner_ref.at[core], offset_ref)

        @pl.when(pick(row, place))
        def _():
            fill_offset(plan, offset_ref, pay_ref.at[core])
            half_tile(plan, acc_ref.at[1], left_ref.at[1], pay_ref.at[core], offset_ref)

    return call(
        kernel,
        [plan.acc(), plan.left(), shaped(FLAG_ROWS, LANES, dtype=F32)],
        [(near_row, SMEM), (pay, VMEM), (partner, VMEM), (acc, VMEM)],
        scratch=plan.offset_scratch(),
        flops=plan.tile_flops,
        aliases={3: 0},
    )


def side_tiles(plan, near_row, row, left, full, passed, acc, reach, last):
    def kernel(near_ref, row_in, left_ref, full_ref, passed_ref, acc_in, acc_ref, *refs):
        offset_ref = refs[-1]
        place = lax.axis_index("leaf")
        core = lax.rem(place, 2)
        away = 2 * core - 1
        row = row_in[...]
        first = place + away * reach
        second = place - away - away * reach
        for source, at in ((full_ref.at[core], first), (passed_ref.at[core], second)):
            on_mine = listed(near_ref, at)
            on_theirs = pick(row, at)

            @pl.when(on_mine | on_theirs)
            def _():
                fill_offset(plan, offset_ref, source)

            @pl.loop(0, 2)
            def _(t):
                @pl.when(jnp.where(t == 0, on_mine, on_theirs))
                def _():
                    half_tile(plan, acc_ref.at[t], left_ref.at[t], source, offset_ref)

        if last:
            refs[0][...] = acc_ref[1]

    outs = [plan.acc()] + ([shaped(plan.n, plan.rhs, dtype=F32)] if last else [])
    return call(
        kernel,
        outs,
        [(near_row, SMEM), (row, VMEM), (left, VMEM), (full, VMEM), (passed, VMEM), (acc, VMEM)],
        scratch=plan.offset_scratch(),
        flops=2 * plan.tile_flops,
        aliases={5: 0},
    )


def wanted_rows(ordering, target):
    n, rhs = target.shape
    step = 2 * LANES

    def kernel(order_ref, target_hbm, out_ref, target_ref, halves_ref, sem):
        copy = pltpu.make_async_copy(target_hbm, target_ref, sem)
        copy.start()
        copy.wait()
        value = target_ref[...]
        high = value.astype(BF16)
        halves_ref[:, 0:rhs] = high
        halves_ref[:, rhs:] = (value - high.astype(F32)).astype(BF16)
        lane = lax.broadcasted_iota(jnp.int32, (LANES, LANES), 1).astype(F32)

        @pl.loop(0, n // step)
        def _(i):
            picks = []
            for k in range(step // LANES):
                rows = pl.ds(pl.multiple_of(i * step + k * LANES, LANES), LANES)
                index = jnp.broadcast_to(order_ref[:, rows].astype(F32), (LANES, LANES)).T
                picks.append(
                    jnp.concatenate(
                        [jnp.where(index == lane + c, 1.0, 0.0).astype(BF16) for c in range(0, n, LANES)], axis=1
                    )
                )
            both = matmul(jnp.concatenate(picks, axis=0), halves_ref[...])
            out_ref[pl.ds(pl.multiple_of(i * step, step), step), :] = both[:, 0:rhs] + both[:, rhs:]

    return call(
        kernel,
        shaped(n, rhs, dtype=F32),
        [(ordering, VMEM), (target, HBM)],
        scratch=[VMEM((n, rhs), F32), VMEM((n, 2 * rhs), BF16), pltpu.SemaphoreType.DMA],
        flops=n * n * 512,
    )


def last_tile(plan, near_row, pay, left, third, acc, returned, iterate, wanted, step_size, basis, local):
    def kernel(near_ref, pay_ref, left_ref, third_ref, acc_ref, returned_ref, iterate_ref, wanted_ref, step_ref, basis_ref, local_ref, out_ref, offset_ref):
        place = lax.axis_index("leaf")
        away = 2 * lax.rem(place, 2) - 1
        out_ref[...] = acc_ref[0] + returned_ref[...]

        @pl.when(listed(near_ref, place + 3 * away))
        def _():
            @pl.loop(0, 2)
            def _(h):
                fill_offset(plan, offset_ref, third_ref.at[h])
                half_tile(plan, out_ref, left_ref.at[0], third_ref.at[h], offset_ref)

        for h in range(2):
            for b in range(plan.blocks):
                first = h * plan.half + b * LANES
                rows = slice(first, first + LANES)
                power = SHIFT - norms(doubled_block(plan, pay_ref.at[h], b))
                factor = jnp.exp2(jnp.broadcast_to(power, (LANES, LANES)).T)
                image = matmul(basis_ref[rows, :], local_ref[...]) + factor * out_ref[rows, :]
                out_ref[rows, :] = iterate_ref[rows, :] + step_ref[...] * (wanted_ref[rows, :] - image)

    return call(
        kernel,
        shaped(plan.n, plan.rhs, dtype=F32),
        [
            (near_row, SMEM),
            (pay, VMEM),
            (left, VMEM),
            (third, VMEM),
            (acc, VMEM),
            (returned, VMEM),
            (iterate, VMEM),
            (wanted, VMEM),
            (step_size.reshape(1, -1), VMEM),
            (basis, VMEM),
            (local, VMEM),
        ],
        scratch=plan.offset_scratch(),
        flops=plan.tile_flops,
    )


def add_far(total, left, block_ref, first, rank, dim):
    right = jnp.concatenate(
        [
            extended(block_ref[first + rank + b * dim : first + rank + (b + 1) * dim, :], False).astype(BF16)
            for b in range(rank // LANES)
        ],
        axis=1,
    )
    return total + matmul(jnp.exp(matmul(left, right)).astype(BF16), block_ref[first : first + rank, :])


def across(cluster_row, cluster_t, own, others, distances, down_block):
    dim, rank = cluster_t.shape[1:]
    count = len(others)
    rows = down_block.shape[0]

    def kernel(far_ref, skeleton_ref, down_ref, own_ref, *refs):
        out_ref, total_ref = refs[count], refs[count + 1]
        me = lax.axis_index("group")
        left = small_left(doubled_of(skeleton_ref))
        total_ref[...] = jnp.zeros_like(total_ref)
        out_ref[0:rows, :] = down_ref[...]

        def include(at, block_ref):
            @pl.when(far_ref[0, at] > 0)
            def _():
                total_ref[...] = add_far(total_ref[...], left, block_ref, 0, rank, dim)

        include(me, own_ref)
        for k in range(count):
            include(distances(me, k), refs[k])
        out_ref[rows:, :] = total_ref[...].astype(BF16)

    return call(
        kernel,
        shaped(rows + rank, LANES),
        [(cluster_row, SMEM), (cluster_t, VMEM), (down_block, VMEM), (own, VMEM)] + [(o, VMEM) for o in others],
        scratch=[VMEM((rank, LANES), F32)],
        flops=2 * 4 * rank * rank * 512,
    )


def joined(mine, got, rank):
    rows = mine.shape[0] - rank

    def kernel(mine_ref, got_ref, out_ref):
        out_ref[0:rows, :] = mine_ref[0:rows, :]
        out_ref[rows : 2 * rows, :] = got_ref[0:rows, :]
        out_ref[2 * rows :, :] = (mine_ref[rows:, :].astype(F32) + got_ref[rows:, :].astype(F32)).astype(BF16)

    return call(kernel, shaped(2 * rows + rank, LANES), [(mine, VMEM), (got, VMEM)])


def down(far_row, leaf_t, transfer, mine, got, xors):
    dim, rank = leaf_t.shape[1:]
    rows = rank + skeleton_rows(rank, dim)
    count = (mine.shape[0] - rank) // rows

    def kernel(far_ref, skeleton_ref, transfer_ref, mine_ref, got_ref, out_ref, total_ref):
        place = lax.axis_index("leaf")
        left = small_left(doubled_of(skeleton_ref))
        lower = (mine_ref[count * rows :, :].astype(F32) + got_ref[count * rows :, :].astype(F32)).astype(BF16)
        total_ref[...] = matmul(transfer_ref[0], lower)
        for k, other in enumerate(xors):
            block_ref, at = (mine_ref, k) if k < count else (got_ref, k - count)

            @pl.when(far_ref[0, place ^ other] > 0)
            def _():
                total_ref[...] = add_far(total_ref[...], left, block_ref, at * rows, rank, dim)

        out_ref[...] = total_ref[...].astype(BF16)

    return call(
        kernel,
        shaped(rank, LANES),
        [(far_row, SMEM), (leaf_t, VMEM), (transfer, VMEM), (mine, VMEM), (got, VMEM)],
        scratch=[VMEM((rank, LANES), F32)],
        flops=2 * 8 * rank * rank * 512,
    )


def routed(block, axis, target):
    size = lax.axis_size(axis)
    route = [(i, target(i)) for i in range(size) if 0 <= target(i) < size]
    return lax.ppermute(block, axis, route)


def over_chips(i):
    return i + 2 - 4 * (i % 2)


def beside_chips(i):
    return i - 1 + 2 * (i % 2)


def on_chip(i):
    return i ^ 1


def body(
    points,
    ordering,
    iterate,
    target,
    step_size,
    leaf_basis,
    transfer,
    leaf_skeleton,
    cluster_skeleton,
    near_table,
    far_table,
    cluster_far,
):
    plan = Plan(points, iterate)
    leaves = lax.axis_size("leaf")
    groups = lax.axis_size("group")
    rank = leaf_basis.shape[1]
    leaf_t = jnp.swapaxes(leaf_skeleton, 1, 2)
    cluster_t = jnp.swapaxes(cluster_skeleton, 1, 2)

    pay, down_block, up_block = prepare(
        plan, near_table, iterate, points.T, leaf_basis, transfer, leaf_t, cluster_t
    )
    partner = routed(pay, "leaf", on_chip)
    over = routed(pay, "leaf", over_chips)
    others = [routed(up_block, "group", lambda i, k=k: i ^ k) for k in range(1, groups)]
    acc = own_tile(plan, pay)
    mine = across(cluster_far, cluster_t, up_block, others, lambda me, k: me ^ (k + 1), down_block)
    acc, left, row = pair_tiles(plan, near_table, pay, partner, acc)

    xors, bit = [0], leaves // 2
    while True:
        got = routed(mine, "leaf", lambda i, bit=bit: i ^ bit)
        xors = xors + [x ^ bit for x in xors]
        if bit == 1:
            break
        mine = joined(mine, got, rank)
        bit //= 2
    local = down(far_table, leaf_t, transfer, mine, got, xors)

    beside = routed(pay, "leaf", beside_chips)
    over_passed = routed(over, "leaf", on_chip)
    (acc,) = side_tiles(plan, near_table, row, left, over, over_passed, acc, 2, False)
    beside_passed = routed(beside, "leaf", on_chip)
    third = routed(beside, "leaf", over_chips)
    acc, theirs = side_tiles(plan, near_table, row, left, beside, beside_passed, acc, 1, True)
    returned = routed(theirs, "leaf", on_chip)
    wanted = wanted_rows(ordering, target)
    return last_tile(
        plan, near_table, pay, left, third, acc, returned, iterate, wanted, step_size, leaf_basis, local
    )


def solution(mesh):
    return jax.shard_map(
        body,
        mesh=mesh,
        in_specs=(
            P(("group", "leaf"), None),
            P(("group", "leaf"), None),
            P(("group", "leaf"), None),
            P(("group", "leaf"), None),
            P(),
            P(("group", "leaf"), None),
            P(("group", "leaf"), None, None),
            P(("group", "leaf"), None, None),
            P("group", None, None),
            P(("group", "leaf"), None),
            P(("group", "leaf"), None),
            P("group", None),
        ),
        out_specs=P(("group", "leaf"), None),
        check_vma=False,
    )
```

profile of v0, /device:TPU:24, one launch (start us, length us, event | category | flops | bytes accessed | tf_op | source)
XLA Modules:
  0.0 94.1 jit_solution(12114577453888815011)
XLA Ops:
  0.0 1.2 %copy-done = f32[2048,128]{1,0:T(8,128)S(1)} copy-done((f32[2048,128]{1,0:T(8,128)S(1)}, f32[2048,128]{1,0:T(8,128)}, u32[]{:S(2)}) %copy-start) | copy-done | bytes 1048600
  1.2 1.2 %copy-done.2 = bf16[2048,256]{1,0:T(8,128)(2,1)S(1)} copy-done((bf16[2048,256]{1,0:T(8,128)(2,1)S(1)}, bf16[2048,256]{1,0:T(8,128)(2,1)}, u32[]{:S(2)}) %copy-start.2) | copy-done | bytes 1048600
  2.5 0.9 %copy-done.4 = bf16[2048,64]{0,1:T(8,128)(2,1)S(1)} copy-done((bf16[2048,64]{0,1:T(8,128)(2,1)S(1)}, bf16[2048,64]{0,1:T(8,128)(2,1)}, u32[]{:S(2)}) %copy-start.4) | copy-done | bytes 262168
  3.4 0.9 copy-done.5
  4.3 0.8 copy-done.7
  5.1 0.8 copy-done.9
  5.8 0.7 copy-done.11
  6.5 1.4 %shard_map.118 = (bf16[2,1552,128]{2,1,0:T(8,128)(2,1)S(1)}, bf16[384,128]{1,0:T(8,128)(2,1)S(1)}, bf16[384,128]{1,0:T(8,128)(2,1)S(1)}) custom-call(bf16[64,2048]{1,0:T(8,128)(2,1)S(1)} %bitcast.4, f32[2048,128]{1,0:T(8,128)S(1)} %copy-done, s32[1,8]{1,0:T(1,128)S(1)} %copy-done.11, bf16[1,64,256]{2,1,0:T(8,128)(2,1)S(1)} %bitcast.7, ...), custom_call_target="tpu_custom_call" | custom-call | flops 134217728 | bytes 2555936 | tf_op jit(solution)/shard_map/pallas_call | solution.py:35
  7.9 1.3 %collective-permute-start.4 = (bf16[2,1552,128]{2,1,0:T(8,128)(2,1)S(1)}, bf16[2,1552,128]{2,1,0:T(8,128)(2,1)S(1)}, u32[]{:S(2)}, u32[]{:S(2)}) collective-permute-start(bf16[2,1552,128]{2,1,0:T(8,128)(2,1)S(1)} %get-tuple-element.13.pay_ref), channel_id=1, source_target_pairs={{0,2},{2,4},{3,1},{4,6},{5,3},{7,5},{8,10},{10,12},{11,9},{12,14},... | collective-permute-start | bytes 2383880 | tf_op jit(solution)/shard_map/ppermute | solution.py:475
  9.2 0.7 collective-permute-start
  9.9 4.0 %collective-permute-start.1 = (bf16[2,1552,128]{2,1,0:T(8,128)(2,1)S(1)}, bf16[2,1552,128]{2,1,0:T(8,128)(2,1)S(1)}, u32[]{:S(2)}, u32[]{:S(2)}) collective-permute-start(bf16[2,1552,128]{2,1,0:T(8,128)(2,1)S(1)} %get-tuple-element.13.pay_ref), channel_id=1, source_target_pairs={{1,2},{2,1},{3,4},{4,3},{5,6},{6,5},{9,10},{10,9},{11,12},{12,11},... | collective-permute-start | bytes 2383880 | tf_op jit(solution)/shard_map/ppermute | solution.py:475
  13.9 1.6 %collective-permute-start.7 = (bf16[384,128]{1,0:T(8,128)(2,1)S(1)}, bf16[384,128]{1,0:T(8,128)(2,1)S(1)}, u32[]{:S(2)}, u32[]{:S(2)}) collective-permute-start(bf16[384,128]{1,0:T(8,128)(2,1)S(1)} %get-tuple-element.20.own_ref), channel_id=1, source_target_pairs={{0,8},{8,0},{16,24},{24,16},{1,9},{9,1},{17,25},{25,17},{2,10},{10... | collective-permute-start | bytes 294920 | tf_op jit(solution)/shard_map/ppermute | solution.py:475
  15.5 1.5 %collective-permute-start.8 = (bf16[384,128]{1,0:T(8,128)(2,1)S(1)}, bf16[384,128]{1,0:T(8,128)(2,1)S(1)}, u32[]{:S(2)}, u32[]{:S(2)}) collective-permute-start(bf16[384,128]{1,0:T(8,128)(2,1)S(1)} %get-tuple-element.20.own_ref), channel_id=1, source_target_pairs={{0,16},{8,24},{16,0},{24,8},{1,17},{9,25},{17,1},{25,9},{2,18},{10... | collective-permute-start | bytes 294920 | tf_op jit(solution)/shard_map/ppermute | solution.py:475
  17.0 11.6 %collective-permute-done.4.full_ref = bf16[2,1552,128]{2,1,0:T(8,128)(2,1)S(1)} collective-permute-done((bf16[2,1552,128]{2,1,0:T(8,128)(2,1)S(1)}, bf16[2,1552,128]{2,1,0:T(8,128)(2,1)S(1)}, u32[]{:S(2)}, u32[]{:S(2)}) %collective-permute-start.4) | collective-permute-done | bytes 794656 | tf_op jit(solution)/shard_map/ppermute | solution.py:475
  28.6 5.2 %shard_map.119.acc_in = f32[2,2048,128]{2,1,0:T(8,128)S(1)} custom-call(bf16[2,1552,128]{2,1,0:T(8,128)(2,1)S(1)} %get-tuple-element.13.pay_ref), custom_call_target="tpu_custom_call" | custom-call | flops 4294967296 | bytes 794624 | tf_op jit(solution)/shard_map/pallas_call | solution.py:35
  33.8 2.5 %collective-permute-start.9 = (bf16[384,128]{1,0:T(8,128)(2,1)S(1)}, bf16[384,128]{1,0:T(8,128)(2,1)S(1)}, u32[]{:S(2)}, u32[]{:S(2)}) collective-permute-start(bf16[384,128]{1,0:T(8,128)(2,1)S(1)} %get-tuple-element.20.own_ref), channel_id=1, source_target_pairs={{0,24},{8,16},{16,8},{24,0},{1,25},{9,17},{17,9},{25,1},{2,26},{10... | collective-permute-start | bytes 294920 | tf_op jit(solution)/shard_map/ppermute | solution.py:475
  36.3 0.2 collective-permute-start.3
  36.6 3.5 %shard_map.120 = (f32[2,2048,128]{2,1,0:T(8,128)S(1)}, bf16[2,2048,64]{2,1,0:T(8,128)(2,1)S(1)}, f32[16,128]{1,0:T(8,128)S(1)}) custom-call(s32[1,8]{1,0:T(1,128)S(1)} %copy-done.12, bf16[2,1552,128]{2,1,0:T(8,128)(2,1)S(1)} %get-tuple-element.13.pay_ref, ...), custom_call_target="tpu_custom_call", output_to_operand_aliasing={{0}: (3, {})} | custom-call | flops 4294967296 | bytes 3686432 | tf_op jit(solution)/shard_map/pallas_call | solution.py:35
  40.0 3.5 %shard_map.121.acc_in = f32[2,2048,128]{2,1,0:T(8,128)S(1)} custom-call(s32[1,8]{1,0:T(1,128)S(1)} %copy-done.12, f32[16,128]{1,0:T(8,128)S(1)} %get-tuple-element.15.row_in, bf16[2,2048,64]{2,1,0:T(8,128)(2,1)S(1)} %get-tuple-element.14.left_ref, bf16[2,1552,128]{2,1,0:T(8,128)(2,1)S(1)} %collective-permute-done.4.full_ref, ...), custom_call_target="tpu_custom_call", output_to_operand_aliasing={{}: (5, {})} | custom-call | flops 8589934592 | bytes 4218912 | tf_op jit(solution)/shard_map/pallas_call | solution.py:35
  43.6 0.0 copy-start.15
  43.6 3.4 %shard_map.122 = (f32[2,2048,128]{2,1,0:T(8,128)S(1)}, f32[2048,128]{1,0:T(8,128)S(1)}) custom-call(s32[1,8]{1,0:T(1,128)S(1)} %copy-done.12, f32[16,128]{1,0:T(8,128)S(1)} %get-tuple-element.15.row_in, bf16[2,2048,64]{2,1,0:T(8,128)(2,1)S(1)} %get-tuple-element.14.left_ref, ...), custom_call_target="tpu_custom_call", output_to_operand_aliasing={{0}: (5, {})} | custom-call | flops 8589934592 | bytes 4218912 | tf_op jit(solution)/shard_map/pallas_call | solution.py:35
  47.0 0.3 collective-permute-start.6
  47.4 1.3 %shard_map.124.mine_ref = bf16[640,128]{1,0:T(8,128)(2,1)S(1)} custom-call(s32[1,4]{1,0:T(1,128)S(1)} %copy-done.15, bf16[1,64,256]{2,1,0:T(8,128)(2,1)S(1)} %bitcast.6, bf16[384,128]{1,0:T(8,128)(2,1)S(1)} %get-tuple-element.19.down_ref, bf16[384,128]{1,0:T(8,128)(2,1)S(1)} %get-tuple-element.20.own_ref, ...), custom_call_target="tpu_custom_call" | custom-call | flops 268435456 | bytes 524304 | tf_op jit(solution)/shard_map/pallas_call | solution.py:35
  48.7 9.1 %collective-permute-start.10 = (bf16[640,128]{1,0:T(8,128)(2,1)S(1)}, bf16[640,128]{1,0:T(8,128)(2,1)S(1)}, u32[]{:S(2)}, u32[]{:S(2)}) collective-permute-start(bf16[640,128]{1,0:T(8,128)(2,1)S(1)} %shard_map.124.mine_ref), channel_id=1, source_target_pairs={{0,4},{1,5},{2,6},{3,7},{4,0},{5,1},{6,2},{7,3},{8,12},{9,13},{10,... | collective-permute-start | bytes 491528 | tf_op jit(solution)/shard_map/ppermute | solution.py:475
  57.8 1.5 %collective-permute-start.2 = (bf16[2,1552,128]{2,1,0:T(8,128)(2,1)S(1)}, bf16[2,1552,128]{2,1,0:T(8,128)(2,1)S(1)}, u32[]{:S(2)}, u32[]{:S(2)}) collective-permute-start(bf16[2,1552,128]{2,1,0:T(8,128)(2,1)S(1)} %collective-permute-done.1.full_ref), channel_id=1, source_target_pairs={{0,2},{2,4},{3,1},{4,6},{5,3},{7,5},{8,10},{10,12},{11,9},{12,14},... | collective-permute-start | bytes 2383880 | tf_op jit(solution)/shard_map/ppermute | solution.py:475
  59.3 6.7 %collective-permute-done.10.got_ref = bf16[640,128]{1,0:T(8,128)(2,1)S(1)} collective-permute-done((bf16[640,128]{1,0:T(8,128)(2,1)S(1)}, bf16[640,128]{1,0:T(8,128)(2,1)S(1)}, u32[]{:S(2)}, u32[]{:S(2)}) %collective-permute-start.10) | collective-permute-done | bytes 163872 | tf_op jit(solution)/shard_map/ppermute | solution.py:475
  66.1 0.1 collective-permute-start.11
  66.1 13.9 %collective-permute-done.11.got_ref = bf16[1024,128]{1,0:T(8,128)(2,1)S(1)} collective-permute-done((bf16[1024,128]{1,0:T(8,128)(2,1)S(1)}, bf16[1024,128]{1,0:T(8,128)(2,1)S(1)}, u32[]{:S(2)}, u32[]{:S(2)}) %collective-permute-start.11) | collective-permute-done | bytes 262176 | tf_op jit(solution)/shard_map/ppermute | solution.py:475
  80.2 0.1 collective-permute-start.12
  80.3 4.1 %shard_map.123.wanted_ref = f32[2048,128]{1,0:T(8,128)S(1)} custom-call(s32[1,2048]{1,0:T(1,128)S(1)} %copy-done.14, f32[2048,128]{1,0:T(8,128)S(1)} %copy-done.13), custom_call_target="tpu_custom_call" | custom-call | flops 2147483648 | bytes 1056768 | tf_op jit(solution)/shard_map/pallas_call | solution.py:35
  84.5 2.4 %shard_map.127.local_ref = bf16[256,128]{1,0:T(8,128)(2,1)S(1)} custom-call(s32[1,8]{1,0:T(1,128)S(1)} %copy-done.16, bf16[1,64,256]{2,1,0:T(8,128)(2,1)S(1)} %bitcast.8, bf16[1,256,256]{2,1,0:T(8,128)(2,1)S(1)} %copy-done.6, bf16[1792,128]{1,0:T(8,128)(2,1)S(1)} %shard_map.126.mine_ref, bf16[1792,128]{1,0:T(8,128)(2,1)S(1)} %collective-permute-done.12.got_ref), custom_call_target="tpu_custom_call" | custom-call | flops 536870912 | bytes 1081376 | tf_op jit(solution)/shard_map/pallas_call | solution.py:35
  86.9 7.2 %shard_map.128 = f32[2048,128]{1,0:T(8,128)} custom-call(s32[1,8]{1,0:T(1,128)S(1)} %copy-done.12, bf16[2,1552,128]{2,1,0:T(8,128)(2,1)S(1)} %get-tuple-element.13.pay_ref, bf16[2,2048,64]{2,1,0:T(8,128)(2,1)S(1)} %get-tuple-element.14.left_ref, bf16[2,1552,128]{2,1,0:T(8,128)(2,1)S(1)} %collective-permute-done.2.third_ref, ...), custom_call_target="tpu_custom_call" | custom-call | flops 4294967296 | bytes 8471072 | tf_op jit(solution)/shard_map/pallas_call | solution.py:35
  (41 shorter events, 0.2 us)
Async XLA Ops:
  0.0 1.2 %copy-start = (f32[2048,128]{1,0:T(8,128)S(1)}, f32[2048,128]{1,0:T(8,128)}, u32[]{:S(2)}) copy-start(f32[2048,128]{1,0:T(8,128)} %iterate_ref.1) | copy-start | bytes 3145732
  1.2 1.2 %copy-start.2 = (bf16[2048,256]{1,0:T(8,128)(2,1)S(1)}, bf16[2048,256]{1,0:T(8,128)(2,1)}, u32[]{:S(2)}) copy-start(bf16[2048,256]{1,0:T(8,128)(2,1)} %basis_ref.1) | copy-start | bytes 3145732
  2.5 0.9 %copy-start.4 = (bf16[2048,64]{0,1:T(8,128)(2,1)S(1)}, bf16[2048,64]{0,1:T(8,128)(2,1)}, u32[]{:S(2)}) copy-start(bf16[2048,64]{0,1:T(8,128)(2,1)} %param.12) | copy-start | bytes 786436
  3.4 0.9 copy-start.5
  4.3 0.8 copy-start.7
  5.1 0.8 copy-start.9
  5.8 0.7 copy-start.11
  7.9 20.7 %collective-permute-start.4 = (bf16[2,1552,128]{2,1,0:T(8,128)(2,1)S(1)}, bf16[2,1552,128]{2,1,0:T(8,128)(2,1)S(1)}, u32[]{:S(2)}, u32[]{:S(2)}) collective-permute-start(bf16[2,1552,128]{2,1,0:T(8,128)(2,1)S(1)} %get-tuple-element.13.pay_ref), channel_id=1, source_target_pairs={{0,2},{2,4},{3,1},{4,6},{5,3},{7,5},{8,10},{10,12},{11,9},{12,14},... | collective-permute-start | bytes 2383880 | tf_op jit(solution)/shard_map/ppermute | solution.py:475
  9.2 24.6 %collective-permute-start = (bf16[2,1552,128]{2,1,0:T(8,128)(2,1)S(1)}, bf16[2,1552,128]{2,1,0:T(8,128)(2,1)S(1)}, u32[]{:S(2)}, u32[]{:S(2)}) collective-permute-start(bf16[2,1552,128]{2,1,0:T(8,128)(2,1)S(1)} %get-tuple-element.13.pay_ref), channel_id=1, source_target_pairs={{0,1},{1,0},{2,3},{3,2},{4,5},{5,4},{6,7},{7,6},{8,9},{9,8},{10,11... | collective-permute-start | bytes 2383880 | tf_op jit(solution)/shard_map/ppermute | solution.py:475
  9.9 26.4 %collective-permute-start.1 = (bf16[2,1552,128]{2,1,0:T(8,128)(2,1)S(1)}, bf16[2,1552,128]{2,1,0:T(8,128)(2,1)S(1)}, u32[]{:S(2)}, u32[]{:S(2)}) collective-permute-start(bf16[2,1552,128]{2,1,0:T(8,128)(2,1)S(1)} %get-tuple-element.13.pay_ref), channel_id=1, source_target_pairs={{1,2},{2,1},{3,4},{4,3},{5,6},{6,5},{9,10},{10,9},{11,12},{12,11},... | collective-permute-start | bytes 2383880 | tf_op jit(solution)/shard_map/ppermute | solution.py:475
  13.9 22.7 %copy-start.12 = (s32[1,8]{1,0:T(1,128)S(1)}, s32[1,8]{1,0:T(1,128)}, u32[]{:S(2)}) copy-start(s32[1,8]{1,0:T(1,128)} %near_ref.7) | copy-start | bytes 100
  13.9 33.5 %collective-permute-start.7 = (bf16[384,128]{1,0:T(8,128)(2,1)S(1)}, bf16[384,128]{1,0:T(8,128)(2,1)S(1)}, u32[]{:S(2)}, u32[]{:S(2)}) collective-permute-start(bf16[384,128]{1,0:T(8,128)(2,1)S(1)} %get-tuple-element.20.own_ref), channel_id=1, source_target_pairs={{0,8},{8,0},{16,24},{24,16},{1,9},{9,1},{17,25},{25,17},{2,10},{10... | collective-permute-start | bytes 294920 | tf_op jit(solution)/shard_map/ppermute | solution.py:475
  15.5 31.9 %collective-permute-start.8 = (bf16[384,128]{1,0:T(8,128)(2,1)S(1)}, bf16[384,128]{1,0:T(8,128)(2,1)S(1)}, u32[]{:S(2)}, u32[]{:S(2)}) collective-permute-start(bf16[384,128]{1,0:T(8,128)(2,1)S(1)} %get-tuple-element.20.own_ref), channel_id=1, source_target_pairs={{0,16},{8,24},{16,0},{24,8},{1,17},{9,25},{17,1},{25,9},{2,18},{10... | collective-permute-start | bytes 294920 | tf_op jit(solution)/shard_map/ppermute | solution.py:475
  28.6 11.5 %collective-permute-start.5 = (bf16[2,1552,128]{2,1,0:T(8,128)(2,1)S(1)}, bf16[2,1552,128]{2,1,0:T(8,128)(2,1)S(1)}, u32[]{:S(2)}, u32[]{:S(2)}) collective-permute-start(bf16[2,1552,128]{2,1,0:T(8,128)(2,1)S(1)} %collective-permute-done.4.full_ref), channel_id=1, source_target_pairs={{0,1},{1,0},{2,3},{3,2},{4,5},{5,4},{6,7},{7,6},{8,9},{9,8},{10,11... | collective-permute-start | bytes 2383880 | tf_op jit(solution)/shard_map/ppermute | solution.py:475
  33.8 13.6 %collective-permute-start.9 = (bf16[384,128]{1,0:T(8,128)(2,1)S(1)}, bf16[384,128]{1,0:T(8,128)(2,1)S(1)}, u32[]{:S(2)}, u32[]{:S(2)}) collective-permute-start(bf16[384,128]{1,0:T(8,128)(2,1)S(1)} %get-tuple-element.20.own_ref), channel_id=1, source_target_pairs={{0,24},{8,16},{16,8},{24,0},{1,25},{9,17},{17,9},{25,1},{2,26},{10... | collective-permute-start | bytes 294920 | tf_op jit(solution)/shard_map/ppermute | solution.py:475
  36.3 7.2 %collective-permute-start.3 = (bf16[2,1552,128]{2,1,0:T(8,128)(2,1)S(1)}, bf16[2,1552,128]{2,1,0:T(8,128)(2,1)S(1)}, u32[]{:S(2)}, u32[]{:S(2)}) collective-permute-start(bf16[2,1552,128]{2,1,0:T(8,128)(2,1)S(1)} %collective-permute-done.1.full_ref), channel_id=1, source_target_pairs={{0,1},{1,0},{2,3},{3,2},{4,5},{5,4},{6,7},{7,6},{8,9},{9,8},{10,11... | collective-permute-start | bytes 2383880 | tf_op jit(solution)/shard_map/ppermute | solution.py:475
  43.5 3.8 %copy-start.8 = (bf16[1,256,64]{1,2,0:T(8,128)(2,1)S(1)}, bf16[1,256,64]{1,2,0:T(8,128)(2,1)}, u32[]{:S(2)}) copy-start(bf16[1,256,64]{1,2,0:T(8,128)(2,1)} %param.20) | copy-start | bytes 98308
  43.6 3.8 %copy-start.15 = (s32[1,4]{1,0:T(1,128)S(1)}, s32[1,4]{1,0:T(1,128)}, u32[]{:S(2)}) copy-start(s32[1,4]{1,0:T(1,128)} %far_ref.2) | copy-start | bytes 52
  47.0 33.3 %copy-start.13 = (f32[2048,128]{1,0:T(8,128)S(1)}, f32[2048,128]{1,0:T(8,128)}, u32[]{:S(2)}) copy-start(f32[2048,128]{1,0:T(8,128)} %target_hbm.1) | copy-start | bytes 3145732
  47.0 33.3 %copy-start.14 = (s32[1,2048]{1,0:T(1,128)S(1)}, s32[1,2048]{1,0:T(1,128)}, u32[]{:S(2)}) copy-start(s32[1,2048]{1,0:T(1,128)} %order_ref.1) | copy-start | bytes 24580
  47.0 39.9 %collective-permute-start.6 = (f32[2048,128]{1,0:T(8,128)S(1)}, f32[2048,128]{1,0:T(8,128)S(1)}, u32[]{:S(2)}, u32[]{:S(2)}) collective-permute-start(f32[2048,128]{1,0:T(8,128)S(1)} %get-tuple-element.18), channel_id=1, source_target_pairs={{0,1},{1,0},{2,3},{3,2},{4,5},{5,4},{6,7},{7,6},{8,9},{9,8},{10,11... | collective-permute-start | bytes 3145736 | tf_op jit(solution)/shard_map/ppermute | solution.py:475
  48.7 17.3 %collective-permute-start.10 = (bf16[640,128]{1,0:T(8,128)(2,1)S(1)}, bf16[640,128]{1,0:T(8,128)(2,1)S(1)}, u32[]{:S(2)}, u32[]{:S(2)}) collective-permute-start(bf16[640,128]{1,0:T(8,128)(2,1)S(1)} %shard_map.124.mine_ref), channel_id=1, source_target_pairs={{0,4},{1,5},{2,6},{3,7},{4,0},{5,1},{6,2},{7,3},{8,12},{9,13},{10,... | collective-permute-start | bytes 491528 | tf_op jit(solution)/shard_map/ppermute | solution.py:475
  57.8 29.1 %collective-permute-start.2 = (bf16[2,1552,128]{2,1,0:T(8,128)(2,1)S(1)}, bf16[2,1552,128]{2,1,0:T(8,128)(2,1)S(1)}, u32[]{:S(2)}, u32[]{:S(2)}) collective-permute-start(bf16[2,1552,128]{2,1,0:T(8,128)(2,1)S(1)} %collective-permute-done.1.full_ref), channel_id=1, source_target_pairs={{0,2},{2,4},{3,1},{4,6},{5,3},{7,5},{8,10},{10,12},{11,9},{12,14},... | collective-permute-start | bytes 2383880 | tf_op jit(solution)/shard_map/ppermute | solution.py:475
  66.1 14.0 %collective-permute-start.11 = (bf16[1024,128]{1,0:T(8,128)(2,1)S(1)}, bf16[1024,128]{1,0:T(8,128)(2,1)S(1)}, u32[]{:S(2)}, u32[]{:S(2)}) collective-permute-start(bf16[1024,128]{1,0:T(8,128)(2,1)S(1)} %shard_map.125.mine_ref), channel_id=1, source_target_pairs={{0,2},{1,3},{2,0},{3,1},{4,6},{5,7},{6,4},{7,5},{8,10},{9,11},{10,... | collective-permute-start | bytes 786440 | tf_op jit(solution)/shard_map/ppermute | solution.py:475
  80.1 4.3 %copy-start.6 = (bf16[1,256,256]{2,1,0:T(8,128)(2,1)S(1)}, bf16[1,256,256]{2,1,0:T(8,128)(2,1)}, u32[]{:S(2)}) copy-start(bf16[1,256,256]{2,1,0:T(8,128)(2,1)} %transfer_ref.1) | copy-start | bytes 393220
  80.1 4.3 %copy-start.10 = (bf16[1,256,64]{1,2,0:T(8,128)(2,1)S(1)}, bf16[1,256,64]{1,2,0:T(8,128)(2,1)}, u32[]{:S(2)}) copy-start(bf16[1,256,64]{1,2,0:T(8,128)(2,1)} %param.19) | copy-start | bytes 98308
  80.1 4.3 %copy-start.16 = (s32[1,8]{1,0:T(1,128)S(1)}, s32[1,8]{1,0:T(1,128)}, u32[]{:S(2)}) copy-start(s32[1,8]{1,0:T(1,128)} %far_ref.3) | copy-start | bytes 100
  80.1 6.8 %copy-start.1 = (f32[2048,128]{1,0:T(8,128)S(1)}, f32[2048,128]{1,0:T(8,128)}, u32[]{:S(2)}) copy-start(f32[2048,128]{1,0:T(8,128)} %iterate_ref.1) | copy-start | bytes 3145732
  80.2 6.8 %copy-start.3 = (bf16[2048,256]{1,0:T(8,128)(2,1)S(1)}, bf16[2048,256]{1,0:T(8,128)(2,1)}, u32[]{:S(2)}) copy-start(bf16[2048,256]{1,0:T(8,128)(2,1)} %basis_ref.1) | copy-start | bytes 3145732
  80.2 6.8 %copy-start.17 = (f32[128]{0:T(128)S(1)}, f32[128]{0:T(128)}, u32[]{:S(2)}) copy-start(f32[128]{0:T(128)} %param.16) | copy-start | bytes 1540
  80.2 4.2 %collective-permute-start.12 = (bf16[1792,128]{1,0:T(8,128)(2,1)S(1)}, bf16[1792,128]{1,0:T(8,128)(2,1)S(1)}, u32[]{:S(2)}, u32[]{:S(2)}) collective-permute-start(bf16[1792,128]{1,0:T(8,128)(2,1)S(1)} %shard_map.126.mine_ref), channel_id=1, source_target_pairs={{0,1},{1,0},{2,3},{3,2},{4,5},{5,4},{6,7},{7,6},{8,9},{9,8},{10,11... | collective-permute-start | bytes 1376264 | tf_op jit(solution)/shard_map/ppermute | solution.py:475
where the time goes:
time: 94.5 us; the launch traced here: 94.1 us
  waiting for transfers between devices  32.2 us (34%)
  Pallas kernels  32.1 us (34%)
  starting transfers between devices  22.9 us (24%)
  local copies, waits for them, and re-layouts  6.54 us (7%)
    ppermute x13, waiting for transfers between devices, routed(): return lax.ppermute(block, axis, route)  32.2 us
    pallas_call x11, Pallas kernels, call(): pl.pallas_call(kernel, out_shape=shapes, in_specs=[pl.BlockSpec(memory_sp...  32.1 us
    ppermute x13, starting transfers between devices, routed(): return lax.ppermute(block, axis, route)  22.9 us
    unnamed x36, local copies, waits for them, and re-layouts  6.54 us
  transfers between devices with their start and end apart: 13, of which 3 were waited for; matrix products, arithmetic and copies ran while one was open for 0% of the time, Pallas kernels for 25%

commit v1 on v0

--- a/solution.py
+++ b/solution.py
@@ -29,14 +29,14 @@
     return contract(left, right, ((1,), (0,)))
 
 
-def call(kernel, outs, ins, scratch=(), flops=0, limit=16, aliases=None):
+def call(kernel, outs, ins, scratch=(), flops=0, limit=16, aliases=None, into=VMEM):
     single = not isinstance(outs, (list, tuple))
     shapes = [outs] if single else list(outs)
     results = pl.pallas_call(
         kernel,
         out_shape=shapes,
         in_specs=[pl.BlockSpec(memory_space=space) for _, space in ins],
-        out_specs=[pl.BlockSpec(memory_space=VMEM)] * len(shapes),
+        out_specs=[pl.BlockSpec(memory_space=into)] * len(shapes),
         scratch_shapes=list(scratch),
         input_output_aliases=aliases or {},
         compiler_params=pltpu.CompilerParams(vmem_limit_bytes=limit << 20),
@@ -214,7 +214,7 @@
     return call(
         kernel,
         [plan.pay(), shaped(rows, plan.rhs), shaped(rows, plan.rhs)],
-        [(value, HBM) for value in inputs],
+        [(pltpu.with_memory_space_constraint(value, HBM), HBM) for value in inputs],
         scratch=[(SMEM if value is near_row else VMEM)(value.shape, value.dtype) for value in inputs]
         + [pltpu.SemaphoreType.DMA((len(inputs),))],
         flops=2 * n * rank * plan.rhs,
@@ -346,7 +346,7 @@
 
 
 def last_tile(plan, near_row, pay, left, third, acc, returned, iterate, wanted, step_size, basis, local):
-    def kernel(near_ref, pay_ref, left_ref, third_ref, acc_ref, returned_ref, iterate_ref, wanted_ref, step_ref, basis_ref, local_ref, out_ref, offset_ref):
+    def kernel(near_ref, pay_ref, left_ref, third_ref, acc_ref, returned_ref, iterate_ref, wanted_ref, step_ref, basis_ref, local_ref, out_hbm, out_ref, offset_ref, sems):
         place = lax.axis_index("leaf")
         away = 2 * lax.rem(place, 2) - 1
         out_ref[...] = acc_ref[0] + returned_ref[...]
@@ -358,6 +358,7 @@
                 fill_offset(plan, offset_ref, third_ref.at[h])
                 half_tile(plan, out_ref, left_ref.at[0], third_ref.at[h], offset_ref)
 
+        copies = []
         for h in range(2):
             for b in range(plan.blocks):
                 first = h * plan.half + b * LANES
@@ -366,6 +367,14 @@
                 factor = jnp.exp2(jnp.broadcast_to(power, (LANES, LANES)).T)
                 image = matmul(basis_ref[rows, :], local_ref[...]) + factor * out_ref[rows, :]
                 out_ref[rows, :] = iterate_ref[rows, :] + step_ref[...] * (wanted_ref[rows, :] - image)
+                if b % 4 == 3:
+                    done = slice(first - 3 * LANES, first + LANES)
+                    copies.append(
+                        pltpu.make_async_copy(out_ref.at[done, :], out_hbm.at[done, :], sems.at[len(copies)])
+                    )
+                    copies[-1].start()
+        for copy in copies:
+            copy.wait()
 
     return call(
         kernel,
@@ -383,7 +392,10 @@
             (basis, VMEM),
             (local, VMEM),
         ],
-        scratch=plan.offset_scratch(),
+        scratch=[VMEM((plan.n, plan.rhs), F32)]
+        + plan.offset_scratch()
+        + [pltpu.SemaphoreType.DMA((plan.n // (4 * LANES),))],
+        into=HBM,
         flops=plan.tile_flops,
     )
 

time: 94.5 us -> 88.8 us (0.940)
  local copies, waits for them, and re-layouts: 6.54 us -> 0.07 us
    unnamed x36 -> x22, local copies, waits for them, and re-layouts: 6.54 us -> 0.07 us
  transfers between devices with their start and end apart: 13 -> 13, of which waited for: 3 -> 3; matrix products, arithmetic and copies ran while one was open for 0% -> 0% of each run, Pallas kernels for 25% -> 27%
where the time goes in v1:
time: 88.8 us; the launch traced here: 88.6 us
  Pallas kernels  32.9 us (37%)
  waiting for transfers between devices  32.2 us (36%)
  starting transfers between devices  22.9 us (26%)
    pallas_call x11, Pallas kernels, call(): pl.pallas_call(kernel, out_shape=shapes, in_specs=[pl.BlockSpec(memory_sp...  32.9 us
    ppermute x13, waiting for transfers between devices, routed(): return lax.ppermute(block, axis, route)  32.2 us
    ppermute x13, starting transfers between devices, routed(): return lax.ppermute(block, axis, route)  22.9 us
  transfers between devices with their start and end apart: 13, of which 3 were waited for; matrix products, arithmetic and copies ran while one was open for 0% of the time, Pallas kernels for 27%

profile of v1, /device:TPU:24, one launch (start us, length us, event | category | flops | bytes accessed | tf_op | source)
XLA Modules:
  0.0 88.6 jit_solution(5812516602128675355)
XLA Ops:
  0.0 2.4 %shard_map.118 = (bf16[2,1552,128]{2,1,0:T(8,128)(2,1)S(1)}, bf16[384,128]{1,0:T(8,128)(2,1)S(1)}, bf16[384,128]{1,0:T(8,128)(2,1)S(1)}) custom-call(bf16[64,2048]{1,0:T(8,128)(2,1)} %bitcast.9, f32[2048,128]{1,0:T(8,128)} %iterate_ref.1, s32[1,8]{1,0:T(1,128)} %near_ref.7, bf16[1,64,256]{2,1,0:T(8,128)(2,1)} %bitcast.6, bf16[1,64,256]{2,1,0:T(8,128)(2,1)} %bitcast.4, ...), custom_call_target="tpu_custom_call" | custom-call | flops 134217728 | bytes 2555936 | tf_op jit(solution)/shard_map/pallas_call | solution.py:35
  2.4 1.3 %collective-permute-start.4 = (bf16[2,1552,128]{2,1,0:T(8,128)(2,1)S(1)}, bf16[2,1552,128]{2,1,0:T(8,128)(2,1)S(1)}, u32[]{:S(2)}, u32[]{:S(2)}) collective-permute-start(bf16[2,1552,128]{2,1,0:T(8,128)(2,1)S(1)} %get-tuple-element.13.pay_ref), channel_id=1, source_target_pairs={{0,2},{2,4},{3,1},{4,6},{5,3},{7,5},{8,10},{10,12},{11,9},{12,14},... | collective-permute-start | bytes 2383880 | tf_op jit(solution)/shard_map/ppermute | solution.py:487
  3.7 0.7 collective-permute-start
  4.5 4.0 %collective-permute-start.1 = (bf16[2,1552,128]{2,1,0:T(8,128)(2,1)S(1)}, bf16[2,1552,128]{2,1,0:T(8,128)(2,1)S(1)}, u32[]{:S(2)}, u32[]{:S(2)}) collective-permute-start(bf16[2,1552,128]{2,1,0:T(8,128)(2,1)S(1)} %get-tuple-element.13.pay_ref), channel_id=1, source_target_pairs={{1,2},{2,1},{3,4},{4,3},{5,6},{6,5},{9,10},{10,9},{11,12},{12,11},... | collective-permute-start | bytes 2383880 | tf_op jit(solution)/shard_map/ppermute | solution.py:487
  8.4 0.0 copy-start.5
  8.5 1.6 %collective-permute-start.7 = (bf16[384,128]{1,0:T(8,128)(2,1)S(1)}, bf16[384,128]{1,0:T(8,128)(2,1)S(1)}, u32[]{:S(2)}, u32[]{:S(2)}) collective-permute-start(bf16[384,128]{1,0:T(8,128)(2,1)S(1)} %get-tuple-element.20.own_ref), channel_id=1, source_target_pairs={{0,8},{8,0},{16,24},{24,16},{1,9},{9,1},{17,25},{25,17},{2,10},{10... | collective-permute-start | bytes 294920 | tf_op jit(solution)/shard_map/ppermute | solution.py:487
  10.0 1.5 %collective-permute-start.8 = (bf16[384,128]{1,0:T(8,128)(2,1)S(1)}, bf16[384,128]{1,0:T(8,128)(2,1)S(1)}, u32[]{:S(2)}, u32[]{:S(2)}) collective-permute-start(bf16[384,128]{1,0:T(8,128)(2,1)S(1)} %get-tuple-element.20.own_ref), channel_id=1, source_target_pairs={{0,16},{8,24},{16,0},{24,8},{1,17},{9,25},{17,1},{25,9},{2,18},{10... | collective-permute-start | bytes 294920 | tf_op jit(solution)/shard_map/ppermute | solution.py:487
  11.5 11.6 %collective-permute-done.4.full_ref = bf16[2,1552,128]{2,1,0:T(8,128)(2,1)S(1)} collective-permute-done((bf16[2,1552,128]{2,1,0:T(8,128)(2,1)S(1)}, bf16[2,1552,128]{2,1,0:T(8,128)(2,1)S(1)}, u32[]{:S(2)}, u32[]{:S(2)}) %collective-permute-start.4) | collective-permute-done | bytes 794656 | tf_op jit(solution)/shard_map/ppermute | solution.py:487
  23.1 5.2 %shard_map.119.acc_in = f32[2,2048,128]{2,1,0:T(8,128)S(1)} custom-call(bf16[2,1552,128]{2,1,0:T(8,128)(2,1)S(1)} %get-tuple-element.13.pay_ref), custom_call_target="tpu_custom_call" | custom-call | flops 4294967296 | bytes 794624 | tf_op jit(solution)/shard_map/pallas_call | solution.py:35
  28.4 2.5 %collective-permute-start.9 = (bf16[384,128]{1,0:T(8,128)(2,1)S(1)}, bf16[384,128]{1,0:T(8,128)(2,1)S(1)}, u32[]{:S(2)}, u32[]{:S(2)}) collective-permute-start(bf16[384,128]{1,0:T(8,128)(2,1)S(1)} %get-tuple-element.20.own_ref), channel_id=1, source_target_pairs={{0,24},{8,16},{16,8},{24,0},{1,25},{9,17},{17,9},{25,1},{2,26},{10... | collective-permute-start | bytes 294920 | tf_op jit(solution)/shard_map/ppermute | solution.py:487
  30.9 0.2 collective-permute-start.3
  31.1 3.5 %shard_map.120 = (f32[2,2048,128]{2,1,0:T(8,128)S(1)}, bf16[2,2048,64]{2,1,0:T(8,128)(2,1)S(1)}, f32[16,128]{1,0:T(8,128)S(1)}) custom-call(s32[1,8]{1,0:T(1,128)S(1)} %copy-done.5, bf16[2,1552,128]{2,1,0:T(8,128)(2,1)S(1)} %get-tuple-element.13.pay_ref, bf16[2,1552,128]{2,1,0:T(8,128)(2,1)S(1)} %collective-permute-done.partner_ref, ...), custom_call_target="tpu_custom_call", output_to_operand_aliasing={{0}: (3, {})} | custom-call | flops 4294967296 | bytes 3686432 | tf_op jit(solution)/shard_map/pallas_call | solution.py:35
  34.6 3.5 %shard_map.121.acc_in = f32[2,2048,128]{2,1,0:T(8,128)S(1)} custom-call(s32[1,8]{1,0:T(1,128)S(1)} %copy-done.5, f32[16,128]{1,0:T(8,128)S(1)} %get-tuple-element.15.row_in, bf16[2,2048,64]{2,1,0:T(8,128)(2,1)S(1)} %get-tuple-element.14.left_ref, bf16[2,1552,128]{2,1,0:T(8,128)(2,1)S(1)} %collective-permute-done.4.full_ref, ...), custom_call_target="tpu_custom_call", output_to_operand_aliasing={{}: (5, {})} | custom-call | flops 8589934592 | bytes 4218912 | tf_op jit(solution)/shard_map/pallas_call | solution.py:35
  38.1 0.0 copy-start.3
  38.1 0.0 copy-start.8
  38.1 3.4 %shard_map.122 = (f32[2,2048,128]{2,1,0:T(8,128)S(1)}, f32[2048,128]{1,0:T(8,128)S(1)}) custom-call(s32[1,8]{1,0:T(1,128)S(1)} %copy-done.5, f32[16,128]{1,0:T(8,128)S(1)} %get-tuple-element.15.row_in, bf16[2,2048,64]{2,1,0:T(8,128)(2,1)S(1)} %get-tuple-element.14.left_ref, ...), custom_call_target="tpu_custom_call", output_to_operand_aliasing={{0}: (5, {})} | custom-call | flops 8589934592 | bytes 4218912 | tf_op jit(solution)/shard_map/pallas_call | solution.py:35
  41.6 0.0 copy-start.7
  41.6 0.3 collective-permute-start.6
  42.0 1.3 %shard_map.124.mine_ref = bf16[640,128]{1,0:T(8,128)(2,1)S(1)} custom-call(s32[1,4]{1,0:T(1,128)S(1)} %copy-done.8, bf16[1,64,256]{2,1,0:T(8,128)(2,1)S(1)} %bitcast.5, bf16[384,128]{1,0:T(8,128)(2,1)S(1)} %get-tuple-element.19.down_ref, bf16[384,128]{1,0:T(8,128)(2,1)S(1)} %get-tuple-element.20.own_ref, ...), custom_call_target="tpu_custom_call" | custom-call | flops 268435456 | bytes 524304 | tf_op jit(solution)/shard_map/pallas_call | solution.py:35
  43.3 9.1 %collective-permute-start.10 = (bf16[640,128]{1,0:T(8,128)(2,1)S(1)}, bf16[640,128]{1,0:T(8,128)(2,1)S(1)}, u32[]{:S(2)}, u32[]{:S(2)}) collective-permute-start(bf16[640,128]{1,0:T(8,128)(2,1)S(1)} %shard_map.124.mine_ref), channel_id=1, source_target_pairs={{0,4},{1,5},{2,6},{3,7},{4,0},{5,1},{6,2},{7,3},{8,12},{9,13},{10,... | collective-permute-start | bytes 491528 | tf_op jit(solution)/shard_map/ppermute | solution.py:487
  52.4 1.5 %collective-permute-start.2 = (bf16[2,1552,128]{2,1,0:T(8,128)(2,1)S(1)}, bf16[2,1552,128]{2,1,0:T(8,128)(2,1)S(1)}, u32[]{:S(2)}, u32[]{:S(2)}) collective-permute-start(bf16[2,1552,128]{2,1,0:T(8,128)(2,1)S(1)} %collective-permute-done.1.full_ref), channel_id=1, source_target_pairs={{0,2},{2,4},{3,1},{4,6},{5,3},{7,5},{8,10},{10,12},{11,9},{12,14},... | collective-permute-start | bytes 2383880 | tf_op jit(solution)/shard_map/ppermute | solution.py:487
  53.9 6.7 %collective-permute-done.10.got_ref = bf16[640,128]{1,0:T(8,128)(2,1)S(1)} collective-permute-done((bf16[640,128]{1,0:T(8,128)(2,1)S(1)}, bf16[640,128]{1,0:T(8,128)(2,1)S(1)}, u32[]{:S(2)}, u32[]{:S(2)}) %collective-permute-start.10) | collective-permute-done | bytes 163872 | tf_op jit(solution)/shard_map/ppermute | solution.py:487
  60.6 0.1 collective-permute-start.11
  60.7 13.9 %collective-permute-done.11.got_ref = bf16[1024,128]{1,0:T(8,128)(2,1)S(1)} collective-permute-done((bf16[1024,128]{1,0:T(8,128)(2,1)S(1)}, bf16[1024,128]{1,0:T(8,128)(2,1)S(1)}, u32[]{:S(2)}, u32[]{:S(2)}) %collective-permute-start.11) | collective-permute-done | bytes 262176 | tf_op jit(solution)/shard_map/ppermute | solution.py:487
  74.7 0.0 copy-start.2
  74.7 0.0 copy-start.4
  74.7 0.0 copy-start.1
  74.7 0.0 copy-start.10
  74.7 0.1 collective-permute-start.12
  74.8 4.1 %shard_map.123.wanted_ref = f32[2048,128]{1,0:T(8,128)S(1)} custom-call(s32[1,2048]{1,0:T(1,128)S(1)} %copy-done.7, f32[2048,128]{1,0:T(8,128)S(1)} %copy-done.6), custom_call_target="tpu_custom_call" | custom-call | flops 2147483648 | bytes 1056768 | tf_op jit(solution)/shard_map/pallas_call | solution.py:35
  79.0 2.4 %shard_map.127.local_ref = bf16[256,128]{1,0:T(8,128)(2,1)S(1)} custom-call(s32[1,8]{1,0:T(1,128)S(1)} %copy-done.9, bf16[1,64,256]{2,1,0:T(8,128)(2,1)S(1)} %bitcast.7, bf16[1,256,256]{2,1,0:T(8,128)(2,1)S(1)} %copy-done.2, bf16[1792,128]{1,0:T(8,128)(2,1)S(1)} %shard_map.126.mine_ref, bf16[1792,128]{1,0:T(8,128)(2,1)S(1)} %collective-permute-done.12.got_ref), custom_call_target="tpu_custom_call" | custom-call | flops 536870912 | bytes 1081376 | tf_op jit(solution)/shard_map/pallas_call | solution.py:35
  81.5 6.9 %shard_map.128 = f32[2048,128]{1,0:T(8,128)} custom-call(s32[1,8]{1,0:T(1,128)S(1)} %copy-done.5, bf16[2,1552,128]{2,1,0:T(8,128)(2,1)S(1)} %get-tuple-element.13.pay_ref, bf16[2,2048,64]{2,1,0:T(8,128)(2,1)S(1)} %get-tuple-element.14.left_ref, bf16[2,1552,128]{2,1,0:T(8,128)(2,1)S(1)} %collective-permute-done.2.third_ref, ...), custom_call_target="tpu_custom_call" | custom-call | flops 4294967296 | bytes 8471072 | tf_op jit(solution)/shard_map/pallas_call | solution.py:35
  (27 shorter events, 0.1 us)
Async XLA Ops:
  2.4 20.7 %collective-permute-start.4 = (bf16[2,1552,128]{2,1,0:T(8,128)(2,1)S(1)}, bf16[2,1552,128]{2,1,0:T(8,128)(2,1)S(1)}, u32[]{:S(2)}, u32[]{:S(2)}) collective-permute-start(bf16[2,1552,128]{2,1,0:T(8,128)(2,1)S(1)} %get-tuple-element.13.pay_ref), channel_id=1, source_target_pairs={{0,2},{2,4},{3,1},{4,6},{5,3},{7,5},{8,10},{10,12},{11,9},{12,14},... | collective-permute-start | bytes 2383880 | tf_op jit(solution)/shard_map/ppermute | solution.py:487
  3.7 24.6 %collective-permute-start = (bf16[2,1552,128]{2,1,0:T(8,128)(2,1)S(1)}, bf16[2,1552,128]{2,1,0:T(8,128)(2,1)S(1)}, u32[]{:S(2)}, u32[]{:S(2)}) collective-permute-start(bf16[2,1552,128]{2,1,0:T(8,128)(2,1)S(1)} %get-tuple-element.13.pay_ref), channel_id=1, source_target_pairs={{0,1},{1,0},{2,3},{3,2},{4,5},{5,4},{6,7},{7,6},{8,9},{9,8},{10,11... | collective-permute-start | bytes 2383880 | tf_op jit(solution)/shard_map/ppermute | solution.py:487
  4.5 26.4 %collective-permute-start.1 = (bf16[2,1552,128]{2,1,0:T(8,128)(2,1)S(1)}, bf16[2,1552,128]{2,1,0:T(8,128)(2,1)S(1)}, u32[]{:S(2)}, u32[]{:S(2)}) collective-permute-start(bf16[2,1552,128]{2,1,0:T(8,128)(2,1)S(1)} %get-tuple-element.13.pay_ref), channel_id=1, source_target_pairs={{1,2},{2,1},{3,4},{4,3},{5,6},{6,5},{9,10},{10,9},{11,12},{12,11},... | collective-permute-start | bytes 2383880 | tf_op jit(solution)/shard_map/ppermute | solution.py:487
  8.4 22.7 %copy-start.5 = (s32[1,8]{1,0:T(1,128)S(1)}, s32[1,8]{1,0:T(1,128)}, u32[]{:S(2)}) copy-start(s32[1,8]{1,0:T(1,128)} %near_ref.7) | copy-start | bytes 100
  8.5 33.5 %collective-permute-start.7 = (bf16[384,128]{1,0:T(8,128)(2,1)S(1)}, bf16[384,128]{1,0:T(8,128)(2,1)S(1)}, u32[]{:S(2)}, u32[]{:S(2)}) collective-permute-start(bf16[384,128]{1,0:T(8,128)(2,1)S(1)} %get-tuple-element.20.own_ref), channel_id=1, source_target_pairs={{0,8},{8,0},{16,24},{24,16},{1,9},{9,1},{17,25},{25,17},{2,10},{10... | collective-permute-start | bytes 294920 | tf_op jit(solution)/shard_map/ppermute | solution.py:487
  10.0 31.9 %collective-permute-start.8 = (bf16[384,128]{1,0:T(8,128)(2,1)S(1)}, bf16[384,128]{1,0:T(8,128)(2,1)S(1)}, u32[]{:S(2)}, u32[]{:S(2)}) collective-permute-start(bf16[384,128]{1,0:T(8,128)(2,1)S(1)} %get-tuple-element.20.own_ref), channel_id=1, source_target_pairs={{0,16},{8,24},{16,0},{24,8},{1,17},{9,25},{17,1},{25,9},{2,18},{10... | collective-permute-start | bytes 294920 | tf_op jit(solution)/shard_map/ppermute | solution.py:487
  23.1 11.5 %collective-permute-start.5 = (bf16[2,1552,128]{2,1,0:T(8,128)(2,1)S(1)}, bf16[2,1552,128]{2,1,0:T(8,128)(2,1)S(1)}, u32[]{:S(2)}, u32[]{:S(2)}) collective-permute-start(bf16[2,1552,128]{2,1,0:T(8,128)(2,1)S(1)} %collective-permute-done.4.full_ref), channel_id=1, source_target_pairs={{0,1},{1,0},{2,3},{3,2},{4,5},{5,4},{6,7},{7,6},{8,9},{9,8},{10,11... | collective-permute-start | bytes 2383880 | tf_op jit(solution)/shard_map/ppermute | solution.py:487
  28.4 13.6 %collective-permute-start.9 = (bf16[384,128]{1,0:T(8,128)(2,1)S(1)}, bf16[384,128]{1,0:T(8,128)(2,1)S(1)}, u32[]{:S(2)}, u32[]{:S(2)}) collective-permute-start(bf16[384,128]{1,0:T(8,128)(2,1)S(1)} %get-tuple-element.20.own_ref), channel_id=1, source_target_pairs={{0,24},{8,16},{16,8},{24,0},{1,25},{9,17},{17,9},{25,1},{2,26},{10... | collective-permute-start | bytes 294920 | tf_op jit(solution)/shard_map/ppermute | solution.py:487
  30.9 7.2 %collective-permute-start.3 = (bf16[2,1552,128]{2,1,0:T(8,128)(2,1)S(1)}, bf16[2,1552,128]{2,1,0:T(8,128)(2,1)S(1)}, u32[]{:S(2)}, u32[]{:S(2)}) collective-permute-start(bf16[2,1552,128]{2,1,0:T(8,128)(2,1)S(1)} %collective-permute-done.1.full_ref), channel_id=1, source_target_pairs={{0,1},{1,0},{2,3},{3,2},{4,5},{5,4},{6,7},{7,6},{8,9},{9,8},{10,11... | collective-permute-start | bytes 2383880 | tf_op jit(solution)/shard_map/ppermute | solution.py:487
  38.1 3.8 %copy-start.3 = (bf16[1,256,64]{1,2,0:T(8,128)(2,1)S(1)}, bf16[1,256,64]{1,2,0:T(8,128)(2,1)}, u32[]{:S(2)}) copy-start(bf16[1,256,64]{1,2,0:T(8,128)(2,1)} %param.20) | copy-start | bytes 98308
  38.1 3.8 %copy-start.8 = (s32[1,4]{1,0:T(1,128)S(1)}, s32[1,4]{1,0:T(1,128)}, u32[]{:S(2)}) copy-start(s32[1,4]{1,0:T(1,128)} %far_ref.2) | copy-start | bytes 52
  41.6 33.3 %copy-start.6 = (f32[2048,128]{1,0:T(8,128)S(1)}, f32[2048,128]{1,0:T(8,128)}, u32[]{:S(2)}) copy-start(f32[2048,128]{1,0:T(8,128)} %target_hbm.1) | copy-start | bytes 3145732
  41.6 33.2 %copy-start.7 = (s32[1,2048]{1,0:T(1,128)S(1)}, s32[1,2048]{1,0:T(1,128)}, u32[]{:S(2)}) copy-start(s32[1,2048]{1,0:T(1,128)} %order_ref.1) | copy-start | bytes 24580
  41.6 39.9 %collective-permute-start.6 = (f32[2048,128]{1,0:T(8,128)S(1)}, f32[2048,128]{1,0:T(8,128)S(1)}, u32[]{:S(2)}, u32[]{:S(2)}) collective-permute-start(f32[2048,128]{1,0:T(8,128)S(1)} %get-tuple-element.18), channel_id=1, source_target_pairs={{0,1},{1,0},{2,3},{3,2},{4,5},{5,4},{6,7},{7,6},{8,9},{9,8},{10,11... | collective-permute-start | bytes 3145736 | tf_op jit(solution)/shard_map/ppermute | solution.py:487
  43.3 17.3 %collective-permute-start.10 = (bf16[640,128]{1,0:T(8,128)(2,1)S(1)}, bf16[640,128]{1,0:T(8,128)(2,1)S(1)}, u32[]{:S(2)}, u32[]{:S(2)}) collective-permute-start(bf16[640,128]{1,0:T(8,128)(2,1)S(1)} %shard_map.124.mine_ref), channel_id=1, source_target_pairs={{0,4},{1,5},{2,6},{3,7},{4,0},{5,1},{6,2},{7,3},{8,12},{9,13},{10,... | collective-permute-start | bytes 491528 | tf_op jit(solution)/shard_map/ppermute | solution.py:487
  52.4 29.0 %collective-permute-start.2 = (bf16[2,1552,128]{2,1,0:T(8,128)(2,1)S(1)}, bf16[2,1552,128]{2,1,0:T(8,128)(2,1)S(1)}, u32[]{:S(2)}, u32[]{:S(2)}) collective-permute-start(bf16[2,1552,128]{2,1,0:T(8,128)(2,1)S(1)} %collective-permute-done.1.full_ref), channel_id=1, source_target_pairs={{0,2},{2,4},{3,1},{4,6},{5,3},{7,5},{8,10},{10,12},{11,9},{12,14},... | collective-permute-start | bytes 2383880 | tf_op jit(solution)/shard_map/ppermute | solution.py:487
  60.6 14.0 %collective-permute-start.11 = (bf16[1024,128]{1,0:T(8,128)(2,1)S(1)}, bf16[1024,128]{1,0:T(8,128)(2,1)S(1)}, u32[]{:S(2)}, u32[]{:S(2)}) collective-permute-start(bf16[1024,128]{1,0:T(8,128)(2,1)S(1)} %shard_map.125.mine_ref), channel_id=1, source_target_pairs={{0,2},{1,3},{2,0},{3,1},{4,6},{5,7},{6,4},{7,5},{8,10},{9,11},{10,... | collective-permute-start | bytes 786440 | tf_op jit(solution)/shard_map/ppermute | solution.py:487
  74.7 4.3 %copy-start.2 = (bf16[1,256,256]{2,1,0:T(8,128)(2,1)S(1)}, bf16[1,256,256]{2,1,0:T(8,128)(2,1)}, u32[]{:S(2)}) copy-start(bf16[1,256,256]{2,1,0:T(8,128)(2,1)} %transfer_ref.1) | copy-start | bytes 393220
  74.7 4.3 %copy-start.4 = (bf16[1,256,64]{1,2,0:T(8,128)(2,1)S(1)}, bf16[1,256,64]{1,2,0:T(8,128)(2,1)}, u32[]{:S(2)}) copy-start(bf16[1,256,64]{1,2,0:T(8,128)(2,1)} %param.19) | copy-start | bytes 98308
  74.7 4.3 %copy-start.9 = (s32[1,8]{1,0:T(1,128)S(1)}, s32[1,8]{1,0:T(1,128)}, u32[]{:S(2)}) copy-start(s32[1,8]{1,0:T(1,128)} %far_ref.3) | copy-start | bytes 100
  74.7 6.8 %copy-start = (f32[2048,128]{1,0:T(8,128)S(1)}, f32[2048,128]{1,0:T(8,128)}, u32[]{:S(2)}) copy-start(f32[2048,128]{1,0:T(8,128)} %iterate_ref.1) | copy-start | bytes 3145732
  74.7 6.8 %copy-start.1 = (bf16[2048,256]{1,0:T(8,128)(2,1)S(1)}, bf16[2048,256]{1,0:T(8,128)(2,1)}, u32[]{:S(2)}) copy-start(bf16[2048,256]{1,0:T(8,128)(2,1)} %basis_ref.1) | copy-start | bytes 3145732
  74.7 6.8 %copy-start.10 = (f32[128]{0:T(128)S(1)}, f32[128]{0:T(128)}, u32[]{:S(2)}) copy-start(f32[128]{0:T(128)} %param.16) | copy-start | bytes 1540
  74.7 4.2 %collective-permute-start.12 = (bf16[1792,128]{1,0:T(8,128)(2,1)S(1)}, bf16[1792,128]{1,0:T(8,128)(2,1)S(1)}, u32[]{:S(2)}, u32[]{:S(2)}) collective-permute-start(bf16[1792,128]{1,0:T(8,128)(2,1)S(1)} %shard_map.126.mine_ref), channel_id=1, source_target_pairs={{0,1},{1,0},{2,3},{3,2},{4,5},{5,4},{6,7},{7,6},{8,9},{9,8},{10,11... | collective-permute-start | bytes 1376264 | tf_op jit(solution)/shard_map/ppermute | solution.py:487

commit v2 on v1

--- a/solution.py
+++ b/solution.py
@@ -129,7 +129,8 @@
         offset_ref[0:1, b * LANES : (b + 1) * LANES] = -norms(doubled_block(plan, ref, b)) - SHIFT
 
 
-def half_tile(plan, acc_ref, left_ref, source_ref, offset_ref):
+def half_tile(plan, acc_ref, left_ref, source_ref, offset_ref, beside=None):
+    step = 0
     for r in range(0, plan.n, ROWS):
         left = left_ref[r : r + ROWS, :]
         total = acc_ref[r : r + ROWS, :]
@@ -140,6 +141,9 @@
             )
             power = matmul(left, right) * LOG2E + offset_ref[0:1, cols]
             total = total + matmul(jnp.exp2(power).astype(BF16), source_ref[cols, :])
+            if beside is not None:
+                beside(step)
+            step += 1
         acc_ref[r : r + ROWS, :] = total
 
 
@@ -221,21 +225,32 @@
     )
 
 
-def own_tile(plan, pay):
-    def kernel(pay_ref, acc_ref, left_ref, offset_ref):
+def own_tile(plan, pay, ordering, target):
+    group = 8
+    steps = (plan.n // ROWS) * (plan.half // COLS)
+
+    def kernel(pay_ref, order_ref, target_ref, acc_ref, wanted_ref, left_ref, offset_ref):
         acc_ref[...] = jnp.zeros_like(acc_ref)
         for h in range(2):
             fill_left(plan, left_ref, pay_ref.at[h], h)
 
         @pl.loop(0, 2)
         def _(h):
+            def gather(step):
+                rows = plan.half // steps
+                for k in range(step * rows, (step + 1) * rows, group):
+                    first = pl.multiple_of(h * plan.half + k, group)
+                    wanted_ref[pl.ds(first, group), :] = jnp.concatenate(
+                        [target_ref[pl.ds(order_ref[0, first + u], 1), :] for u in range(group)], axis=0
+                    )
+
             fill_offset(plan, offset_ref, pay_ref.at[h])
-            half_tile(plan, acc_ref.at[0], left_ref, pay_ref.at[h], offset_ref)
-
-    return call(
-        kernel,
-        plan.acc(),
-        [(pay, VMEM)],
+            half_tile(plan, acc_ref.at[0], left_ref, pay_ref.at[h], offset_ref, gather)
+
+    return call(
+        kernel,
+        [plan.acc(), shaped(plan.n, plan.rhs, dtype=F32)],
+        [(pay, VMEM), (ordering, SMEM), (target, VMEM)],
         scratch=[VMEM(plan.left().shape[1:], BF16)] + plan.offset_scratch(),
         flops=plan.tile_flops,
     )
@@ -295,9 +310,9 @@
                     half_tile(plan, acc_ref.at[t], left_ref.at[t], source, offset_ref)
 
         if last:
-            refs[0][...] = acc_ref[1]
-
-    outs = [plan.acc()] + ([shaped(plan.n, plan.rhs, dtype=F32)] if last else [])
+            refs[0][...] = acc_ref[1].astype(BF16)
+
+    outs = [plan.acc()] + ([shaped(plan.n, plan.rhs)] if last else [])
     return call(
         kernel,
         outs,
@@ -308,48 +323,11 @@
     )
 
 
-def wanted_rows(ordering, target):
-    n, rhs = target.shape
-    step = 2 * LANES
-
-    def kernel(order_ref, target_hbm, out_ref, target_ref, halves_ref, sem):
-        copy = pltpu.make_async_copy(target_hbm, target_ref, sem)
-        copy.start()
-        copy.wait()
-        value = target_ref[...]
-        high = value.astype(BF16)
-        halves_ref[:, 0:rhs] = high
-        halves_ref[:, rhs:] = (value - high.astype(F32)).astype(BF16)
-        lane = lax.broadcasted_iota(jnp.int32, (LANES, LANES), 1).astype(F32)
-
-        @pl.loop(0, n // step)
-        def _(i):
-            picks = []
-            for k in range(step // LANES):
-                rows = pl.ds(pl.multiple_of(i * step + k * LANES, LANES), LANES)
-                index = jnp.broadcast_to(order_ref[:, rows].astype(F32), (LANES, LANES)).T
-                picks.append(
-                    jnp.concatenate(
-                        [jnp.where(index == lane + c, 1.0, 0.0).astype(BF16) for c in range(0, n, LANES)], axis=1
-                    )
-                )
-            both = matmul(jnp.concatenate(picks, axis=0), halves_ref[...])
-            out_ref[pl.ds(pl.multiple_of(i * step, step), step), :] = both[:, 0:rhs] + both[:, rhs:]
-
-    return call(
-        kernel,
-        shaped(n, rhs, dtype=F32),
-        [(ordering, VMEM), (target, HBM)],
-        scratch=[VMEM((n, rhs), F32), VMEM((n, 2 * rhs), BF16), pltpu.SemaphoreType.DMA],
-        flops=n * n * 512,
-    )
-
-
 def last_tile(plan, near_row, pay, left, third, acc, returned, iterate, wanted, step_size, basis, local):
     def kernel(near_ref, pay_ref, left_ref, third_ref, acc_ref, returned_ref, iterate_ref, wanted_ref, step_ref, basis_ref, local_ref, out_hbm, out_ref, offset_ref, sems):
         place = lax.axis_index("leaf")
         away = 2 * lax.rem(place, 2) - 1
-        out_ref[...] = acc_ref[0] + returned_ref[...]
+        out_ref[...] = acc_ref[0] + returned_ref[...].astype(F32)
 
         @pl.when(listed(near_ref, place + 3 * away))
         def _():
@@ -444,13 +422,17 @@
 
 def joined(mine, got, rank):
     rows = mine.shape[0] - rank
-
-    def kernel(mine_ref, got_ref, out_ref):
-        out_ref[0:rows, :] = mine_ref[0:rows, :]
-        out_ref[rows : 2 * rows, :] = got_ref[0:rows, :]
-        out_ref[2 * rows :, :] = (mine_ref[rows:, :].astype(F32) + got_ref[rows:, :].astype(F32)).astype(BF16)
-
-    return call(kernel, shaped(2 * rows + rank, LANES), [(mine, VMEM), (got, VMEM)])
+    count = 1 + len(got)
+
+    def kernel(*refs):
+        out_ref = refs[-1]
+        share = jnp.zeros((rank, LANES), F32)
+        for k, ref in enumerate(refs[:-1]):
+            out_ref[k * rows : (k + 1) * rows, :] = ref[0:rows, :]
+            share = share + ref[rows:, :].astype(F32)
+        out_ref[count * rows :, :] = share.astype(BF16)
+
+    return call(kernel, shaped(count * rows + rank, LANES), [(b, VMEM) for b in (mine, *got)])
 
 
 def down(far_row, leaf_t, transfer, mine, got, xors):
@@ -526,18 +508,16 @@
     partner = routed(pay, "leaf", on_chip)
     over = routed(pay, "leaf", over_chips)
     others = [routed(up_block, "group", lambda i, k=k: i ^ k) for k in range(1, groups)]
-    acc = own_tile(plan, pay)
+    acc, wanted = own_tile(plan, pay, ordering, target)
     mine = across(cluster_far, cluster_t, up_block, others, lambda me, k: me ^ (k + 1), down_block)
     acc, left, row = pair_tiles(plan, near_table, pay, partner, acc)
 
-    xors, bit = [0], leaves // 2
-    while True:
-        got = routed(mine, "leaf", lambda i, bit=bit: i ^ bit)
-        xors = xors + [x ^ bit for x in xors]
-        if bit == 1:
-            break
-        mine = joined(mine, got, rank)
-        bit //= 2
+    even = list(range(2, leaves, 2))[::-1]
+    blocks = [routed(mine, "leaf", lambda i, other=other: i ^ other) for other in even]
+    mine = joined(mine, blocks, rank)
+    got = routed(mine, "leaf", on_chip)
+    xors = [0] + even
+    xors = xors + [x ^ 1 for x in xors]
     local = down(far_table, leaf_t, transfer, mine, got, xors)
 
     beside = routed(pay, "leaf", beside_chips)
@@ -547,7 +527,6 @@
     third = routed(beside, "leaf", over_chips)
     acc, theirs = side_tiles(plan, near_table, row, left, beside, beside_passed, acc, 1, True)
     returned = routed(theirs, "leaf", on_chip)
-    wanted = wanted_rows(ordering, target)
     return last_tile(
         plan, near_table, pay, left, third, acc, returned, iterate, wanted, step_size, leaf_basis, local
     )

time: 88.8 us -> 74.1 us (0.83)
  the two profiles are of different devices: /device:TPU:24 before, /device:TPU:15 now
where the time goes in v2:
time: 74.1 us; the launch traced here: 73.9 us
  Pallas kernels  40.6 us (55%)
  starting transfers between devices  22.1 us (30%)
  waiting for transfers between devices  10.6 us (14%)
    pallas_call x9, Pallas kernels, call(): pl.pallas_call(kernel, out_shape=shapes, in_specs=[pl.BlockSpec(memory_sp...  40.6 us
    ppermute x14, starting transfers between devices, routed(): return lax.ppermute(block, axis, route)  22.1 us
    ppermute x14, waiting for transfers between devices, routed(): return lax.ppermute(block, axis, route)  10.6 us
  transfers between devices with their start and end apart: 14, of which 3 were waited for; matrix products, arithmetic and copies ran while one was open for 0% of the time, Pallas kernels for 42%

profile of v2, /device:TPU:15, one launch (start us, length us, event | category | flops | bytes accessed | tf_op | source)
XLA Modules:
  0.0 73.9 jit_solution(821181982129248364)
XLA Ops:
  0.0 2.5 %shard_map.118 = (bf16[2,1552,128]{2,1,0:T(8,128)(2,1)S(1)}, bf16[384,128]{1,0:T(8,128)(2,1)S(1)}, bf16[384,128]{1,0:T(8,128)(2,1)S(1)}) custom-call(bf16[64,2048]{1,0:T(8,128)(2,1)} %bitcast.9, f32[2048,128]{1,0:T(8,128)} %iterate_ref.1, s32[1,8]{1,0:T(1,128)} %near_ref.7, bf16[1,64,256]{2,1,0:T(8,128)(2,1)} %bitcast.6, bf16[1,64,256]{2,1,0:T(8,128)(2,1)} %bitcast.4, ...), custom_call_target="tpu_custom_call" | custom-call | flops 134217728 | bytes 2555936 | tf_op jit(solution)/shard_map/pallas_call | solution.py:35
  2.5 2.1 %collective-permute-start.4 = (bf16[2,1552,128]{2,1,0:T(8,128)(2,1)S(1)}, bf16[2,1552,128]{2,1,0:T(8,128)(2,1)S(1)}, u32[]{:S(2)}, u32[]{:S(2)}) collective-permute-start(bf16[2,1552,128]{2,1,0:T(8,128)(2,1)S(1)} %get-tuple-element.15.pay_ref), channel_id=1, source_target_pairs={{0,2},{2,4},{3,1},{4,6},{5,3},{7,5},{8,10},{10,12},{11,9},{12,14},... | collective-permute-start | bytes 2383880 | tf_op jit(solution)/shard_map/ppermute | solution.py:469
  4.6 2.1 %collective-permute-start = (bf16[2,1552,128]{2,1,0:T(8,128)(2,1)S(1)}, bf16[2,1552,128]{2,1,0:T(8,128)(2,1)S(1)}, u32[]{:S(2)}, u32[]{:S(2)}) collective-permute-start(bf16[2,1552,128]{2,1,0:T(8,128)(2,1)S(1)} %get-tuple-element.15.pay_ref), channel_id=1, source_target_pairs={{0,1},{1,0},{2,3},{3,2},{4,5},{5,4},{6,7},{7,6},{8,9},{9,8},{10,11... | collective-permute-start | bytes 2383880 | tf_op jit(solution)/shard_map/ppermute | solution.py:469
  6.7 3.1 %collective-permute-start.1 = (bf16[2,1552,128]{2,1,0:T(8,128)(2,1)S(1)}, bf16[2,1552,128]{2,1,0:T(8,128)(2,1)S(1)}, u32[]{:S(2)}, u32[]{:S(2)}) collective-permute-start(bf16[2,1552,128]{2,1,0:T(8,128)(2,1)S(1)} %get-tuple-element.15.pay_ref), channel_id=1, source_target_pairs={{1,2},{2,1},{3,4},{4,3},{5,6},{6,5},{9,10},{10,9},{11,12},{12,11},... | collective-permute-start | bytes 2383880 | tf_op jit(solution)/shard_map/ppermute | solution.py:469
  9.8 0.0 copy-start.3
  9.9 0.0 copy-start.5
  9.9 0.3 collective-permute-start.7
  10.2 0.2 collective-permute-start.8
  10.4 4.2 %collective-permute-done.7.refs_0_ = bf16[384,128]{1,0:T(8,128)(2,1)S(1)} collective-permute-done((bf16[384,128]{1,0:T(8,128)(2,1)S(1)}, bf16[384,128]{1,0:T(8,128)(2,1)S(1)}, u32[]{:S(2)}, u32[]{:S(2)}) %collective-permute-start.7) | collective-permute-done | bytes 98336 | tf_op jit(solution)/shard_map/ppermute | solution.py:469
  14.6 0.2 collective-permute-start.9
  14.8 4.5 %collective-permute-done.4.full_ref = bf16[2,1552,128]{2,1,0:T(8,128)(2,1)S(1)} collective-permute-done((bf16[2,1552,128]{2,1,0:T(8,128)(2,1)S(1)}, bf16[2,1552,128]{2,1,0:T(8,128)(2,1)S(1)}, u32[]{:S(2)}, u32[]{:S(2)}) %collective-permute-start.4) | collective-permute-done | bytes 794656 | tf_op jit(solution)/shard_map/ppermute | solution.py:469
  19.3 3.3 %collective-permute-start.5 = (bf16[2,1552,128]{2,1,0:T(8,128)(2,1)S(1)}, bf16[2,1552,128]{2,1,0:T(8,128)(2,1)S(1)}, u32[]{:S(2)}, u32[]{:S(2)}) collective-permute-start(bf16[2,1552,128]{2,1,0:T(8,128)(2,1)S(1)} %collective-permute-done.4.full_ref), channel_id=1, source_target_pairs={{0,1},{1,0},{2,3},{3,2},{4,5},{5,4},{6,7},{7,6},{8,9},{9,8},{10,11... | collective-permute-start | bytes 2383880 | tf_op jit(solution)/shard_map/ppermute | solution.py:469
  22.7 5.9 %shard_map.119 = (f32[2,2048,128]{2,1,0:T(8,128)S(1)}, f32[2048,128]{1,0:T(8,128)S(1)}) custom-call(bf16[2,1552,128]{2,1,0:T(8,128)(2,1)S(1)} %get-tuple-element.15.pay_ref, s32[1,2048]{1,0:T(1,128)S(1)} %copy-done.7, f32[2048,128]{1,0:T(8,128)S(1)} %copy-done.6), custom_call_target="tpu_custom_call" | custom-call | flops 4294967296 | bytes 1851392 | tf_op jit(solution)/shard_map/pallas_call | solution.py:35
  28.6 1.3 %shard_map.123.refs_0_ = bf16[640,128]{1,0:T(8,128)(2,1)S(1)} custom-call(s32[1,4]{1,0:T(1,128)S(1)} %copy-done.8, bf16[1,64,256]{2,1,0:T(8,128)(2,1)S(1)} %bitcast.5, bf16[384,128]{1,0:T(8,128)(2,1)S(1)} %get-tuple-element.23.down_ref, bf16[384,128]{1,0:T(8,128)(2,1)S(1)} %get-tuple-element.24.own_ref, bf16[384,128]{1,0:T(8,128)(2,1)S(1)} %collective-permute-done.7.refs_0_, ...), custom_call_target="tpu_custom_call" | custom-call | flops 268435456 | bytes 524304 | tf_op jit(solution)/shard_map/pallas_call | solution.py:35
  30.0 1.7 %collective-permute-start.10 = (bf16[640,128]{1,0:T(8,128)(2,1)S(1)}, bf16[640,128]{1,0:T(8,128)(2,1)S(1)}, u32[]{:S(2)}, u32[]{:S(2)}) collective-permute-start(bf16[640,128]{1,0:T(8,128)(2,1)S(1)} %shard_map.123.refs_0_), channel_id=1, source_target_pairs={{0,6},{1,7},{2,4},{3,5},{4,2},{5,3},{6,0},{7,1},{8,14},{9,15},{10,... | collective-permute-start | bytes 491528 | tf_op jit(solution)/shard_map/ppermute | solution.py:469
  31.6 2.0 %collective-permute-start.11 = (bf16[640,128]{1,0:T(8,128)(2,1)S(1)}, bf16[640,128]{1,0:T(8,128)(2,1)S(1)}, u32[]{:S(2)}, u32[]{:S(2)}) collective-permute-start(bf16[640,128]{1,0:T(8,128)(2,1)S(1)} %shard_map.123.refs_0_), channel_id=1, source_target_pairs={{0,4},{1,5},{2,6},{3,7},{4,0},{5,1},{6,2},{7,3},{8,12},{9,13},{10,... | collective-permute-start | bytes 491528 | tf_op jit(solution)/shard_map/ppermute | solution.py:469
  33.6 1.1 %collective-permute-start.12 = (bf16[640,128]{1,0:T(8,128)(2,1)S(1)}, bf16[640,128]{1,0:T(8,128)(2,1)S(1)}, u32[]{:S(2)}, u32[]{:S(2)}) collective-permute-start(bf16[640,128]{1,0:T(8,128)(2,1)S(1)} %shard_map.123.refs_0_), channel_id=1, source_target_pairs={{0,2},{1,3},{2,0},{3,1},{4,6},{5,7},{6,4},{7,5},{8,10},{9,11},{10,... | collective-permute-start | bytes 491528 | tf_op jit(solution)/shard_map/ppermute | solution.py:469
  34.8 0.6 collective-permute-start.3
  35.3 3.5 %shard_map.120 = (f32[2,2048,128]{2,1,0:T(8,128)S(1)}, bf16[2,2048,64]{2,1,0:T(8,128)(2,1)S(1)}, f32[16,128]{1,0:T(8,128)S(1)}) custom-call(s32[1,8]{1,0:T(1,128)S(1)} %copy-done.5, bf16[2,1552,128]{2,1,0:T(8,128)(2,1)S(1)} %get-tuple-element.15.pay_ref, bf16[2,1552,128]{2,1,0:T(8,128)(2,1)S(1)} %collective-permute-done.partner_ref, ...), custom_call_target="tpu_custom_call", output_to_operand_aliasing={{0}: (3, {})} | custom-call | flops 4294967296 | bytes 3686432 | tf_op jit(solution)/shard_map/pallas_call | solution.py:35
  38.8 4.7 %collective-permute-start.2 = (bf16[2,1552,128]{2,1,0:T(8,128)(2,1)S(1)}, bf16[2,1552,128]{2,1,0:T(8,128)(2,1)S(1)}, u32[]{:S(2)}, u32[]{:S(2)}) collective-permute-start(bf16[2,1552,128]{2,1,0:T(8,128)(2,1)S(1)} %collective-permute-done.1.full_ref), channel_id=1, source_target_pairs={{0,2},{2,4},{3,1},{4,6},{5,3},{7,5},{8,10},{10,12},{11,9},{12,14},... | collective-permute-start | bytes 2383880 | tf_op jit(solution)/shard_map/ppermute | solution.py:469
  43.5 8.4 %shard_map.121.acc_in = f32[2,2048,128]{2,1,0:T(8,128)S(1)} custom-call(s32[1,8]{1,0:T(1,128)S(1)} %copy-done.5, f32[16,128]{1,0:T(8,128)S(1)} %get-tuple-element.18.row_in, bf16[2,2048,64]{2,1,0:T(8,128)(2,1)S(1)} %get-tuple-element.17.left_ref, bf16[2,1552,128]{2,1,0:T(8,128)(2,1)S(1)} %collective-permute-done.4.full_ref, ...), custom_call_target="tpu_custom_call", output_to_operand_aliasing={{}: (5, {})} | custom-call | flops 8589934592 | bytes 4218912 | tf_op jit(solution)/shard_map/pallas_call | solution.py:35
  52.0 0.0 copy-start.4
  52.0 0.0 copy-start.9
  52.0 10.8 %shard_map.122 = (f32[2,2048,128]{2,1,0:T(8,128)S(1)}, bf16[2048,128]{1,0:T(8,128)(2,1)S(1)}) custom-call(s32[1,8]{1,0:T(1,128)S(1)} %copy-done.5, f32[16,128]{1,0:T(8,128)S(1)} %get-tuple-element.18.row_in, bf16[2,2048,64]{2,1,0:T(8,128)(2,1)S(1)} %get-tuple-element.17.left_ref, ...), custom_call_target="tpu_custom_call", output_to_operand_aliasing={{0}: (5, {})} | custom-call | flops 8589934592 | bytes 4218912 | tf_op jit(solution)/shard_map/pallas_call | solution.py:35
  62.8 0.0 copy-start.1
  62.8 0.0 copy-start.10
  62.8 0.1 collective-permute-start.6
  62.9 0.1 shard_map.124.mine_ref
  63.0 0.5 collective-permute-start.13
  63.6 1.9 %collective-permute-done.13.got_ref = bf16[1792,128]{1,0:T(8,128)(2,1)S(1)} collective-permute-done((bf16[1792,128]{1,0:T(8,128)(2,1)S(1)}, bf16[1792,128]{1,0:T(8,128)(2,1)S(1)}, u32[]{:S(2)}, u32[]{:S(2)}) %collective-permute-start.13) | collective-permute-done | bytes 458784 | tf_op jit(solution)/shard_map/ppermute | solution.py:469
  65.5 1.1 %shard_map.125.local_ref = bf16[256,128]{1,0:T(8,128)(2,1)S(1)} custom-call(s32[1,8]{1,0:T(1,128)S(1)} %copy-done.9, bf16[1,64,256]{2,1,0:T(8,128)(2,1)S(1)} %bitcast.7, bf16[1,256,256]{2,1,0:T(8,128)(2,1)S(1)} %copy-done.2, bf16[1792,128]{1,0:T(8,128)(2,1)S(1)} %shard_map.124.mine_ref, bf16[1792,128]{1,0:T(8,128)(2,1)S(1)} %collective-permute-done.13.got_ref), custom_call_target="tpu_custom_call" | custom-call | flops 536870912 | bytes 1081376 | tf_op jit(solution)/shard_map/pallas_call | solution.py:35
  66.6 7.1 %shard_map.126 = f32[2048,128]{1,0:T(8,128)} custom-call(s32[1,8]{1,0:T(1,128)S(1)} %copy-done.5, bf16[2,1552,128]{2,1,0:T(8,128)(2,1)S(1)} %get-tuple-element.15.pay_ref, bf16[2,2048,64]{2,1,0:T(8,128)(2,1)S(1)} %get-tuple-element.17.left_ref, bf16[2,1552,128]{2,1,0:T(8,128)(2,1)S(1)} %collective-permute-done.2.third_ref, ...), custom_call_target="tpu_custom_call" | custom-call | flops 4294967296 | bytes 7946784 | tf_op jit(solution)/shard_map/pallas_call | solution.py:35
  (27 shorter events, 0.1 us)
Async XLA Ops:
  0.0 22.7 %copy-start.7 = (s32[1,2048]{1,0:T(1,128)S(1)}, s32[1,2048]{1,0:T(1,128)}, u32[]{:S(2)}) copy-start(s32[1,2048]{1,0:T(1,128)} %order_ref.1) | copy-start | bytes 24580
  0.0 22.7 %copy-start.6 = (f32[2048,128]{1,0:T(8,128)S(1)}, f32[2048,128]{1,0:T(8,128)}, u32[]{:S(2)}) copy-start(f32[2048,128]{1,0:T(8,128)} %target_ref.1) | copy-start | bytes 3145732
  2.5 16.8 %collective-permute-start.4 = (bf16[2,1552,128]{2,1,0:T(8,128)(2,1)S(1)}, bf16[2,1552,128]{2,1,0:T(8,128)(2,1)S(1)}, u32[]{:S(2)}, u32[]{:S(2)}) collective-permute-start(bf16[2,1552,128]{2,1,0:T(8,128)(2,1)S(1)} %get-tuple-element.15.pay_ref), channel_id=1, source_target_pairs={{0,2},{2,4},{3,1},{4,6},{5,3},{7,5},{8,10},{10,12},{11,9},{12,14},... | collective-permute-start | bytes 2383880 | tf_op jit(solution)/shard_map/ppermute | solution.py:469
  4.6 29.1 %collective-permute-start = (bf16[2,1552,128]{2,1,0:T(8,128)(2,1)S(1)}, bf16[2,1552,128]{2,1,0:T(8,128)(2,1)S(1)}, u32[]{:S(2)}, u32[]{:S(2)}) collective-permute-start(bf16[2,1552,128]{2,1,0:T(8,128)(2,1)S(1)} %get-tuple-element.15.pay_ref), channel_id=1, source_target_pairs={{0,1},{1,0},{2,3},{3,2},{4,5},{5,4},{6,7},{7,6},{8,9},{9,8},{10,11... | collective-permute-start | bytes 2383880 | tf_op jit(solution)/shard_map/ppermute | solution.py:469
  6.7 28.0 %collective-permute-start.1 = (bf16[2,1552,128]{2,1,0:T(8,128)(2,1)S(1)}, bf16[2,1552,128]{2,1,0:T(8,128)(2,1)S(1)}, u32[]{:S(2)}, u32[]{:S(2)}) collective-permute-start(bf16[2,1552,128]{2,1,0:T(8,128)(2,1)S(1)} %get-tuple-element.15.pay_ref), channel_id=1, source_target_pairs={{1,2},{2,1},{3,4},{4,3},{5,6},{6,5},{9,10},{10,9},{11,12},{12,11},... | collective-permute-start | bytes 2383880 | tf_op jit(solution)/shard_map/ppermute | solution.py:469
  9.8 18.8 %copy-start.3 = (bf16[1,256,64]{1,2,0:T(8,128)(2,1)S(1)}, bf16[1,256,64]{1,2,0:T(8,128)(2,1)}, u32[]{:S(2)}) copy-start(bf16[1,256,64]{1,2,0:T(8,128)(2,1)} %param.20) | copy-start | bytes 98308
  9.9 18.8 %copy-start.8 = (s32[1,4]{1,0:T(1,128)S(1)}, s32[1,4]{1,0:T(1,128)}, u32[]{:S(2)}) copy-start(s32[1,4]{1,0:T(1,128)} %far_ref.2) | copy-start | bytes 52
  9.9 25.5 %copy-start.5 = (s32[1,8]{1,0:T(1,128)S(1)}, s32[1,8]{1,0:T(1,128)}, u32[]{:S(2)}) copy-start(s32[1,8]{1,0:T(1,128)} %near_ref.7) | copy-start | bytes 100
  9.9 4.7 %collective-permute-start.7 = (bf16[384,128]{1,0:T(8,128)(2,1)S(1)}, bf16[384,128]{1,0:T(8,128)(2,1)S(1)}, u32[]{:S(2)}, u32[]{:S(2)}) collective-permute-start(bf16[384,128]{1,0:T(8,128)(2,1)S(1)} %get-tuple-element.24.own_ref), channel_id=1, source_target_pairs={{0,8},{8,0},{16,24},{24,16},{1,9},{9,1},{17,25},{25,17},{2,10},{10... | collective-permute-start | bytes 294920 | tf_op jit(solution)/shard_map/ppermute | solution.py:469
  10.2 18.4 %collective-permute-start.8 = (bf16[384,128]{1,0:T(8,128)(2,1)S(1)}, bf16[384,128]{1,0:T(8,128)(2,1)S(1)}, u32[]{:S(2)}, u32[]{:S(2)}) collective-permute-start(bf16[384,128]{1,0:T(8,128)(2,1)S(1)} %get-tuple-element.24.own_ref), channel_id=1, source_target_pairs={{0,16},{8,24},{16,0},{24,8},{1,17},{9,25},{17,1},{25,9},{2,18},{10... | collective-permute-start | bytes 294920 | tf_op jit(solution)/shard_map/ppermute | solution.py:469
  14.6 14.0 %collective-permute-start.9 = (bf16[384,128]{1,0:T(8,128)(2,1)S(1)}, bf16[384,128]{1,0:T(8,128)(2,1)S(1)}, u32[]{:S(2)}, u32[]{:S(2)}) collective-permute-start(bf16[384,128]{1,0:T(8,128)(2,1)S(1)} %get-tuple-element.24.own_ref), channel_id=1, source_target_pairs={{0,24},{8,16},{16,8},{24,0},{1,25},{9,17},{17,9},{25,1},{2,26},{10... | collective-permute-start | bytes 294920 | tf_op jit(solution)/shard_map/ppermute | solution.py:469
  19.3 19.5 %collective-permute-start.5 = (bf16[2,1552,128]{2,1,0:T(8,128)(2,1)S(1)}, bf16[2,1552,128]{2,1,0:T(8,128)(2,1)S(1)}, u32[]{:S(2)}, u32[]{:S(2)}) collective-permute-start(bf16[2,1552,128]{2,1,0:T(8,128)(2,1)S(1)} %collective-permute-done.4.full_ref), channel_id=1, source_target_pairs={{0,1},{1,0},{2,3},{3,2},{4,5},{5,4},{6,7},{7,6},{8,9},{9,8},{10,11... | collective-permute-start | bytes 2383880 | tf_op jit(solution)/shard_map/ppermute | solution.py:469
  30.0 32.9 %collective-permute-start.10 = (bf16[640,128]{1,0:T(8,128)(2,1)S(1)}, bf16[640,128]{1,0:T(8,128)(2,1)S(1)}, u32[]{:S(2)}, u32[]{:S(2)}) collective-permute-start(bf16[640,128]{1,0:T(8,128)(2,1)S(1)} %shard_map.123.refs_0_), channel_id=1, source_target_pairs={{0,6},{1,7},{2,4},{3,5},{4,2},{5,3},{6,0},{7,1},{8,14},{9,15},{10,... | collective-permute-start | bytes 491528 | tf_op jit(solution)/shard_map/ppermute | solution.py:469
  31.6 31.3 %collective-permute-start.11 = (bf16[640,128]{1,0:T(8,128)(2,1)S(1)}, bf16[640,128]{1,0:T(8,128)(2,1)S(1)}, u32[]{:S(2)}, u32[]{:S(2)}) collective-permute-start(bf16[640,128]{1,0:T(8,128)(2,1)S(1)} %shard_map.123.refs_0_), channel_id=1, source_target_pairs={{0,4},{1,5},{2,6},{3,7},{4,0},{5,1},{6,2},{7,3},{8,12},{9,13},{10,... | collective-permute-start | bytes 491528 | tf_op jit(solution)/shard_map/ppermute | solution.py:469
  33.6 29.3 %collective-permute-start.12 = (bf16[640,128]{1,0:T(8,128)(2,1)S(1)}, bf16[640,128]{1,0:T(8,128)(2,1)S(1)}, u32[]{:S(2)}, u32[]{:S(2)}) collective-permute-start(bf16[640,128]{1,0:T(8,128)(2,1)S(1)} %shard_map.123.refs_0_), channel_id=1, source_target_pairs={{0,2},{1,3},{2,0},{3,1},{4,6},{5,7},{6,4},{7,5},{8,10},{9,11},{10,... | collective-permute-start | bytes 491528 | tf_op jit(solution)/shard_map/ppermute | solution.py:469
  34.8 17.3 %collective-permute-start.3 = (bf16[2,1552,128]{2,1,0:T(8,128)(2,1)S(1)}, bf16[2,1552,128]{2,1,0:T(8,128)(2,1)S(1)}, u32[]{:S(2)}, u32[]{:S(2)}) collective-permute-start(bf16[2,1552,128]{2,1,0:T(8,128)(2,1)S(1)} %collective-permute-done.1.full_ref), channel_id=1, source_target_pairs={{0,1},{1,0},{2,3},{3,2},{4,5},{5,4},{6,7},{7,6},{8,9},{9,8},{10,11... | collective-permute-start | bytes 2383880 | tf_op jit(solution)/shard_map/ppermute | solution.py:469
  38.8 27.8 %collective-permute-start.2 = (bf16[2,1552,128]{2,1,0:T(8,128)(2,1)S(1)}, bf16[2,1552,128]{2,1,0:T(8,128)(2,1)S(1)}, u32[]{:S(2)}, u32[]{:S(2)}) collective-permute-start(bf16[2,1552,128]{2,1,0:T(8,128)(2,1)S(1)} %collective-permute-done.1.full_ref), channel_id=1, source_target_pairs={{0,2},{2,4},{3,1},{4,6},{5,3},{7,5},{8,10},{10,12},{11,9},{12,14},... | collective-permute-start | bytes 2383880 | tf_op jit(solution)/shard_map/ppermute | solution.py:469
  52.0 13.5 %copy-start.2 = (bf16[1,256,256]{2,1,0:T(8,128)(2,1)S(1)}, bf16[1,256,256]{2,1,0:T(8,128)(2,1)}, u32[]{:S(2)}) copy-start(bf16[1,256,256]{2,1,0:T(8,128)(2,1)} %transfer_ref.1) | copy-start | bytes 393220
  52.0 13.5 %copy-start.4 = (bf16[1,256,64]{1,2,0:T(8,128)(2,1)S(1)}, bf16[1,256,64]{1,2,0:T(8,128)(2,1)}, u32[]{:S(2)}) copy-start(bf16[1,256,64]{1,2,0:T(8,128)(2,1)} %param.19) | copy-start | bytes 98308
  52.0 13.5 %copy-start.9 = (s32[1,8]{1,0:T(1,128)S(1)}, s32[1,8]{1,0:T(1,128)}, u32[]{:S(2)}) copy-start(s32[1,8]{1,0:T(1,128)} %far_ref.3) | copy-start | bytes 100
  62.8 3.8 %copy-start = (f32[2048,128]{1,0:T(8,128)S(1)}, f32[2048,128]{1,0:T(8,128)}, u32[]{:S(2)}) copy-start(f32[2048,128]{1,0:T(8,128)} %iterate_ref.1) | copy-start | bytes 3145732
  62.8 3.8 %copy-start.1 = (bf16[2048,256]{1,0:T(8,128)(2,1)S(1)}, bf16[2048,256]{1,0:T(8,128)(2,1)}, u32[]{:S(2)}) copy-start(bf16[2048,256]{1,0:T(8,128)(2,1)} %basis_ref.1) | copy-start | bytes 3145732
  62.8 3.8 %copy-start.10 = (f32[128]{0:T(128)S(1)}, f32[128]{0:T(128)}, u32[]{:S(2)}) copy-start(f32[128]{0:T(128)} %param.16) | copy-start | bytes 1540
  62.8 3.8 %collective-permute-start.6 = (bf16[2048,128]{1,0:T(8,128)(2,1)S(1)}, bf16[2048,128]{1,0:T(8,128)(2,1)S(1)}, u32[]{:S(2)}, u32[]{:S(2)}) collective-permute-start(bf16[2048,128]{1,0:T(8,128)(2,1)S(1)} %get-tuple-element.21), channel_id=1, source_target_pairs={{0,1},{1,0},{2,3},{3,2},{4,5},{5,4},{6,7},{7,6},{8,9},{9,8},{10,11... | collective-permute-start | bytes 1572872 | tf_op jit(solution)/shard_map/ppermute | solution.py:469
  63.0 2.5 %collective-permute-start.13 = (bf16[1792,128]{1,0:T(8,128)(2,1)S(1)}, bf16[1792,128]{1,0:T(8,128)(2,1)S(1)}, u32[]{:S(2)}, u32[]{:S(2)}) collective-permute-start(bf16[1792,128]{1,0:T(8,128)(2,1)S(1)} %shard_map.124.mine_ref), channel_id=1, source_target_pairs={{0,1},{1,0},{2,3},{3,2},{4,5},{5,4},{6,7},{7,6},{8,9},{9,8},{10,11... | collective-permute-start | bytes 1376264 | tf_op jit(solution)/shard_map/ppermute | solution.py:469

commit v3 on v2

--- a/solution.py
+++ b/solution.py
@@ -225,32 +225,41 @@
     )
 
 
-def own_tile(plan, pay, ordering, target):
+def own_tile(plan, pay, ordering, target, iterate, step_size):
     group = 8
     steps = (plan.n // ROWS) * (plan.half // COLS)
-
-    def kernel(pay_ref, order_ref, target_ref, acc_ref, wanted_ref, left_ref, offset_ref):
+    rows = plan.half // steps
+
+    def kernel(pay_ref, order_ref, target_ref, iterate_ref, step_ref, acc_ref, base_ref, factor_ref, left_ref, offset_ref):
         acc_ref[...] = jnp.zeros_like(acc_ref)
         for h in range(2):
             fill_left(plan, left_ref, pay_ref.at[h], h)
+        step_row = step_ref[...]
 
         @pl.loop(0, 2)
         def _(h):
-            def gather(step):
-                rows = plan.half // steps
+            def beside(step):
                 for k in range(step * rows, (step + 1) * rows, group):
                     first = pl.multiple_of(h * plan.half + k, group)
-                    wanted_ref[pl.ds(first, group), :] = jnp.concatenate(
+                    here = pl.ds(first, group)
+                    wanted = jnp.concatenate(
                         [target_ref[pl.ds(order_ref[0, first + u], 1), :] for u in range(group)], axis=0
                     )
+                    base_ref[here, :] = iterate_ref[here, :] + step_row * wanted
+                if (step * rows) % LANES == 0:
+                    b = step * rows // LANES
+                    here = pl.ds(pl.multiple_of(h * plan.half + b * LANES, LANES), LANES)
+                    power = SHIFT + offset_ref[0:1, b * LANES : (b + 1) * LANES] + SHIFT
+                    factor_ref[here, :] = step_row * jnp.exp2(jnp.broadcast_to(power, (LANES, LANES)).T)
 
             fill_offset(plan, offset_ref, pay_ref.at[h])
-            half_tile(plan, acc_ref.at[0], left_ref, pay_ref.at[h], offset_ref, gather)
-
-    return call(
-        kernel,
-        [plan.acc(), shaped(plan.n, plan.rhs, dtype=F32)],
-        [(pay, VMEM), (ordering, SMEM), (target, VMEM)],
+            half_tile(plan, acc_ref.at[0], left_ref, pay_ref.at[h], offset_ref, beside)
+
+    full = shaped(plan.n, plan.rhs, dtype=F32)
+    return call(
+        kernel,
+        [plan.acc(), full, full],
+        [(pay, VMEM), (ordering, SMEM), (target, VMEM), (iterate, VMEM), (step_size, VMEM)],
         scratch=[VMEM(plan.left().shape[1:], BF16)] + plan.offset_scratch(),
         flops=plan.tile_flops,
     )
@@ -323,58 +332,50 @@
     )
 
 
-def last_tile(plan, near_row, pay, left, third, acc, returned, iterate, wanted, step_size, basis, local):
-    def kernel(near_ref, pay_ref, left_ref, third_ref, acc_ref, returned_ref, iterate_ref, wanted_ref, step_ref, basis_ref, local_ref, out_hbm, out_ref, offset_ref, sems):
+def third_tile(plan, near_row, left, third, acc):
+    def kernel(near_ref, left_ref, third_ref, acc_in, acc_ref, offset_ref):
         place = lax.axis_index("leaf")
         away = 2 * lax.rem(place, 2) - 1
-        out_ref[...] = acc_ref[0] + returned_ref[...].astype(F32)
 
         @pl.when(listed(near_ref, place + 3 * away))
         def _():
             @pl.loop(0, 2)
             def _(h):
                 fill_offset(plan, offset_ref, third_ref.at[h])
-                half_tile(plan, out_ref, left_ref.at[0], third_ref.at[h], offset_ref)
-
+                half_tile(plan, acc_ref.at[0], left_ref.at[0], third_ref.at[h], offset_ref)
+
+    return call(
+        kernel,
+        plan.acc(),
+        [(near_row, SMEM), (left, VMEM), (third, VMEM), (acc, VMEM)],
+        scratch=plan.offset_scratch(),
+        flops=plan.tile_flops,
+        aliases={3: 0},
+    )
+
+
+def finish(plan, acc, returned, base, factor, step_size, basis, local):
+    piece = 4 * LANES
+
+    def kernel(acc_ref, returned_ref, base_ref, factor_ref, step_ref, basis_ref, local_ref, out_hbm, out_ref, sems):
         copies = []
-        for h in range(2):
-            for b in range(plan.blocks):
-                first = h * plan.half + b * LANES
-                rows = slice(first, first + LANES)
-                power = SHIFT - norms(doubled_block(plan, pay_ref.at[h], b))
-                factor = jnp.exp2(jnp.broadcast_to(power, (LANES, LANES)).T)
-                image = matmul(basis_ref[rows, :], local_ref[...]) + factor * out_ref[rows, :]
-                out_ref[rows, :] = iterate_ref[rows, :] + step_ref[...] * (wanted_ref[rows, :] - image)
-                if b % 4 == 3:
-                    done = slice(first - 3 * LANES, first + LANES)
-                    copies.append(
-                        pltpu.make_async_copy(out_ref.at[done, :], out_hbm.at[done, :], sems.at[len(copies)])
-                    )
-                    copies[-1].start()
+        for first in range(0, plan.n, piece):
+            rows = slice(first, first + piece)
+            far = step_ref[...] * matmul(basis_ref[rows, :], local_ref[...])
+            near = factor_ref[rows, :] * (acc_ref[0, rows, :] + returned_ref[rows, :].astype(F32))
+            out_ref[rows, :] = base_ref[rows, :] - (far + near)
+            copies.append(pltpu.make_async_copy(out_ref.at[rows, :], out_hbm.at[rows, :], sems.at[len(copies)]))
+            copies[-1].start()
         for copy in copies:
             copy.wait()
 
     return call(
         kernel,
         shaped(plan.n, plan.rhs, dtype=F32),
-        [
-            (near_row, SMEM),
-            (pay, VMEM),
-            (left, VMEM),
-            (third, VMEM),
-            (acc, VMEM),
-            (returned, VMEM),
-            (iterate, VMEM),
-            (wanted, VMEM),
-            (step_size.reshape(1, -1), VMEM),
-            (basis, VMEM),
-            (local, VMEM),
-        ],
-        scratch=[VMEM((plan.n, plan.rhs), F32)]
-        + plan.offset_scratch()
-        + [pltpu.SemaphoreType.DMA((plan.n // (4 * LANES),))],
+        [(value, VMEM) for value in (acc, returned, base, factor, step_size, basis, local)],
+        scratch=[VMEM((plan.n, plan.rhs), F32), pltpu.SemaphoreType.DMA((plan.n // piece,))],
         into=HBM,
-        flops=plan.tile_flops,
+        flops=2 * plan.n * basis.shape[1] * plan.rhs,
     )
 
 
@@ -508,7 +509,8 @@
     partner = routed(pay, "leaf", on_chip)
     over = routed(pay, "leaf", over_chips)
     others = [routed(up_block, "group", lambda i, k=k: i ^ k) for k in range(1, groups)]
-    acc, wanted = own_tile(plan, pay, ordering, target)
+    step_row = step_size.reshape(1, -1)
+    acc, base, factor = own_tile(plan, pay, ordering, target, iterate, step_row)
     mine = across(cluster_far, cluster_t, up_block, others, lambda me, k: me ^ (k + 1), down_block)
     acc, left, row = pair_tiles(plan, near_table, pay, partner, acc)
 
@@ -527,9 +529,8 @@
     third = routed(beside, "leaf", over_chips)
     acc, theirs = side_tiles(plan, near_table, row, left, beside, beside_passed, acc, 1, True)
     returned = routed(theirs, "leaf", on_chip)
-    return last_tile(
-        plan, near_table, pay, left, third, acc, returned, iterate, wanted, step_size, leaf_basis, local
-    )
+    acc = third_tile(plan, near_table, left, third, acc)
+    return finish(plan, acc, returned, base, factor, step_row, leaf_basis, local)
 
 
 def solution(mesh):

time: 74.1 us -> 80.4 us (1.085)
  waiting for transfers between devices: 10.6 us -> 22 us
  starting transfers between devices: 22.1 us -> 15.6 us
  Pallas kernels: 40.6 us -> 42.1 us
    ppermute x14, waiting for transfers between devices: 10.6 us -> 22 us  [routed(): return lax.ppermute(block, axis, route)]
    ppermute x14, starting transfers between devices: 22.1 us -> 15.6 us  [routed(): return lax.ppermute(block, axis, route)]
    pallas_call x9 -> x10, Pallas kernels: 40.6 us -> 42.1 us  [call(): pl.pallas_call(kernel, out_shape=shapes, in_specs=[pl.BlockSpec(memory_sp...]
  transfers between devices with their start and end apart: 14 -> 14, of which waited for: 3 -> 3; matrix products, arithmetic and copies ran while one was open for 0% -> 0% of each run, Pallas kernels for 42% -> 48%
where the time goes in v3:
time: 80.4 us; the launch traced here: 80.2 us
  Pallas kernels  42.1 us (52%)
  waiting for transfers between devices  22 us (27%)
  starting transfers between devices  15.6 us (19%)
    pallas_call x10, Pallas kernels, call(): pl.pallas_call(kernel, out_shape=shapes, in_specs=[pl.BlockSpec(memory_sp...  42.1 us
    ppermute x14, waiting for transfers between devices, routed(): return lax.ppermute(block, axis, route)  22 us
    ppermute x14, starting transfers between devices, routed(): return lax.ppermute(block, axis, route)  15.6 us
  transfers between devices with their start and end apart: 14, of which 3 were waited for; matrix products, arithmetic and copies ran while one was open for 0% of the time, Pallas kernels for 48%

profile of v3, /device:TPU:15, one launch (start us, length us, event | category | flops | bytes accessed | tf_op | source)
XLA Modules:
  0.0 80.2 jit_solution(4751567815844153681)
XLA Ops:
  0.0 2.5 %shard_map.118 = (bf16[2,1552,128]{2,1,0:T(8,128)(2,1)S(1)}, bf16[384,128]{1,0:T(8,128)(2,1)S(1)}, bf16[384,128]{1,0:T(8,128)(2,1)S(1)}) custom-call(bf16[64,2048]{1,0:T(8,128)(2,1)} %bitcast.10, f32[2048,128]{1,0:T(8,128)} %iterate_ref.1, s32[1,8]{1,0:T(1,128)} %near_ref.7, bf16[1,64,256]{2,1,0:T(8,128)(2,1)} %bitcast.6, bf16[1,64,256]{2,1,0:T(8,128)(2,1)} %bitcast.4, ...), custom_call_target="tpu_custom_call" | custom-call | flops 134217728 | bytes 2555936 | tf_op jit(solution)/shard_map/pallas_call | solution.py:35
  2.6 2.1 %collective-permute-start.4 = (bf16[2,1552,128]{2,1,0:T(8,128)(2,1)S(1)}, bf16[2,1552,128]{2,1,0:T(8,128)(2,1)S(1)}, u32[]{:S(2)}, u32[]{:S(2)}) collective-permute-start(bf16[2,1552,128]{2,1,0:T(8,128)(2,1)S(1)} %get-tuple-element.16.pay_ref), channel_id=1, source_target_pairs={{0,2},{2,4},{3,1},{4,6},{5,3},{7,5},{8,10},{10,12},{11,9},{12,14},... | collective-permute-start | bytes 2383880 | tf_op jit(solution)/shard_map/ppermute | solution.py:470
  4.7 5.2 %collective-permute-start.1 = (bf16[2,1552,128]{2,1,0:T(8,128)(2,1)S(1)}, bf16[2,1552,128]{2,1,0:T(8,128)(2,1)S(1)}, u32[]{:S(2)}, u32[]{:S(2)}) collective-permute-start(bf16[2,1552,128]{2,1,0:T(8,128)(2,1)S(1)} %get-tuple-element.16.pay_ref), channel_id=1, source_target_pairs={{1,2},{2,1},{3,4},{4,3},{5,6},{6,5},{9,10},{10,9},{11,12},{12,11},... | collective-permute-start | bytes 2383880 | tf_op jit(solution)/shard_map/ppermute | solution.py:470
  9.9 0.1 collective-permute-start
  9.9 0.3 collective-permute-start.7
  10.2 0.2 collective-permute-start.8
  10.5 3.4 %collective-permute-done.7.refs_0_ = bf16[384,128]{1,0:T(8,128)(2,1)S(1)} collective-permute-done((bf16[384,128]{1,0:T(8,128)(2,1)S(1)}, bf16[384,128]{1,0:T(8,128)(2,1)S(1)}, u32[]{:S(2)}, u32[]{:S(2)}) %collective-permute-start.7) | collective-permute-done | bytes 98336 | tf_op jit(solution)/shard_map/ppermute | solution.py:470
  13.9 0.2 collective-permute-start.9
  14.1 0.0 collective-permute-done.8.refs_1_
  14.1 4.2 %collective-permute-done.9.refs_2_ = bf16[384,128]{1,0:T(8,128)(2,1)S(1)} collective-permute-done((bf16[384,128]{1,0:T(8,128)(2,1)S(1)}, bf16[384,128]{1,0:T(8,128)(2,1)S(1)}, u32[]{:S(2)}, u32[]{:S(2)}) %collective-permute-start.9) | collective-permute-done | bytes 98336 | tf_op jit(solution)/shard_map/ppermute | solution.py:470
  18.3 1.3 %shard_map.124.refs_0_ = bf16[640,128]{1,0:T(8,128)(2,1)S(1)} custom-call(s32[1,4]{1,0:T(1,128)S(1)} %copy-done.9, bf16[1,64,256]{2,1,0:T(8,128)(2,1)S(1)} %bitcast.5, bf16[384,128]{1,0:T(8,128)(2,1)S(1)} %get-tuple-element.25.down_ref, bf16[384,128]{1,0:T(8,128)(2,1)S(1)} %get-tuple-element.26.own_ref, bf16[384,128]{1,0:T(8,128)(2,1)S(1)} %collective-permute-done.7.refs_0_, ...), custom_call_target="tpu_custom_call" | custom-call | flops 268435456 | bytes 524304 | tf_op jit(solution)/shard_map/pallas_call | solution.py:35
  19.6 0.5 collective-permute-start.10
  20.1 1.9 %collective-permute-start.11 = (bf16[640,128]{1,0:T(8,128)(2,1)S(1)}, bf16[640,128]{1,0:T(8,128)(2,1)S(1)}, u32[]{:S(2)}, u32[]{:S(2)}) collective-permute-start(bf16[640,128]{1,0:T(8,128)(2,1)S(1)} %shard_map.124.refs_0_), channel_id=1, source_target_pairs={{0,4},{1,5},{2,6},{3,7},{4,0},{5,1},{6,2},{7,3},{8,12},{9,13},{10,... | collective-permute-start | bytes 491528 | tf_op jit(solution)/shard_map/ppermute | solution.py:470
  22.0 14.3 %collective-permute-done.10.refs_1_ = bf16[640,128]{1,0:T(8,128)(2,1)S(1)} collective-permute-done((bf16[640,128]{1,0:T(8,128)(2,1)S(1)}, bf16[640,128]{1,0:T(8,128)(2,1)S(1)}, u32[]{:S(2)}, u32[]{:S(2)}) %collective-permute-start.10) | collective-permute-done | bytes 163872 | tf_op jit(solution)/shard_map/ppermute | solution.py:470
  36.3 0.6 collective-permute-start.5
  36.9 0.0 copy-start.6
  36.9 7.4 %shard_map.119 = (f32[2,2048,128]{2,1,0:T(8,128)S(1)}, f32[2048,128]{1,0:T(8,128)S(1)}, f32[2048,128]{1,0:T(8,128)S(1)}) custom-call(bf16[2,1552,128]{2,1,0:T(8,128)(2,1)S(1)} %get-tuple-element.16.pay_ref, s32[1,2048]{1,0:T(1,128)S(1)} %copy-done.8, f32[2048,128]{1,0:T(8,128)S(1)} %copy-done.7, f32[2048,128]{1,0:T(8,128)S(1)} %copy-done.1, f32[1,128]{1,0:T(1,128)S(1)} %bitcast.8), custom_call_target="tpu_custom_call" | custom-call | flops 4294967296 | bytes 2900480 | tf_op jit(solution)/shard_map/pallas_call | solution.py:35
  44.3 0.1 shard_map.125.mine_ref
  44.4 0.1 collective-permute-start.13
  44.5 0.5 collective-permute-start.3
  45.0 3.6 %collective-permute-start.2 = (bf16[2,1552,128]{2,1,0:T(8,128)(2,1)S(1)}, bf16[2,1552,128]{2,1,0:T(8,128)(2,1)S(1)}, u32[]{:S(2)}, u32[]{:S(2)}) collective-permute-start(bf16[2,1552,128]{2,1,0:T(8,128)(2,1)S(1)} %collective-permute-done.1.full_ref), channel_id=1, source_target_pairs={{0,2},{2,4},{3,1},{4,6},{5,3},{7,5},{8,10},{10,12},{11,9},{12,14},... | collective-permute-start | bytes 2383880 | tf_op jit(solution)/shard_map/ppermute | solution.py:470
  48.6 3.5 %shard_map.120 = (f32[2,2048,128]{2,1,0:T(8,128)S(1)}, bf16[2,2048,64]{2,1,0:T(8,128)(2,1)S(1)}, f32[16,128]{1,0:T(8,128)S(1)}) custom-call(s32[1,8]{1,0:T(1,128)S(1)} %copy-done.6, bf16[2,1552,128]{2,1,0:T(8,128)(2,1)S(1)} %get-tuple-element.16.pay_ref, bf16[2,1552,128]{2,1,0:T(8,128)(2,1)S(1)} %collective-permute-done.partner_ref, ...), custom_call_target="tpu_custom_call", output_to_operand_aliasing={{0}: (3, {})} | custom-call | flops 4294967296 | bytes 3686432 | tf_op jit(solution)/shard_map/pallas_call | solution.py:35
  52.1 8.5 %shard_map.121.acc_in = f32[2,2048,128]{2,1,0:T(8,128)S(1)} custom-call(s32[1,8]{1,0:T(1,128)S(1)} %copy-done.6, f32[16,128]{1,0:T(8,128)S(1)} %get-tuple-element.19.row_in, bf16[2,2048,64]{2,1,0:T(8,128)(2,1)S(1)} %get-tuple-element.18.left_ref, bf16[2,1552,128]{2,1,0:T(8,128)(2,1)S(1)} %collective-permute-done.4.full_ref, ...), custom_call_target="tpu_custom_call", output_to_operand_aliasing={{}: (5, {})} | custom-call | flops 8589934592 | bytes 4218912 | tf_op jit(solution)/shard_map/pallas_call | solution.py:35
  60.6 0.0 copy-start.2
  60.6 0.0 copy-start.4
  60.6 0.0 copy-start.10
  60.6 10.8 %shard_map.122 = (f32[2,2048,128]{2,1,0:T(8,128)S(1)}, bf16[2048,128]{1,0:T(8,128)(2,1)S(1)}) custom-call(s32[1,8]{1,0:T(1,128)S(1)} %copy-done.6, f32[16,128]{1,0:T(8,128)S(1)} %get-tuple-element.19.row_in, bf16[2,2048,64]{2,1,0:T(8,128)(2,1)S(1)} %get-tuple-element.18.left_ref, ...), custom_call_target="tpu_custom_call", output_to_operand_aliasing={{0}: (5, {})} | custom-call | flops 8589934592 | bytes 4218912 | tf_op jit(solution)/shard_map/pallas_call | solution.py:35
  71.4 0.4 collective-permute-start.6
  71.8 1.1 %shard_map.126.local_ref = bf16[256,128]{1,0:T(8,128)(2,1)S(1)} custom-call(s32[1,8]{1,0:T(1,128)S(1)} %copy-done.10, bf16[1,64,256]{2,1,0:T(8,128)(2,1)S(1)} %bitcast.7, bf16[1,256,256]{2,1,0:T(8,128)(2,1)S(1)} %copy-done.2, bf16[1792,128]{1,0:T(8,128)(2,1)S(1)} %shard_map.125.mine_ref, bf16[1792,128]{1,0:T(8,128)(2,1)S(1)} %collective-permute-done.13.got_ref), custom_call_target="tpu_custom_call" | custom-call | flops 536870912 | bytes 1081376 | tf_op jit(solution)/shard_map/pallas_call | solution.py:35
  73.0 0.0 copy-start
  73.0 5.7 %shard_map.123.acc_ref = f32[2,2048,128]{2,1,0:T(8,128)S(1)} custom-call(s32[1,8]{1,0:T(1,128)S(1)} %copy-done.6, bf16[2,2048,64]{2,1,0:T(8,128)(2,1)S(1)} %get-tuple-element.18.left_ref, bf16[2,1552,128]{2,1,0:T(8,128)(2,1)S(1)} %collective-permute-done.2.third_ref, f32[2,2048,128]{2,1,0:T(8,128)S(1)} %get-tuple-element.21.acc_in), custom_call_target="tpu_custom_call", output_to_operand_aliasing={{}: (3, {})} | custom-call | flops 4294967296 | bytes 3416096 | tf_op jit(solution)/shard_map/pallas_call | solution.py:35
  78.7 1.3 %shard_map.127 = f32[2048,128]{1,0:T(8,128)} custom-call(f32[2,2048,128]{2,1,0:T(8,128)S(1)} %shard_map.123.acc_ref, bf16[2048,128]{1,0:T(8,128)(2,1)S(1)} %collective-permute-done.6.returned_ref, f32[2048,128]{1,0:T(8,128)S(1)} %get-tuple-element.23.base_ref, f32[2048,128]{1,0:T(8,128)S(1)} %get-tuple-element.24.factor_ref, f32[1,128]{1,0:T(1,128)S(1)} %bitcast.9, ...), custom_call_target="tpu_custom_call" | custom-call | flops 134217728 | bytes 5833216 | tf_op jit(solution)/shard_map/pallas_call | solution.py:35
  (28 shorter events, 0.1 us)
Async XLA Ops:
  0.0 18.3 %copy-start.3 = (bf16[1,256,64]{1,2,0:T(8,128)(2,1)S(1)}, bf16[1,256,64]{1,2,0:T(8,128)(2,1)}, u32[]{:S(2)}) copy-start(bf16[1,256,64]{1,2,0:T(8,128)(2,1)} %param.20) | copy-start | bytes 98308
  0.0 36.9 %copy-start.1 = (f32[2048,128]{1,0:T(8,128)S(1)}, f32[2048,128]{1,0:T(8,128)}, u32[]{:S(2)}) copy-start(f32[2048,128]{1,0:T(8,128)} %iterate_ref.1) | copy-start | bytes 3145732
  0.0 18.3 %copy-start.9 = (s32[1,4]{1,0:T(1,128)S(1)}, s32[1,4]{1,0:T(1,128)}, u32[]{:S(2)}) copy-start(s32[1,4]{1,0:T(1,128)} %far_ref.2) | copy-start | bytes 52
  0.0 36.9 %copy-start.5 = (f32[128]{0:T(128)S(1)}, f32[128]{0:T(128)}, u32[]{:S(2)}) copy-start(f32[128]{0:T(128)} %param.16) | copy-start | bytes 1540
  0.0 36.9 %copy-start.8 = (s32[1,2048]{1,0:T(1,128)S(1)}, s32[1,2048]{1,0:T(1,128)}, u32[]{:S(2)}) copy-start(s32[1,2048]{1,0:T(1,128)} %order_ref.1) | copy-start | bytes 24580
  0.0 36.9 %copy-start.7 = (f32[2048,128]{1,0:T(8,128)S(1)}, f32[2048,128]{1,0:T(8,128)}, u32[]{:S(2)}) copy-start(f32[2048,128]{1,0:T(8,128)} %target_ref.1) | copy-start | bytes 3145732
  2.6 33.7 %collective-permute-start.4 = (bf16[2,1552,128]{2,1,0:T(8,128)(2,1)S(1)}, bf16[2,1552,128]{2,1,0:T(8,128)(2,1)S(1)}, u32[]{:S(2)}, u32[]{:S(2)}) collective-permute-start(bf16[2,1552,128]{2,1,0:T(8,128)(2,1)S(1)} %get-tuple-element.16.pay_ref), channel_id=1, source_target_pairs={{0,2},{2,4},{3,1},{4,6},{5,3},{7,5},{8,10},{10,12},{11,9},{12,14},... | collective-permute-start | bytes 2383880 | tf_op jit(solution)/shard_map/ppermute | solution.py:470
  4.7 39.8 %collective-permute-start.1 = (bf16[2,1552,128]{2,1,0:T(8,128)(2,1)S(1)}, bf16[2,1552,128]{2,1,0:T(8,128)(2,1)S(1)}, u32[]{:S(2)}, u32[]{:S(2)}) collective-permute-start(bf16[2,1552,128]{2,1,0:T(8,128)(2,1)S(1)} %get-tuple-element.16.pay_ref), channel_id=1, source_target_pairs={{1,2},{2,1},{3,4},{4,3},{5,6},{6,5},{9,10},{10,9},{11,12},{12,11},... | collective-permute-start | bytes 2383880 | tf_op jit(solution)/shard_map/ppermute | solution.py:470
  9.9 38.8 %collective-permute-start = (bf16[2,1552,128]{2,1,0:T(8,128)(2,1)S(1)}, bf16[2,1552,128]{2,1,0:T(8,128)(2,1)S(1)}, u32[]{:S(2)}, u32[]{:S(2)}) collective-permute-start(bf16[2,1552,128]{2,1,0:T(8,128)(2,1)S(1)} %get-tuple-element.16.pay_ref), channel_id=1, source_target_pairs={{0,1},{1,0},{2,3},{3,2},{4,5},{5,4},{6,7},{7,6},{8,9},{9,8},{10,11... | collective-permute-start | bytes 2383880 | tf_op jit(solution)/shard_map/ppermute | solution.py:470
  9.9 4.0 %collective-permute-start.7 = (bf16[384,128]{1,0:T(8,128)(2,1)S(1)}, bf16[384,128]{1,0:T(8,128)(2,1)S(1)}, u32[]{:S(2)}, u32[]{:S(2)}) collective-permute-start(bf16[384,128]{1,0:T(8,128)(2,1)S(1)} %get-tuple-element.26.own_ref), channel_id=1, source_target_pairs={{0,8},{8,0},{16,24},{24,16},{1,9},{9,1},{17,25},{25,17},{2,10},{10... | collective-permute-start | bytes 294920 | tf_op jit(solution)/shard_map/ppermute | solution.py:470
  10.2 3.9 %collective-permute-start.8 = (bf16[384,128]{1,0:T(8,128)(2,1)S(1)}, bf16[384,128]{1,0:T(8,128)(2,1)S(1)}, u32[]{:S(2)}, u32[]{:S(2)}) collective-permute-start(bf16[384,128]{1,0:T(8,128)(2,1)S(1)} %get-tuple-element.26.own_ref), channel_id=1, source_target_pairs={{0,16},{8,24},{16,0},{24,8},{1,17},{9,25},{17,1},{25,9},{2,18},{10... | collective-permute-start | bytes 294920 | tf_op jit(solution)/shard_map/ppermute | solution.py:470
  13.9 4.4 %collective-permute-start.9 = (bf16[384,128]{1,0:T(8,128)(2,1)S(1)}, bf16[384,128]{1,0:T(8,128)(2,1)S(1)}, u32[]{:S(2)}, u32[]{:S(2)}) collective-permute-start(bf16[384,128]{1,0:T(8,128)(2,1)S(1)} %get-tuple-element.26.own_ref), channel_id=1, source_target_pairs={{0,24},{8,16},{16,8},{24,0},{1,25},{9,17},{17,9},{25,1},{2,26},{10... | collective-permute-start | bytes 294920 | tf_op jit(solution)/shard_map/ppermute | solution.py:470
  19.6 16.6 %collective-permute-start.10 = (bf16[640,128]{1,0:T(8,128)(2,1)S(1)}, bf16[640,128]{1,0:T(8,128)(2,1)S(1)}, u32[]{:S(2)}, u32[]{:S(2)}) collective-permute-start(bf16[640,128]{1,0:T(8,128)(2,1)S(1)} %shard_map.124.refs_0_), channel_id=1, source_target_pairs={{0,6},{1,7},{2,4},{3,5},{4,2},{5,3},{6,0},{7,1},{8,14},{9,15},{10,... | collective-permute-start | bytes 491528 | tf_op jit(solution)/shard_map/ppermute | solution.py:470
  20.1 24.2 %collective-permute-start.11 = (bf16[640,128]{1,0:T(8,128)(2,1)S(1)}, bf16[640,128]{1,0:T(8,128)(2,1)S(1)}, u32[]{:S(2)}, u32[]{:S(2)}) collective-permute-start(bf16[640,128]{1,0:T(8,128)(2,1)S(1)} %shard_map.124.refs_0_), channel_id=1, source_target_pairs={{0,4},{1,5},{2,6},{3,7},{4,0},{5,1},{6,2},{7,3},{8,12},{9,13},{10,... | collective-permute-start | bytes 491528 | tf_op jit(solution)/shard_map/ppermute | solution.py:470
  36.3 8.1 %collective-permute-start.12 = (bf16[640,128]{1,0:T(8,128)(2,1)S(1)}, bf16[640,128]{1,0:T(8,128)(2,1)S(1)}, u32[]{:S(2)}, u32[]{:S(2)}) collective-permute-start(bf16[640,128]{1,0:T(8,128)(2,1)S(1)} %shard_map.124.refs_0_), channel_id=1, source_target_pairs={{0,2},{1,3},{2,0},{3,1},{4,6},{5,7},{6,4},{7,5},{8,10},{9,11},{10,... | collective-permute-start | bytes 491528 | tf_op jit(solution)/shard_map/ppermute | solution.py:470
  36.3 15.8 %collective-permute-start.5 = (bf16[2,1552,128]{2,1,0:T(8,128)(2,1)S(1)}, bf16[2,1552,128]{2,1,0:T(8,128)(2,1)S(1)}, u32[]{:S(2)}, u32[]{:S(2)}) collective-permute-start(bf16[2,1552,128]{2,1,0:T(8,128)(2,1)S(1)} %collective-permute-done.4.full_ref), channel_id=1, source_target_pairs={{0,1},{1,0},{2,3},{3,2},{4,5},{5,4},{6,7},{7,6},{8,9},{9,8},{10,11... | collective-permute-start | bytes 2383880 | tf_op jit(solution)/shard_map/ppermute | solution.py:470
  36.9 11.7 %copy-start.6 = (s32[1,8]{1,0:T(1,128)S(1)}, s32[1,8]{1,0:T(1,128)}, u32[]{:S(2)}) copy-start(s32[1,8]{1,0:T(1,128)} %near_ref.7) | copy-start | bytes 100
  44.4 27.4 %collective-permute-start.13 = (bf16[1792,128]{1,0:T(8,128)(2,1)S(1)}, bf16[1792,128]{1,0:T(8,128)(2,1)S(1)}, u32[]{:S(2)}, u32[]{:S(2)}) collective-permute-start(bf16[1792,128]{1,0:T(8,128)(2,1)S(1)} %shard_map.125.mine_ref), channel_id=1, source_target_pairs={{0,1},{1,0},{2,3},{3,2},{4,5},{5,4},{6,7},{7,6},{8,9},{9,8},{10,11... | collective-permute-start | bytes 1376264 | tf_op jit(solution)/shard_map/ppermute | solution.py:470
  44.5 16.1 %collective-permute-start.3 = (bf16[2,1552,128]{2,1,0:T(8,128)(2,1)S(1)}, bf16[2,1552,128]{2,1,0:T(8,128)(2,1)S(1)}, u32[]{:S(2)}, u32[]{:S(2)}) collective-permute-start(bf16[2,1552,128]{2,1,0:T(8,128)(2,1)S(1)} %collective-permute-done.1.full_ref), channel_id=1, source_target_pairs={{0,1},{1,0},{2,3},{3,2},{4,5},{5,4},{6,7},{7,6},{8,9},{9,8},{10,11... | collective-permute-start | bytes 2383880 | tf_op jit(solution)/shard_map/ppermute | solution.py:470
  45.0 28.0 %collective-permute-start.2 = (bf16[2,1552,128]{2,1,0:T(8,128)(2,1)S(1)}, bf16[2,1552,128]{2,1,0:T(8,128)(2,1)S(1)}, u32[]{:S(2)}, u32[]{:S(2)}) collective-permute-start(bf16[2,1552,128]{2,1,0:T(8,128)(2,1)S(1)} %collective-permute-done.1.full_ref), channel_id=1, source_target_pairs={{0,2},{2,4},{3,1},{4,6},{5,3},{7,5},{8,10},{10,12},{11,9},{12,14},... | collective-permute-start | bytes 2383880 | tf_op jit(solution)/shard_map/ppermute | solution.py:470
  60.6 11.2 %copy-start.2 = (bf16[1,256,256]{2,1,0:T(8,128)(2,1)S(1)}, bf16[1,256,256]{2,1,0:T(8,128)(2,1)}, u32[]{:S(2)}) copy-start(bf16[1,256,256]{2,1,0:T(8,128)(2,1)} %transfer_ref.1) | copy-start | bytes 393220
  60.6 11.2 %copy-start.4 = (bf16[1,256,64]{1,2,0:T(8,128)(2,1)S(1)}, bf16[1,256,64]{1,2,0:T(8,128)(2,1)}, u32[]{:S(2)}) copy-start(bf16[1,256,64]{1,2,0:T(8,128)(2,1)} %param.19) | copy-start | bytes 98308
  60.6 11.2 %copy-start.10 = (s32[1,8]{1,0:T(1,128)S(1)}, s32[1,8]{1,0:T(1,128)}, u32[]{:S(2)}) copy-start(s32[1,8]{1,0:T(1,128)} %far_ref.3) | copy-start | bytes 100
  71.4 7.3 %collective-permute-start.6 = (bf16[2048,128]{1,0:T(8,128)(2,1)S(1)}, bf16[2048,128]{1,0:T(8,128)(2,1)S(1)}, u32[]{:S(2)}, u32[]{:S(2)}) collective-permute-start(bf16[2048,128]{1,0:T(8,128)(2,1)S(1)} %get-tuple-element.22), channel_id=1, source_target_pairs={{0,1},{1,0},{2,3},{3,2},{4,5},{5,4},{6,7},{7,6},{8,9},{9,8},{10,11... | collective-permute-start | bytes 1572872 | tf_op jit(solution)/shard_map/ppermute | solution.py:470
  73.0 5.7 %copy-start = (bf16[2048,256]{1,0:T(8,128)(2,1)S(1)}, bf16[2048,256]{1,0:T(8,128)(2,1)}, u32[]{:S(2)}) copy-start(bf16[2048,256]{1,0:T(8,128)(2,1)} %basis_ref.1) | copy-start | bytes 3145732

commit v4 on v3

--- a/solution.py
+++ b/solution.py
@@ -150,12 +150,6 @@
 def pick(row, place):
     lane = lax.broadcasted_iota(jnp.int32, row.shape, 1)
     return jnp.sum(jnp.where(lane == place, row, 0.0)) > 0
-
-
-def listed(row_ref, place):
-    size = row_ref.shape[1]
-    inside = (place >= 0) & (place < size)
-    return inside & (row_ref[0, jnp.clip(place, 0, size - 1)] > 0)
 
 
 def skeleton_rows(rank, dim):
@@ -230,7 +224,7 @@
     steps = (plan.n // ROWS) * (plan.half // COLS)
     rows = plan.half // steps
 
-    def kernel(pay_ref, order_ref, target_ref, iterate_ref, step_ref, acc_ref, base_ref, factor_ref, left_ref, offset_ref):
+    def kernel(pay_ref, order_ref, target_ref, iterate_ref, step_ref, acc_ref, base_ref, left_ref, offset_ref):
         acc_ref[...] = jnp.zeros_like(acc_ref)
         for h in range(2):
             fill_left(plan, left_ref, pay_ref.at[h], h)
@@ -246,11 +240,6 @@
                         [target_ref[pl.ds(order_ref[0, first + u], 1), :] for u in range(group)], axis=0
                     )
                     base_ref[here, :] = iterate_ref[here, :] + step_row * wanted
-                if (step * rows) % LANES == 0:
-                    b = step * rows // LANES
-                    here = pl.ds(pl.multiple_of(h * plan.half + b * LANES, LANES), LANES)
-                    power = SHIFT + offset_ref[0:1, b * LANES : (b + 1) * LANES] + SHIFT
-                    factor_ref[here, :] = step_row * jnp.exp2(jnp.broadcast_to(power, (LANES, LANES)).T)
 
             fill_offset(plan, offset_ref, pay_ref.at[h])
             half_tile(plan, acc_ref.at[0], left_ref, pay_ref.at[h], offset_ref, beside)
@@ -258,55 +247,55 @@
     full = shaped(plan.n, plan.rhs, dtype=F32)
     return call(
         kernel,
-        [plan.acc(), full, full],
+        [plan.acc(), full],
         [(pay, VMEM), (ordering, SMEM), (target, VMEM), (iterate, VMEM), (step_size, VMEM)],
         scratch=[VMEM(plan.left().shape[1:], BF16)] + plan.offset_scratch(),
         flops=plan.tile_flops,
     )
 
 
-def pair_tiles(plan, near_row, pay, partner, acc):
-    def kernel(near_ref, pay_ref, partner_ref, acc_in, acc_ref, left_ref, row_ref, offset_ref):
+def pair_tiles(plan, pay, partner, acc):
+    def kernel(pay_ref, partner_ref, acc_in, acc_ref, left_ref, row_ref, offset_ref):
         place = lax.axis_index("leaf")
         core = lax.rem(place, 2)
         for h in range(2):
             fill_left(plan, left_ref.at[0], pay_ref.at[h], h)
             fill_left(plan, left_ref.at[1], partner_ref.at[h], h)
-        row = partner_ref[0, plan.flags :, :].astype(F32)
-        row_ref[...] = row
-
-        @pl.when(listed(near_ref, place + 1 - 2 * core))
+        rows = [ref[0, plan.flags :, :].astype(F32) for ref in (pay_ref, partner_ref)]
+        for t in range(2):
+            row_ref[t] = rows[t][0:8, :]
+
+        @pl.when(pick(rows[0][0:8, :], place + 1 - 2 * core))
         def _():
             fill_offset(plan, offset_ref, partner_ref.at[core])
             half_tile(plan, acc_ref.at[0], left_ref.at[0], partner_ref.at[core], offset_ref)
 
-        @pl.when(pick(row, place))
+        @pl.when(pick(rows[1][0:8, :], place))
         def _():
             fill_offset(plan, offset_ref, pay_ref.at[core])
             half_tile(plan, acc_ref.at[1], left_ref.at[1], pay_ref.at[core], offset_ref)
 
     return call(
         kernel,
-        [plan.acc(), plan.left(), shaped(FLAG_ROWS, LANES, dtype=F32)],
-        [(near_row, SMEM), (pay, VMEM), (partner, VMEM), (acc, VMEM)],
+        [plan.acc(), plan.left(), shaped(2, 8, LANES, dtype=F32)],
+        [(pay, VMEM), (partner, VMEM), (acc, VMEM)],
         scratch=plan.offset_scratch(),
         flops=plan.tile_flops,
-        aliases={3: 0},
-    )
-
-
-def side_tiles(plan, near_row, row, left, full, passed, acc, reach, last):
-    def kernel(near_ref, row_in, left_ref, full_ref, passed_ref, acc_in, acc_ref, *refs):
+        aliases={2: 0},
+    )
+
+
+def side_tiles(plan, row, left, full, passed, acc, reach, last):
+    def kernel(row_ref, left_ref, full_ref, passed_ref, acc_in, acc_ref, *refs):
         offset_ref = refs[-1]
         place = lax.axis_index("leaf")
         core = lax.rem(place, 2)
         away = 2 * core - 1
-        row = row_in[...]
         first = place + away * reach
         second = place - away - away * reach
         for source, at in ((full_ref.at[core], first), (passed_ref.at[core], second)):
-            on_mine = listed(near_ref, at)
-            on_theirs = pick(row, at)
+            on_mine = pick(row_ref[0], at)
+            on_theirs = pick(row_ref[1], at)
 
             @pl.when(on_mine | on_theirs)
             def _():
@@ -325,19 +314,19 @@
     return call(
         kernel,
         outs,
-        [(near_row, SMEM), (row, VMEM), (left, VMEM), (full, VMEM), (passed, VMEM), (acc, VMEM)],
+        [(row, VMEM), (left, VMEM), (full, VMEM), (passed, VMEM), (acc, VMEM)],
         scratch=plan.offset_scratch(),
         flops=2 * plan.tile_flops,
-        aliases={5: 0},
-    )
-
-
-def third_tile(plan, near_row, left, third, acc):
-    def kernel(near_ref, left_ref, third_ref, acc_in, acc_ref, offset_ref):
+        aliases={4: 0},
+    )
+
+
+def third_tile(plan, row, left, third, acc):
+    def kernel(row_ref, left_ref, third_ref, acc_in, acc_ref, offset_ref):
         place = lax.axis_index("leaf")
         away = 2 * lax.rem(place, 2) - 1
 
-        @pl.when(listed(near_ref, place + 3 * away))
+        @pl.when(pick(row_ref[0], place + 3 * away))
         def _():
             @pl.loop(0, 2)
             def _(h):
@@ -347,23 +336,28 @@
     return call(
         kernel,
         plan.acc(),
-        [(near_row, SMEM), (left, VMEM), (third, VMEM), (acc, VMEM)],
+        [(row, VMEM), (left, VMEM), (third, VMEM), (acc, VMEM)],
         scratch=plan.offset_scratch(),
         flops=plan.tile_flops,
         aliases={3: 0},
     )
 
 
-def finish(plan, acc, returned, base, factor, step_size, basis, local):
+def finish(plan, pay, acc, returned, base, step_size, basis, local):
     piece = 4 * LANES
 
-    def kernel(acc_ref, returned_ref, base_ref, factor_ref, step_ref, basis_ref, local_ref, out_hbm, out_ref, sems):
+    def kernel(pay_ref, acc_ref, returned_ref, base_ref, step_ref, basis_ref, local_ref, out_hbm, out_ref, sems):
         copies = []
         for first in range(0, plan.n, piece):
             rows = slice(first, first + piece)
-            far = step_ref[...] * matmul(basis_ref[rows, :], local_ref[...])
-            near = factor_ref[rows, :] * (acc_ref[0, rows, :] + returned_ref[rows, :].astype(F32))
-            out_ref[rows, :] = base_ref[rows, :] - (far + near)
+            far = matmul(basis_ref[rows, :], local_ref[...])
+            near = acc_ref[0, rows, :] + returned_ref[rows, :].astype(F32)
+            powers = [
+                SHIFT - norms(doubled_block(plan, pay_ref.at[at // plan.half], at % plan.half // LANES))
+                for at in range(first, first + piece, LANES)
+            ]
+            factor = jnp.concatenate([jnp.exp2(jnp.broadcast_to(p, (LANES, LANES)).T) for p in powers], axis=0)
+            out_ref[rows, :] = base_ref[rows, :] - step_ref[...] * (far + factor * near)
             copies.append(pltpu.make_async_copy(out_ref.at[rows, :], out_hbm.at[rows, :], sems.at[len(copies)]))
             copies[-1].start()
         for copy in copies:
@@ -372,7 +366,7 @@
     return call(
         kernel,
         shaped(plan.n, plan.rhs, dtype=F32),
-        [(value, VMEM) for value in (acc, returned, base, factor, step_size, basis, local)],
+        [(value, VMEM) for value in (pay, acc, returned, base, step_size, basis, local)],
         scratch=[VMEM((plan.n, plan.rhs), F32), pltpu.SemaphoreType.DMA((plan.n // piece,))],
         into=HBM,
         flops=2 * plan.n * basis.shape[1] * plan.rhs,
@@ -423,17 +417,13 @@
 
 def joined(mine, got, rank):
     rows = mine.shape[0] - rank
-    count = 1 + len(got)
-
-    def kernel(*refs):
-        out_ref = refs[-1]
-        share = jnp.zeros((rank, LANES), F32)
-        for k, ref in enumerate(refs[:-1]):
-            out_ref[k * rows : (k + 1) * rows, :] = ref[0:rows, :]
-            share = share + ref[rows:, :].astype(F32)
-        out_ref[count * rows :, :] = share.astype(BF16)
-
-    return call(kernel, shaped(count * rows + rank, LANES), [(b, VMEM) for b in (mine, *got)])
+
+    def kernel(mine_ref, got_ref, out_ref):
+        out_ref[0:rows, :] = mine_ref[0:rows, :]
+        out_ref[rows : 2 * rows, :] = got_ref[0:rows, :]
+        out_ref[2 * rows :, :] = (mine_ref[rows:, :].astype(F32) + got_ref[rows:, :].astype(F32)).astype(BF16)
+
+    return call(kernel, shaped(2 * rows + rank, LANES), [(mine, VMEM), (got, VMEM)])
 
 
 def down(far_row, leaf_t, transfer, mine, got, xors):
@@ -510,27 +500,29 @@
     over = routed(pay, "leaf", over_chips)
     others = [routed(up_block, "group", lambda i, k=k: i ^ k) for k in range(1, groups)]
     step_row = step_size.reshape(1, -1)
-    acc, base, factor = own_tile(plan, pay, ordering, target, iterate, step_row)
+    acc, base = own_tile(plan, pay, ordering, target, iterate, step_row)
     mine = across(cluster_far, cluster_t, up_block, others, lambda me, k: me ^ (k + 1), down_block)
-    acc, left, row = pair_tiles(plan, near_table, pay, partner, acc)
-
-    even = list(range(2, leaves, 2))[::-1]
-    blocks = [routed(mine, "leaf", lambda i, other=other: i ^ other) for other in even]
-    mine = joined(mine, blocks, rank)
-    got = routed(mine, "leaf", on_chip)
-    xors = [0] + even
-    xors = xors + [x ^ 1 for x in xors]
+    acc, left, row = pair_tiles(plan, pay, partner, acc)
+
+    xors, bit = [0], leaves // 2
+    while True:
+        got = routed(mine, "leaf", lambda i, bit=bit: i ^ bit)
+        xors = xors + [x ^ bit for x in xors]
+        if bit == 1:
+            break
+        mine = joined(mine, got, rank)
+        bit //= 2
     local = down(far_table, leaf_t, transfer, mine, got, xors)
 
     beside = routed(pay, "leaf", beside_chips)
     over_passed = routed(over, "leaf", on_chip)
-    (acc,) = side_tiles(plan, near_table, row, left, over, over_passed, acc, 2, False)
+    (acc,) = side_tiles(plan, row, left, over, over_passed, acc, 2, False)
     beside_passed = routed(beside, "leaf", on_chip)
     third = routed(beside, "leaf", over_chips)
-    acc, theirs = side_tiles(plan, near_table, row, left, beside, beside_passed, acc, 1, True)
+    acc, theirs = side_tiles(plan, row, left, beside, beside_passed, acc, 1, True)
     returned = routed(theirs, "leaf", on_chip)
-    acc = third_tile(plan, near_table, left, third, acc)
-    return finish(plan, acc, returned, base, factor, step_row, leaf_basis, local)
+    acc = third_tile(plan, row, left, third, acc)
+    return finish(plan, pay, acc, returned, base, step_row, leaf_basis, local)
 
 
 def solution(mesh):

time: 80.4 us -> 73.5 us (0.914)
  Pallas kernels: 42.1 us -> 38.8 us
  waiting for transfers between devices: 22 us -> 20 us
  starting transfers between devices: 15.6 us -> 14 us
    pallas_call x10 -> x11, Pallas kernels: 42.1 us -> 38.8 us  [call(): pl.pallas_call(kernel, out_shape=shapes, in_specs=[pl.BlockSpec(memory_sp...]
    ppermute x14 -> x13, waiting for transfers between devices: 22 us -> 20 us  [routed(): return lax.ppermute(block, axis, route)]
    ppermute x14 -> x13, starting transfers between devices: 15.6 us -> 14 us  [routed(): return lax.ppermute(block, axis, route)]
  transfers between devices with their start and end apart: 14 -> 13, of which waited for: 3 -> 4; matrix products, arithmetic and copies ran while one was open for 0% -> 0% of each run, Pallas kernels for 48% -> 48%
where the time goes in v4:
time: 73.5 us; the launch traced here: 73.3 us
  Pallas kernels  38.8 us (53%)
  waiting for transfers between devices  20 us (27%)
  starting transfers between devices  14 us (19%)
    pallas_call x11, Pallas kernels, call(): pl.pallas_call(kernel, out_shape=shapes, in_specs=[pl.BlockSpec(memory_sp...  38.8 us
    ppermute x13, waiting for transfers between devices, routed(): return lax.ppermute(block, axis, route)  20 us
    ppermute x13, starting transfers between devices, routed(): return lax.ppermute(block, axis, route)  14 us
  transfers between devices with their start and end apart: 13, of which 4 were waited for; matrix products, arithmetic and copies ran while one was open for 0% of the time, Pallas kernels for 48%

profile of v4, /device:TPU:15, one launch (start us, length us, event | category | flops | bytes accessed | tf_op | source)
XLA Modules:
  0.0 73.3 jit_solution(1776960098619708474)
XLA Ops:
  0.0 2.5 %shard_map.118 = (bf16[2,1552,128]{2,1,0:T(8,128)(2,1)S(1)}, bf16[384,128]{1,0:T(8,128)(2,1)S(1)}, bf16[384,128]{1,0:T(8,128)(2,1)S(1)}) custom-call(bf16[64,2048]{1,0:T(8,128)(2,1)} %bitcast.10, f32[2048,128]{1,0:T(8,128)} %iterate_ref.1, s32[1,8]{1,0:T(1,128)} %refs_2_.1, bf16[1,64,256]{2,1,0:T(8,128)(2,1)} %bitcast.6, bf16[1,64,256]{2,1,0:T(8,128)(2,1)} %bitcast.4, ...), custom_call_target="tpu_custom_call" | custom-call | flops 134217728 | bytes 2555936 | tf_op jit(solution)/shard_map/pallas_call | solution.py:35
  2.6 2.1 %collective-permute-start.4 = (bf16[2,1552,128]{2,1,0:T(8,128)(2,1)S(1)}, bf16[2,1552,128]{2,1,0:T(8,128)(2,1)S(1)}, u32[]{:S(2)}, u32[]{:S(2)}) collective-permute-start(bf16[2,1552,128]{2,1,0:T(8,128)(2,1)S(1)} %get-tuple-element.15.pay_ref), channel_id=1, source_target_pairs={{0,2},{2,4},{3,1},{4,6},{5,3},{7,5},{8,10},{10,12},{11,9},{12,14},... | collective-permute-start | bytes 2383880 | tf_op jit(solution)/shard_map/ppermute | solution.py:460
  4.7 5.2 %collective-permute-start.1 = (bf16[2,1552,128]{2,1,0:T(8,128)(2,1)S(1)}, bf16[2,1552,128]{2,1,0:T(8,128)(2,1)S(1)}, u32[]{:S(2)}, u32[]{:S(2)}) collective-permute-start(bf16[2,1552,128]{2,1,0:T(8,128)(2,1)S(1)} %get-tuple-element.15.pay_ref), channel_id=1, source_target_pairs={{1,2},{2,1},{3,4},{4,3},{5,6},{6,5},{9,10},{10,9},{11,12},{12,11},... | collective-permute-start | bytes 2383880 | tf_op jit(solution)/shard_map/ppermute | solution.py:460
  9.8 0.1 collective-permute-start
  9.9 0.3 collective-permute-start.7
  10.2 0.2 collective-permute-start.8
  10.5 3.4 %collective-permute-done.7.refs_0_ = bf16[384,128]{1,0:T(8,128)(2,1)S(1)} collective-permute-done((bf16[384,128]{1,0:T(8,128)(2,1)S(1)}, bf16[384,128]{1,0:T(8,128)(2,1)S(1)}, u32[]{:S(2)}, u32[]{:S(2)}) %collective-permute-start.7) | collective-permute-done | bytes 98336 | tf_op jit(solution)/shard_map/ppermute | solution.py:460
  13.9 0.2 collective-permute-start.9
  14.1 0.0 collective-permute-done.8.refs_1_
  14.1 4.2 %collective-permute-done.9.refs_2_ = bf16[384,128]{1,0:T(8,128)(2,1)S(1)} collective-permute-done((bf16[384,128]{1,0:T(8,128)(2,1)S(1)}, bf16[384,128]{1,0:T(8,128)(2,1)S(1)}, u32[]{:S(2)}, u32[]{:S(2)}) %collective-permute-start.9) | collective-permute-done | bytes 98336 | tf_op jit(solution)/shard_map/ppermute | solution.py:460
  18.3 1.3 %shard_map.124.mine_ref = bf16[640,128]{1,0:T(8,128)(2,1)S(1)} custom-call(s32[1,4]{1,0:T(1,128)S(1)} %copy-done.8, bf16[1,64,256]{2,1,0:T(8,128)(2,1)S(1)} %bitcast.5, bf16[384,128]{1,0:T(8,128)(2,1)S(1)} %get-tuple-element.23.down_ref, bf16[384,128]{1,0:T(8,128)(2,1)S(1)} %get-tuple-element.24.own_ref, ...), custom_call_target="tpu_custom_call" | custom-call | flops 268435456 | bytes 524304 | tf_op jit(solution)/shard_map/pallas_call | solution.py:35
  19.6 0.1 collective-permute-start.10
  19.7 11.8 %collective-permute-done.10.got_ref = bf16[640,128]{1,0:T(8,128)(2,1)S(1)} collective-permute-done((bf16[640,128]{1,0:T(8,128)(2,1)S(1)}, bf16[640,128]{1,0:T(8,128)(2,1)S(1)}, u32[]{:S(2)}, u32[]{:S(2)}) %collective-permute-start.10) | collective-permute-done | bytes 163872 | tf_op jit(solution)/shard_map/ppermute | solution.py:460
  31.5 0.1 collective-permute-start.11
  31.6 1.6 %collective-permute-start.5 = (bf16[2,1552,128]{2,1,0:T(8,128)(2,1)S(1)}, bf16[2,1552,128]{2,1,0:T(8,128)(2,1)S(1)}, u32[]{:S(2)}, u32[]{:S(2)}) collective-permute-start(bf16[2,1552,128]{2,1,0:T(8,128)(2,1)S(1)} %collective-permute-done.4.full_ref), channel_id=1, source_target_pairs={{0,1},{1,0},{2,3},{3,2},{4,5},{5,4},{6,7},{7,6},{8,9},{9,8},{10,11... | collective-permute-start | bytes 2383880 | tf_op jit(solution)/shard_map/ppermute | solution.py:460
  33.2 6.0 %shard_map.119 = (f32[2,2048,128]{2,1,0:T(8,128)S(1)}, f32[2048,128]{1,0:T(8,128)S(1)}) custom-call(bf16[2,1552,128]{2,1,0:T(8,128)(2,1)S(1)} %get-tuple-element.15.pay_ref, s32[1,2048]{1,0:T(1,128)S(1)} %copy-done.7, f32[2048,128]{1,0:T(8,128)S(1)} %copy-done.6, f32[2048,128]{1,0:T(8,128)S(1)} %copy-done.1, f32[1,128]{1,0:T(1,128)S(1)} %bitcast.8), custom_call_target="tpu_custom_call" | custom-call | flops 4294967296 | bytes 2900480 | tf_op jit(solution)/shard_map/pallas_call | solution.py:35
  39.2 0.7 collective-permute-done.11.got_ref
  39.9 0.5 collective-permute-start.12
  40.4 0.0 collective-permute-done.1.full_ref
  40.4 0.1 collective-permute-start.3
  40.5 1.9 %collective-permute-start.2 = (bf16[2,1552,128]{2,1,0:T(8,128)(2,1)S(1)}, bf16[2,1552,128]{2,1,0:T(8,128)(2,1)S(1)}, u32[]{:S(2)}, u32[]{:S(2)}) collective-permute-start(bf16[2,1552,128]{2,1,0:T(8,128)(2,1)S(1)} %collective-permute-done.1.full_ref), channel_id=1, source_target_pairs={{0,2},{2,4},{3,1},{4,6},{5,3},{7,5},{8,10},{10,12},{11,9},{12,14},... | collective-permute-start | bytes 2383880 | tf_op jit(solution)/shard_map/ppermute | solution.py:460
  42.4 3.0 %shard_map.120 = (f32[2,2048,128]{2,1,0:T(8,128)S(1)}, bf16[2,2048,64]{2,1,0:T(8,128)(2,1)S(1)}, f32[2,8,128]{2,1,0:T(8,128)S(1)}) custom-call(bf16[2,1552,128]{2,1,0:T(8,128)(2,1)S(1)} %get-tuple-element.15.pay_ref, bf16[2,1552,128]{2,1,0:T(8,128)(2,1)S(1)} %collective-permute-done.partner_ref, ...), custom_call_target="tpu_custom_call", output_to_operand_aliasing={{0}: (2, {})} | custom-call | flops 4294967296 | bytes 3686400 | tf_op jit(solution)/shard_map/pallas_call | solution.py:35
  45.4 7.9 %shard_map.121.acc_in = f32[2,2048,128]{2,1,0:T(8,128)S(1)} custom-call(f32[2,8,128]{2,1,0:T(8,128)S(1)} %get-tuple-element.17.row_ref, bf16[2,2048,64]{2,1,0:T(8,128)(2,1)S(1)} %get-tuple-element.18.left_ref, bf16[2,1552,128]{2,1,0:T(8,128)(2,1)S(1)} %collective-permute-done.4.full_ref, ...), custom_call_target="tpu_custom_call", output_to_operand_aliasing={{}: (4, {})} | custom-call | flops 8589934592 | bytes 4218880 | tf_op jit(solution)/shard_map/pallas_call | solution.py:35
  53.3 0.0 copy-start.2
  53.3 0.0 copy-start.4
  53.3 0.0 copy-start.9
  53.4 10.2 %shard_map.122 = (f32[2,2048,128]{2,1,0:T(8,128)S(1)}, bf16[2048,128]{1,0:T(8,128)(2,1)S(1)}) custom-call(f32[2,8,128]{2,1,0:T(8,128)S(1)} %get-tuple-element.17.row_ref, bf16[2,2048,64]{2,1,0:T(8,128)(2,1)S(1)} %get-tuple-element.18.left_ref, bf16[2,1552,128]{2,1,0:T(8,128)(2,1)S(1)} %collective-permute-done.1.full_ref, ...), custom_call_target="tpu_custom_call", output_to_operand_aliasing={{0}: (4, {})} | custom-call | flops 8589934592 | bytes 4218880 | tf_op jit(solution)/shard_map/pallas_call | solution.py:35
  63.6 1.7 %collective-permute-start.6 = (bf16[2048,128]{1,0:T(8,128)(2,1)S(1)}, bf16[2048,128]{1,0:T(8,128)(2,1)S(1)}, u32[]{:S(2)}, u32[]{:S(2)}) collective-permute-start(bf16[2048,128]{1,0:T(8,128)(2,1)S(1)} %get-tuple-element.21), channel_id=1, source_target_pairs={{0,1},{1,0},{2,3},{3,2},{4,5},{5,4},{6,7},{7,6},{8,9},{9,8},{10,11... | collective-permute-start | bytes 1572872 | tf_op jit(solution)/shard_map/ppermute | solution.py:460
  65.3 1.1 %shard_map.127.local_ref = bf16[256,128]{1,0:T(8,128)(2,1)S(1)} custom-call(s32[1,8]{1,0:T(1,128)S(1)} %copy-done.9, bf16[1,64,256]{2,1,0:T(8,128)(2,1)S(1)} %bitcast.7, bf16[1,256,256]{2,1,0:T(8,128)(2,1)S(1)} %copy-done.2, bf16[1792,128]{1,0:T(8,128)(2,1)S(1)} %shard_map.126.mine_ref, bf16[1792,128]{1,0:T(8,128)(2,1)S(1)} %collective-permute-done.12.got_ref), custom_call_target="tpu_custom_call" | custom-call | flops 536870912 | bytes 1081376 | tf_op jit(solution)/shard_map/pallas_call | solution.py:35
  66.4 0.0 copy-start
  66.4 5.3 %shard_map.123.acc_ref = f32[2,2048,128]{2,1,0:T(8,128)S(1)} custom-call(f32[2,8,128]{2,1,0:T(8,128)S(1)} %get-tuple-element.17.row_ref, bf16[2,2048,64]{2,1,0:T(8,128)(2,1)S(1)} %get-tuple-element.18.left_ref, bf16[2,1552,128]{2,1,0:T(8,128)(2,1)S(1)} %collective-permute-done.2.third_ref, ...), custom_call_target="tpu_custom_call", output_to_operand_aliasing={{}: (3, {})} | custom-call | flops 4294967296 | bytes 3424256 | tf_op jit(solution)/shard_map/pallas_call | solution.py:35
  71.7 1.4 %shard_map.128 = f32[2048,128]{1,0:T(8,128)} custom-call(bf16[2,1552,128]{2,1,0:T(8,128)(2,1)S(1)} %get-tuple-element.15.pay_ref, f32[2,2048,128]{2,1,0:T(8,128)S(1)} %shard_map.123.acc_ref, bf16[2048,128]{1,0:T(8,128)(2,1)S(1)} %collective-permute-done.6.returned_ref, f32[2048,128]{1,0:T(8,128)S(1)} %get-tuple-element.22.base_ref, f32[1,128]{1,0:T(1,128)S(1)} %bitcast.9, ...), custom_call_target="tpu_custom_call" | custom-call | flops 134217728 | bytes 5579264 | tf_op jit(solution)/shard_map/pallas_call | solution.py:35
  (25 shorter events, 0.1 us)
Async XLA Ops:
  0.0 18.3 %copy-start.3 = (bf16[1,256,64]{1,2,0:T(8,128)(2,1)S(1)}, bf16[1,256,64]{1,2,0:T(8,128)(2,1)}, u32[]{:S(2)}) copy-start(bf16[1,256,64]{1,2,0:T(8,128)(2,1)} %param.20) | copy-start | bytes 98308
  0.0 33.2 %copy-start.1 = (f32[2048,128]{1,0:T(8,128)S(1)}, f32[2048,128]{1,0:T(8,128)}, u32[]{:S(2)}) copy-start(f32[2048,128]{1,0:T(8,128)} %iterate_ref.1) | copy-start | bytes 3145732
  0.0 18.3 %copy-start.8 = (s32[1,4]{1,0:T(1,128)S(1)}, s32[1,4]{1,0:T(1,128)}, u32[]{:S(2)}) copy-start(s32[1,4]{1,0:T(1,128)} %far_ref.2) | copy-start | bytes 52
  0.0 33.2 %copy-start.5 = (f32[128]{0:T(128)S(1)}, f32[128]{0:T(128)}, u32[]{:S(2)}) copy-start(f32[128]{0:T(128)} %param.16) | copy-start | bytes 1540
  0.0 33.2 %copy-start.7 = (s32[1,2048]{1,0:T(1,128)S(1)}, s32[1,2048]{1,0:T(1,128)}, u32[]{:S(2)}) copy-start(s32[1,2048]{1,0:T(1,128)} %order_ref.1) | copy-start | bytes 24580
  0.0 33.2 %copy-start.6 = (f32[2048,128]{1,0:T(8,128)S(1)}, f32[2048,128]{1,0:T(8,128)}, u32[]{:S(2)}) copy-start(f32[2048,128]{1,0:T(8,128)} %target_ref.1) | copy-start | bytes 3145732
  2.6 29.0 %collective-permute-start.4 = (bf16[2,1552,128]{2,1,0:T(8,128)(2,1)S(1)}, bf16[2,1552,128]{2,1,0:T(8,128)(2,1)S(1)}, u32[]{:S(2)}, u32[]{:S(2)}) collective-permute-start(bf16[2,1552,128]{2,1,0:T(8,128)(2,1)S(1)} %get-tuple-element.15.pay_ref), channel_id=1, source_target_pairs={{0,2},{2,4},{3,1},{4,6},{5,3},{7,5},{8,10},{10,12},{11,9},{12,14},... | collective-permute-start | bytes 2383880 | tf_op jit(solution)/shard_map/ppermute | solution.py:460
  4.7 35.7 %collective-permute-start.1 = (bf16[2,1552,128]{2,1,0:T(8,128)(2,1)S(1)}, bf16[2,1552,128]{2,1,0:T(8,128)(2,1)S(1)}, u32[]{:S(2)}, u32[]{:S(2)}) collective-permute-start(bf16[2,1552,128]{2,1,0:T(8,128)(2,1)S(1)} %get-tuple-element.15.pay_ref), channel_id=1, source_target_pairs={{1,2},{2,1},{3,4},{4,3},{5,6},{6,5},{9,10},{10,9},{11,12},{12,11},... | collective-permute-start | bytes 2383880 | tf_op jit(solution)/shard_map/ppermute | solution.py:460
  9.8 32.6 %collective-permute-start = (bf16[2,1552,128]{2,1,0:T(8,128)(2,1)S(1)}, bf16[2,1552,128]{2,1,0:T(8,128)(2,1)S(1)}, u32[]{:S(2)}, u32[]{:S(2)}) collective-permute-start(bf16[2,1552,128]{2,1,0:T(8,128)(2,1)S(1)} %get-tuple-element.15.pay_ref), channel_id=1, source_target_pairs={{0,1},{1,0},{2,3},{3,2},{4,5},{5,4},{6,7},{7,6},{8,9},{9,8},{10,11... | collective-permute-start | bytes 2383880 | tf_op jit(solution)/shard_map/ppermute | solution.py:460
  9.9 4.0 %collective-permute-start.7 = (bf16[384,128]{1,0:T(8,128)(2,1)S(1)}, bf16[384,128]{1,0:T(8,128)(2,1)S(1)}, u32[]{:S(2)}, u32[]{:S(2)}) collective-permute-start(bf16[384,128]{1,0:T(8,128)(2,1)S(1)} %get-tuple-element.24.own_ref), channel_id=1, source_target_pairs={{0,8},{8,0},{16,24},{24,16},{1,9},{9,1},{17,25},{25,17},{2,10},{10... | collective-permute-start | bytes 294920 | tf_op jit(solution)/shard_map/ppermute | solution.py:460
  10.2 3.9 %collective-permute-start.8 = (bf16[384,128]{1,0:T(8,128)(2,1)S(1)}, bf16[384,128]{1,0:T(8,128)(2,1)S(1)}, u32[]{:S(2)}, u32[]{:S(2)}) collective-permute-start(bf16[384,128]{1,0:T(8,128)(2,1)S(1)} %get-tuple-element.24.own_ref), channel_id=1, source_target_pairs={{0,16},{8,24},{16,0},{24,8},{1,17},{9,25},{17,1},{25,9},{2,18},{10... | collective-permute-start | bytes 294920 | tf_op jit(solution)/shard_map/ppermute | solution.py:460
  13.9 4.4 %collective-permute-start.9 = (bf16[384,128]{1,0:T(8,128)(2,1)S(1)}, bf16[384,128]{1,0:T(8,128)(2,1)S(1)}, u32[]{:S(2)}, u32[]{:S(2)}) collective-permute-start(bf16[384,128]{1,0:T(8,128)(2,1)S(1)} %get-tuple-element.24.own_ref), channel_id=1, source_target_pairs={{0,24},{8,16},{16,8},{24,0},{1,25},{9,17},{17,9},{25,1},{2,26},{10... | collective-permute-start | bytes 294920 | tf_op jit(solution)/shard_map/ppermute | solution.py:460
  19.6 11.8 %collective-permute-start.10 = (bf16[640,128]{1,0:T(8,128)(2,1)S(1)}, bf16[640,128]{1,0:T(8,128)(2,1)S(1)}, u32[]{:S(2)}, u32[]{:S(2)}) collective-permute-start(bf16[640,128]{1,0:T(8,128)(2,1)S(1)} %shard_map.124.mine_ref), channel_id=1, source_target_pairs={{0,4},{1,5},{2,6},{3,7},{4,0},{5,1},{6,2},{7,3},{8,12},{9,13},{10,... | collective-permute-start | bytes 491528 | tf_op jit(solution)/shard_map/ppermute | solution.py:460
  31.5 8.3 %collective-permute-start.11 = (bf16[1024,128]{1,0:T(8,128)(2,1)S(1)}, bf16[1024,128]{1,0:T(8,128)(2,1)S(1)}, u32[]{:S(2)}, u32[]{:S(2)}) collective-permute-start(bf16[1024,128]{1,0:T(8,128)(2,1)S(1)} %shard_map.125.mine_ref), channel_id=1, source_target_pairs={{0,2},{1,3},{2,0},{3,1},{4,6},{5,7},{6,4},{7,5},{8,10},{9,11},{10,... | collective-permute-start | bytes 786440 | tf_op jit(solution)/shard_map/ppermute | solution.py:460
  31.6 13.8 %collective-permute-start.5 = (bf16[2,1552,128]{2,1,0:T(8,128)(2,1)S(1)}, bf16[2,1552,128]{2,1,0:T(8,128)(2,1)S(1)}, u32[]{:S(2)}, u32[]{:S(2)}) collective-permute-start(bf16[2,1552,128]{2,1,0:T(8,128)(2,1)S(1)} %collective-permute-done.4.full_ref), channel_id=1, source_target_pairs={{0,1},{1,0},{2,3},{3,2},{4,5},{5,4},{6,7},{7,6},{8,9},{9,8},{10,11... | collective-permute-start | bytes 2383880 | tf_op jit(solution)/shard_map/ppermute | solution.py:460
  39.9 25.4 %collective-permute-start.12 = (bf16[1792,128]{1,0:T(8,128)(2,1)S(1)}, bf16[1792,128]{1,0:T(8,128)(2,1)S(1)}, u32[]{:S(2)}, u32[]{:S(2)}) collective-permute-start(bf16[1792,128]{1,0:T(8,128)(2,1)S(1)} %shard_map.126.mine_ref), channel_id=1, source_target_pairs={{0,1},{1,0},{2,3},{3,2},{4,5},{5,4},{6,7},{7,6},{8,9},{9,8},{10,11... | collective-permute-start | bytes 1376264 | tf_op jit(solution)/shard_map/ppermute | solution.py:460
  40.4 12.9 %collective-permute-start.3 = (bf16[2,1552,128]{2,1,0:T(8,128)(2,1)S(1)}, bf16[2,1552,128]{2,1,0:T(8,128)(2,1)S(1)}, u32[]{:S(2)}, u32[]{:S(2)}) collective-permute-start(bf16[2,1552,128]{2,1,0:T(8,128)(2,1)S(1)} %collective-permute-done.1.full_ref), channel_id=1, source_target_pairs={{0,1},{1,0},{2,3},{3,2},{4,5},{5,4},{6,7},{7,6},{8,9},{9,8},{10,11... | collective-permute-start | bytes 2383880 | tf_op jit(solution)/shard_map/ppermute | solution.py:460
  40.5 25.9 %collective-permute-start.2 = (bf16[2,1552,128]{2,1,0:T(8,128)(2,1)S(1)}, bf16[2,1552,128]{2,1,0:T(8,128)(2,1)S(1)}, u32[]{:S(2)}, u32[]{:S(2)}) collective-permute-start(bf16[2,1552,128]{2,1,0:T(8,128)(2,1)S(1)} %collective-permute-done.1.full_ref), channel_id=1, source_target_pairs={{0,2},{2,4},{3,1},{4,6},{5,3},{7,5},{8,10},{10,12},{11,9},{12,14},... | collective-permute-start | bytes 2383880 | tf_op jit(solution)/shard_map/ppermute | solution.py:460
  53.3 12.0 %copy-start.2 = (bf16[1,256,256]{2,1,0:T(8,128)(2,1)S(1)}, bf16[1,256,256]{2,1,0:T(8,128)(2,1)}, u32[]{:S(2)}) copy-start(bf16[1,256,256]{2,1,0:T(8,128)(2,1)} %transfer_ref.1) | copy-start | bytes 393220
  53.3 11.9 %copy-start.4 = (bf16[1,256,64]{1,2,0:T(8,128)(2,1)S(1)}, bf16[1,256,64]{1,2,0:T(8,128)(2,1)}, u32[]{:S(2)}) copy-start(bf16[1,256,64]{1,2,0:T(8,128)(2,1)} %param.19) | copy-start | bytes 98308
  53.3 11.9 %copy-start.9 = (s32[1,8]{1,0:T(1,128)S(1)}, s32[1,8]{1,0:T(1,128)}, u32[]{:S(2)}) copy-start(s32[1,8]{1,0:T(1,128)} %far_ref.3) | copy-start | bytes 100
  63.6 8.1 %collective-permute-start.6 = (bf16[2048,128]{1,0:T(8,128)(2,1)S(1)}, bf16[2048,128]{1,0:T(8,128)(2,1)S(1)}, u32[]{:S(2)}, u32[]{:S(2)}) collective-permute-start(bf16[2048,128]{1,0:T(8,128)(2,1)S(1)} %get-tuple-element.21), channel_id=1, source_target_pairs={{0,1},{1,0},{2,3},{3,2},{4,5},{5,4},{6,7},{7,6},{8,9},{9,8},{10,11... | collective-permute-start | bytes 1572872 | tf_op jit(solution)/shard_map/ppermute | solution.py:460
  66.4 5.3 %copy-start = (bf16[2048,256]{1,0:T(8,128)(2,1)S(1)}, bf16[2048,256]{1,0:T(8,128)(2,1)}, u32[]{:S(2)}) copy-start(bf16[2048,256]{1,0:T(8,128)(2,1)} %basis_ref.1) | copy-start | bytes 3145732

commit v5 on v4

--- a/solution.py
+++ b/solution.py
@@ -285,7 +285,7 @@
     )
 
 
-def side_tiles(plan, row, left, full, passed, acc, reach, last):
+def side_tiles(plan, row, left, full, passed, acc, reach):
     def kernel(row_ref, left_ref, full_ref, passed_ref, acc_in, acc_ref, *refs):
         offset_ref = refs[-1]
         place = lax.axis_index("leaf")
@@ -307,10 +307,7 @@
                 def _():
                     half_tile(plan, acc_ref.at[t], left_ref.at[t], source, offset_ref)
 
-        if last:
-            refs[0][...] = acc_ref[1].astype(BF16)
-
-    outs = [plan.acc()] + ([shaped(plan.n, plan.rhs)] if last else [])
+    outs = plan.acc()
     return call(
         kernel,
         outs,
@@ -321,25 +318,27 @@
     )
 
 
-def third_tile(plan, row, left, third, acc):
-    def kernel(row_ref, left_ref, third_ref, acc_in, acc_ref, offset_ref):
+def third_tile(plan, row, left, third, passed, acc):
+    def kernel(row_ref, left_ref, third_ref, passed_ref, acc_in, acc_ref, theirs_ref, offset_ref):
         place = lax.axis_index("leaf")
-        away = 2 * lax.rem(place, 2) - 1
-
-        @pl.when(pick(row_ref[0], place + 3 * away))
-        def _():
-            @pl.loop(0, 2)
-            def _(h):
-                fill_offset(plan, offset_ref, third_ref.at[h])
-                half_tile(plan, acc_ref.at[0], left_ref.at[0], third_ref.at[h], offset_ref)
-
-    return call(
-        kernel,
-        plan.acc(),
-        [(row, VMEM), (left, VMEM), (third, VMEM), (acc, VMEM)],
+        core = lax.rem(place, 2)
+        away = 2 * core - 1
+        for t, source, at in ((0, third_ref.at[core], place + 3 * away), (1, passed_ref.at[core], place - 4 * away)):
+
+            @pl.when(pick(row_ref[t], at))
+            def _():
+                fill_offset(plan, offset_ref, source)
+                half_tile(plan, acc_ref.at[t], left_ref.at[t], source, offset_ref)
+
+        theirs_ref[...] = acc_ref[1].astype(BF16)
+
+    return call(
+        kernel,
+        [plan.acc(), shaped(plan.n, plan.rhs)],
+        [(row, VMEM), (left, VMEM), (third, VMEM), (passed, VMEM), (acc, VMEM)],
         scratch=plan.offset_scratch(),
         flops=plan.tile_flops,
-        aliases={3: 0},
+        aliases={4: 0},
     )
 
 
@@ -516,12 +515,13 @@
 
     beside = routed(pay, "leaf", beside_chips)
     over_passed = routed(over, "leaf", on_chip)
-    (acc,) = side_tiles(plan, row, left, over, over_passed, acc, 2, False)
+    acc = side_tiles(plan, row, left, over, over_passed, acc, 2)
     beside_passed = routed(beside, "leaf", on_chip)
     third = routed(beside, "leaf", over_chips)
-    acc, theirs = side_tiles(plan, row, left, beside, beside_passed, acc, 1, True)
+    acc = side_tiles(plan, row, left, beside, beside_passed, acc, 1)
+    third_passed = routed(third, "leaf", on_chip)
+    acc, theirs = third_tile(plan, row, left, third, third_passed, acc)
     returned = routed(theirs, "leaf", on_chip)
-    acc = third_tile(plan, row, left, third, acc)
     return finish(plan, pay, acc, returned, base, step_row, leaf_basis, local)
 
 

time: 73.5 us -> 70.2 us (0.955)
  the two profiles are of different devices: /device:TPU:15 before, /device:TPU:14 now
where the time goes in v5:
time: 70.2 us; the launch traced here: 70 us
  Pallas kernels  37.4 us (53%)
  starting transfers between devices  18.4 us (26%)
  waiting for transfers between devices  13.7 us (20%)
    pallas_call x11, Pallas kernels, call(): pl.pallas_call(kernel, out_shape=shapes, in_specs=[pl.BlockSpec(memory_sp...  37.4 us
    ppermute x14, starting transfers between devices, routed(): return lax.ppermute(block, axis, route)  18.4 us
    ppermute x14, waiting for transfers between devices, routed(): return lax.ppermute(block, axis, route)  13.7 us
  transfers between devices with their start and end apart: 14, of which 5 were waited for; matrix products, arithmetic and copies ran while one was open for 0% of the time, Pallas kernels for 48%

profile of v5, /device:TPU:14, one launch (start us, length us, event | category | flops | bytes accessed | tf_op | source)
XLA Modules:
  0.0 70.0 jit_solution(14058713066652935877)
XLA Ops:
  0.0 2.5 %shard_map.118 = (bf16[2,1552,128]{2,1,0:T(8,128)(2,1)S(1)}, bf16[384,128]{1,0:T(8,128)(2,1)S(1)}, bf16[384,128]{1,0:T(8,128)(2,1)S(1)}) custom-call(bf16[64,2048]{1,0:T(8,128)(2,1)} %bitcast.10, f32[2048,128]{1,0:T(8,128)} %iterate_ref.1, s32[1,8]{1,0:T(1,128)} %refs_2_.1, bf16[1,64,256]{2,1,0:T(8,128)(2,1)} %bitcast.6, bf16[1,64,256]{2,1,0:T(8,128)(2,1)} %bitcast.4, ...), custom_call_target="tpu_custom_call" | custom-call | flops 134217728 | bytes 2555936 | tf_op jit(solution)/shard_map/pallas_call | solution.py:35
  2.6 3.5 %collective-permute-start.5 = (bf16[2,1552,128]{2,1,0:T(8,128)(2,1)S(1)}, bf16[2,1552,128]{2,1,0:T(8,128)(2,1)S(1)}, u32[]{:S(2)}, u32[]{:S(2)}) collective-permute-start(bf16[2,1552,128]{2,1,0:T(8,128)(2,1)S(1)} %get-tuple-element.15.pay_ref), channel_id=1, source_target_pairs={{0,2},{2,4},{3,1},{4,6},{5,3},{7,5},{8,10},{10,12},{11,9},{12,14},... | collective-permute-start | bytes 2383880 | tf_op jit(solution)/shard_map/ppermute | solution.py:459
  6.1 1.9 %collective-permute-start.1 = (bf16[2,1552,128]{2,1,0:T(8,128)(2,1)S(1)}, bf16[2,1552,128]{2,1,0:T(8,128)(2,1)S(1)}, u32[]{:S(2)}, u32[]{:S(2)}) collective-permute-start(bf16[2,1552,128]{2,1,0:T(8,128)(2,1)S(1)} %get-tuple-element.15.pay_ref), channel_id=1, source_target_pairs={{1,2},{2,1},{3,4},{4,3},{5,6},{6,5},{9,10},{10,9},{11,12},{12,11},... | collective-permute-start | bytes 2383880 | tf_op jit(solution)/shard_map/ppermute | solution.py:459
  8.0 1.7 %collective-permute-start = (bf16[2,1552,128]{2,1,0:T(8,128)(2,1)S(1)}, bf16[2,1552,128]{2,1,0:T(8,128)(2,1)S(1)}, u32[]{:S(2)}, u32[]{:S(2)}) collective-permute-start(bf16[2,1552,128]{2,1,0:T(8,128)(2,1)S(1)} %get-tuple-element.15.pay_ref), channel_id=1, source_target_pairs={{0,1},{1,0},{2,3},{3,2},{4,5},{5,4},{6,7},{7,6},{8,9},{9,8},{10,11... | collective-permute-start | bytes 2383880 | tf_op jit(solution)/shard_map/ppermute | solution.py:459
  9.7 0.5 collective-permute-start.10
  10.2 1.5 %collective-permute-start.8 = (bf16[384,128]{1,0:T(8,128)(2,1)S(1)}, bf16[384,128]{1,0:T(8,128)(2,1)S(1)}, u32[]{:S(2)}, u32[]{:S(2)}) collective-permute-start(bf16[384,128]{1,0:T(8,128)(2,1)S(1)} %get-tuple-element.24.own_ref), channel_id=1, source_target_pairs={{0,8},{8,0},{16,24},{24,16},{1,9},{9,1},{17,25},{25,17},{2,10},{10... | collective-permute-start | bytes 294920 | tf_op jit(solution)/shard_map/ppermute | solution.py:459
  11.7 4.6 %collective-permute-done.10.refs_2_ = bf16[384,128]{1,0:T(8,128)(2,1)S(1)} collective-permute-done((bf16[384,128]{1,0:T(8,128)(2,1)S(1)}, bf16[384,128]{1,0:T(8,128)(2,1)S(1)}, u32[]{:S(2)}, u32[]{:S(2)}) %collective-permute-start.10) | collective-permute-done | bytes 98336 | tf_op jit(solution)/shard_map/ppermute | solution.py:459
  16.3 0.5 collective-permute-start.9
  16.8 4.1 %collective-permute-done.9.refs_1_ = bf16[384,128]{1,0:T(8,128)(2,1)S(1)} collective-permute-done((bf16[384,128]{1,0:T(8,128)(2,1)S(1)}, bf16[384,128]{1,0:T(8,128)(2,1)S(1)}, u32[]{:S(2)}, u32[]{:S(2)}) %collective-permute-start.9) | collective-permute-done | bytes 98336 | tf_op jit(solution)/shard_map/ppermute | solution.py:459
  20.9 1.3 %shard_map.124.mine_ref = bf16[640,128]{1,0:T(8,128)(2,1)S(1)} custom-call(s32[1,4]{1,0:T(1,128)S(1)} %copy-done.8, bf16[1,64,256]{2,1,0:T(8,128)(2,1)S(1)} %bitcast.5, bf16[384,128]{1,0:T(8,128)(2,1)S(1)} %get-tuple-element.23.down_ref, bf16[384,128]{1,0:T(8,128)(2,1)S(1)} %get-tuple-element.24.own_ref, ...), custom_call_target="tpu_custom_call" | custom-call | flops 268435456 | bytes 524304 | tf_op jit(solution)/shard_map/pallas_call | solution.py:35
  22.3 0.1 collective-permute-start.11
  22.4 0.1 collective-permute-start.6
  22.5 2.6 %collective-permute-done.1.full_ref = bf16[2,1552,128]{2,1,0:T(8,128)(2,1)S(1)} collective-permute-done((bf16[2,1552,128]{2,1,0:T(8,128)(2,1)S(1)}, bf16[2,1552,128]{2,1,0:T(8,128)(2,1)S(1)}, u32[]{:S(2)}, u32[]{:S(2)}) %collective-permute-start.1) | collective-permute-done | bytes 794656 | tf_op jit(solution)/shard_map/ppermute | solution.py:459
  25.1 7.7 %collective-permute-start.2 = (bf16[2,1552,128]{2,1,0:T(8,128)(2,1)S(1)}, bf16[2,1552,128]{2,1,0:T(8,128)(2,1)S(1)}, u32[]{:S(2)}, u32[]{:S(2)}) collective-permute-start(bf16[2,1552,128]{2,1,0:T(8,128)(2,1)S(1)} %collective-permute-done.1.full_ref), channel_id=1, source_target_pairs={{0,2},{2,4},{3,1},{4,6},{5,3},{7,5},{8,10},{10,12},{11,9},{12,14},... | collective-permute-start | bytes 2383880 | tf_op jit(solution)/shard_map/ppermute | solution.py:459
  32.8 6.0 %shard_map.119 = (f32[2,2048,128]{2,1,0:T(8,128)S(1)}, f32[2048,128]{1,0:T(8,128)S(1)}) custom-call(bf16[2,1552,128]{2,1,0:T(8,128)(2,1)S(1)} %get-tuple-element.15.pay_ref, s32[1,2048]{1,0:T(1,128)S(1)} %copy-done.7, f32[2048,128]{1,0:T(8,128)S(1)} %copy-done.6, f32[2048,128]{1,0:T(8,128)S(1)} %copy-done.1, f32[1,128]{1,0:T(1,128)S(1)} %bitcast.8), custom_call_target="tpu_custom_call" | custom-call | flops 4294967296 | bytes 2900480 | tf_op jit(solution)/shard_map/pallas_call | solution.py:35
  38.8 0.1 collective-permute-start.12
  38.9 0.1 collective-permute-start.4
  39.0 3.0 %shard_map.120 = (f32[2,2048,128]{2,1,0:T(8,128)S(1)}, bf16[2,2048,64]{2,1,0:T(8,128)(2,1)S(1)}, f32[2,8,128]{2,1,0:T(8,128)S(1)}) custom-call(bf16[2,1552,128]{2,1,0:T(8,128)(2,1)S(1)} %get-tuple-element.15.pay_ref, bf16[2,1552,128]{2,1,0:T(8,128)(2,1)S(1)} %collective-permute-done.partner_ref, ...), custom_call_target="tpu_custom_call", output_to_operand_aliasing={{0}: (2, {})} | custom-call | flops 4294967296 | bytes 3686400 | tf_op jit(solution)/shard_map/pallas_call | solution.py:35
  42.0 0.4 collective-permute-done.2.third_ref
  42.4 0.2 collective-permute-start.3
  42.5 7.9 %shard_map.121.acc_in = f32[2,2048,128]{2,1,0:T(8,128)S(1)} custom-call(f32[2,8,128]{2,1,0:T(8,128)S(1)} %get-tuple-element.17.row_ref, bf16[2,2048,64]{2,1,0:T(8,128)(2,1)S(1)} %get-tuple-element.18.left_ref, bf16[2,1552,128]{2,1,0:T(8,128)(2,1)S(1)} %collective-permute-done.5.full_ref, ...), custom_call_target="tpu_custom_call", output_to_operand_aliasing={{}: (4, {})} | custom-call | flops 8589934592 | bytes 4218880 | tf_op jit(solution)/shard_map/pallas_call | solution.py:35
  50.5 10.2 %shard_map.122.acc_in = f32[2,2048,128]{2,1,0:T(8,128)S(1)} custom-call(f32[2,8,128]{2,1,0:T(8,128)S(1)} %get-tuple-element.17.row_ref, bf16[2,2048,64]{2,1,0:T(8,128)(2,1)S(1)} %get-tuple-element.18.left_ref, bf16[2,1552,128]{2,1,0:T(8,128)(2,1)S(1)} %collective-permute-done.1.full_ref, ...), custom_call_target="tpu_custom_call", output_to_operand_aliasing={{}: (4, {})} | custom-call | flops 8589934592 | bytes 4218880 | tf_op jit(solution)/shard_map/pallas_call | solution.py:35
  60.7 0.0 copy-start.2
  60.7 0.0 copy-start.4
  60.7 0.0 copy-start.9
  60.7 3.0 %shard_map.123 = (f32[2,2048,128]{2,1,0:T(8,128)S(1)}, bf16[2048,128]{1,0:T(8,128)(2,1)S(1)}) custom-call(f32[2,8,128]{2,1,0:T(8,128)S(1)} %get-tuple-element.17.row_ref, bf16[2,2048,64]{2,1,0:T(8,128)(2,1)S(1)} %get-tuple-element.18.left_ref, bf16[2,1552,128]{2,1,0:T(8,128)(2,1)S(1)} %collective-permute-done.2.third_ref, ...), custom_call_target="tpu_custom_call", output_to_operand_aliasing={{0}: (4, {})} | custom-call | flops 4294967296 | bytes 4218880 | tf_op jit(solution)/shard_map/pallas_call | solution.py:35
  63.7 0.0 copy-start
  63.7 0.4 collective-permute-start.7
  64.2 0.2 collective-permute-start.13
  64.4 1.9 %collective-permute-done.13.got_ref = bf16[1792,128]{1,0:T(8,128)(2,1)S(1)} collective-permute-done((bf16[1792,128]{1,0:T(8,128)(2,1)S(1)}, bf16[1792,128]{1,0:T(8,128)(2,1)S(1)}, u32[]{:S(2)}, u32[]{:S(2)}) %collective-permute-start.13) | collective-permute-done | bytes 458784 | tf_op jit(solution)/shard_map/ppermute | solution.py:459
  66.3 2.1 %shard_map.127.local_ref = bf16[256,128]{1,0:T(8,128)(2,1)S(1)} custom-call(s32[1,8]{1,0:T(1,128)S(1)} %copy-done.9, bf16[1,64,256]{2,1,0:T(8,128)(2,1)S(1)} %bitcast.7, bf16[1,256,256]{2,1,0:T(8,128)(2,1)S(1)} %copy-done.2, bf16[1792,128]{1,0:T(8,128)(2,1)S(1)} %shard_map.126.mine_ref, bf16[1792,128]{1,0:T(8,128)(2,1)S(1)} %collective-permute-done.13.got_ref), custom_call_target="tpu_custom_call" | custom-call | flops 536870912 | bytes 1081376 | tf_op jit(solution)/shard_map/pallas_call | solution.py:35
  68.5 1.4 %shard_map.128 = f32[2048,128]{1,0:T(8,128)} custom-call(bf16[2,1552,128]{2,1,0:T(8,128)(2,1)S(1)} %get-tuple-element.15.pay_ref, f32[2,2048,128]{2,1,0:T(8,128)S(1)} %get-tuple-element.20.acc_ref, bf16[2048,128]{1,0:T(8,128)(2,1)S(1)} %collective-permute-done.7.returned_ref, f32[2048,128]{1,0:T(8,128)S(1)} %get-tuple-element.22.base_ref, ...), custom_call_target="tpu_custom_call" | custom-call | flops 134217728 | bytes 5579264 | tf_op jit(solution)/shard_map/pallas_call | solution.py:35
  (27 shorter events, 0.1 us)
Async XLA Ops:
  0.0 20.9 %copy-start.3 = (bf16[1,256,64]{1,2,0:T(8,128)(2,1)S(1)}, bf16[1,256,64]{1,2,0:T(8,128)(2,1)}, u32[]{:S(2)}) copy-start(bf16[1,256,64]{1,2,0:T(8,128)(2,1)} %param.20) | copy-start | bytes 98308
  0.0 32.8 %copy-start.1 = (f32[2048,128]{1,0:T(8,128)S(1)}, f32[2048,128]{1,0:T(8,128)}, u32[]{:S(2)}) copy-start(f32[2048,128]{1,0:T(8,128)} %iterate_ref.1) | copy-start | bytes 3145732
  0.0 20.9 %copy-start.8 = (s32[1,4]{1,0:T(1,128)S(1)}, s32[1,4]{1,0:T(1,128)}, u32[]{:S(2)}) copy-start(s32[1,4]{1,0:T(1,128)} %far_ref.2) | copy-start | bytes 52
  0.0 32.8 %copy-start.5 = (f32[128]{0:T(128)S(1)}, f32[128]{0:T(128)}, u32[]{:S(2)}) copy-start(f32[128]{0:T(128)} %param.16) | copy-start | bytes 1540
  0.0 32.8 %copy-start.7 = (s32[1,2048]{1,0:T(1,128)S(1)}, s32[1,2048]{1,0:T(1,128)}, u32[]{:S(2)}) copy-start(s32[1,2048]{1,0:T(1,128)} %order_ref.1) | copy-start | bytes 24580
  0.0 32.8 %copy-start.6 = (f32[2048,128]{1,0:T(8,128)S(1)}, f32[2048,128]{1,0:T(8,128)}, u32[]{:S(2)}) copy-start(f32[2048,128]{1,0:T(8,128)} %target_ref.1) | copy-start | bytes 3145732
  2.6 19.8 %collective-permute-start.5 = (bf16[2,1552,128]{2,1,0:T(8,128)(2,1)S(1)}, bf16[2,1552,128]{2,1,0:T(8,128)(2,1)S(1)}, u32[]{:S(2)}, u32[]{:S(2)}) collective-permute-start(bf16[2,1552,128]{2,1,0:T(8,128)(2,1)S(1)} %get-tuple-element.15.pay_ref), channel_id=1, source_target_pairs={{0,2},{2,4},{3,1},{4,6},{5,3},{7,5},{8,10},{10,12},{11,9},{12,14},... | collective-permute-start | bytes 2383880 | tf_op jit(solution)/shard_map/ppermute | solution.py:459
  6.1 19.0 %collective-permute-start.1 = (bf16[2,1552,128]{2,1,0:T(8,128)(2,1)S(1)}, bf16[2,1552,128]{2,1,0:T(8,128)(2,1)S(1)}, u32[]{:S(2)}, u32[]{:S(2)}) collective-permute-start(bf16[2,1552,128]{2,1,0:T(8,128)(2,1)S(1)} %get-tuple-element.15.pay_ref), channel_id=1, source_target_pairs={{1,2},{2,1},{3,4},{4,3},{5,6},{6,5},{9,10},{10,9},{11,12},{12,11},... | collective-permute-start | bytes 2383880 | tf_op jit(solution)/shard_map/ppermute | solution.py:459
  8.0 31.0 %collective-permute-start = (bf16[2,1552,128]{2,1,0:T(8,128)(2,1)S(1)}, bf16[2,1552,128]{2,1,0:T(8,128)(2,1)S(1)}, u32[]{:S(2)}, u32[]{:S(2)}) collective-permute-start(bf16[2,1552,128]{2,1,0:T(8,128)(2,1)S(1)} %get-tuple-element.15.pay_ref), channel_id=1, source_target_pairs={{0,1},{1,0},{2,3},{3,2},{4,5},{5,4},{6,7},{7,6},{8,9},{9,8},{10,11... | collective-permute-start | bytes 2383880 | tf_op jit(solution)/shard_map/ppermute | solution.py:459
  9.7 6.6 %collective-permute-start.10 = (bf16[384,128]{1,0:T(8,128)(2,1)S(1)}, bf16[384,128]{1,0:T(8,128)(2,1)S(1)}, u32[]{:S(2)}, u32[]{:S(2)}) collective-permute-start(bf16[384,128]{1,0:T(8,128)(2,1)S(1)} %get-tuple-element.24.own_ref), channel_id=1, source_target_pairs={{0,24},{8,16},{16,8},{24,0},{1,25},{9,17},{17,9},{25,1},{2,26},{10... | collective-permute-start | bytes 294920 | tf_op jit(solution)/shard_map/ppermute | solution.py:459
  10.2 6.6 %collective-permute-start.8 = (bf16[384,128]{1,0:T(8,128)(2,1)S(1)}, bf16[384,128]{1,0:T(8,128)(2,1)S(1)}, u32[]{:S(2)}, u32[]{:S(2)}) collective-permute-start(bf16[384,128]{1,0:T(8,128)(2,1)S(1)} %get-tuple-element.24.own_ref), channel_id=1, source_target_pairs={{0,8},{8,0},{16,24},{24,16},{1,9},{9,1},{17,25},{25,17},{2,10},{10... | collective-permute-start | bytes 294920 | tf_op jit(solution)/shard_map/ppermute | solution.py:459
  16.3 4.6 %collective-permute-start.9 = (bf16[384,128]{1,0:T(8,128)(2,1)S(1)}, bf16[384,128]{1,0:T(8,128)(2,1)S(1)}, u32[]{:S(2)}, u32[]{:S(2)}) collective-permute-start(bf16[384,128]{1,0:T(8,128)(2,1)S(1)} %get-tuple-element.24.own_ref), channel_id=1, source_target_pairs={{0,16},{8,24},{16,0},{24,8},{1,17},{9,25},{17,1},{25,9},{2,18},{10... | collective-permute-start | bytes 294920 | tf_op jit(solution)/shard_map/ppermute | solution.py:459
  22.3 16.5 %collective-permute-start.11 = (bf16[640,128]{1,0:T(8,128)(2,1)S(1)}, bf16[640,128]{1,0:T(8,128)(2,1)S(1)}, u32[]{:S(2)}, u32[]{:S(2)}) collective-permute-start(bf16[640,128]{1,0:T(8,128)(2,1)S(1)} %shard_map.124.mine_ref), channel_id=1, source_target_pairs={{0,4},{1,5},{2,6},{3,7},{4,0},{5,1},{6,2},{7,3},{8,12},{9,13},{10,... | collective-permute-start | bytes 491528 | tf_op jit(solution)/shard_map/ppermute | solution.py:459
  22.4 20.2 %collective-permute-start.6 = (bf16[2,1552,128]{2,1,0:T(8,128)(2,1)S(1)}, bf16[2,1552,128]{2,1,0:T(8,128)(2,1)S(1)}, u32[]{:S(2)}, u32[]{:S(2)}) collective-permute-start(bf16[2,1552,128]{2,1,0:T(8,128)(2,1)S(1)} %collective-permute-done.5.full_ref), channel_id=1, source_target_pairs={{0,1},{1,0},{2,3},{3,2},{4,5},{5,4},{6,7},{7,6},{8,9},{9,8},{10,11... | collective-permute-start | bytes 2383880 | tf_op jit(solution)/shard_map/ppermute | solution.py:459
  25.1 17.3 %collective-permute-start.2 = (bf16[2,1552,128]{2,1,0:T(8,128)(2,1)S(1)}, bf16[2,1552,128]{2,1,0:T(8,128)(2,1)S(1)}, u32[]{:S(2)}, u32[]{:S(2)}) collective-permute-start(bf16[2,1552,128]{2,1,0:T(8,128)(2,1)S(1)} %collective-permute-done.1.full_ref), channel_id=1, source_target_pairs={{0,2},{2,4},{3,1},{4,6},{5,3},{7,5},{8,10},{10,12},{11,9},{12,14},... | collective-permute-start | bytes 2383880 | tf_op jit(solution)/shard_map/ppermute | solution.py:459
  38.8 25.3 %collective-permute-start.12 = (bf16[1024,128]{1,0:T(8,128)(2,1)S(1)}, bf16[1024,128]{1,0:T(8,128)(2,1)S(1)}, u32[]{:S(2)}, u32[]{:S(2)}) collective-permute-start(bf16[1024,128]{1,0:T(8,128)(2,1)S(1)} %shard_map.125.mine_ref), channel_id=1, source_target_pairs={{0,2},{1,3},{2,0},{3,1},{4,6},{5,7},{6,4},{7,5},{8,10},{9,11},{10,... | collective-permute-start | bytes 786440 | tf_op jit(solution)/shard_map/ppermute | solution.py:459
  38.9 11.5 %collective-permute-start.4 = (bf16[2,1552,128]{2,1,0:T(8,128)(2,1)S(1)}, bf16[2,1552,128]{2,1,0:T(8,128)(2,1)S(1)}, u32[]{:S(2)}, u32[]{:S(2)}) collective-permute-start(bf16[2,1552,128]{2,1,0:T(8,128)(2,1)S(1)} %collective-permute-done.1.full_ref), channel_id=1, source_target_pairs={{0,1},{1,0},{2,3},{3,2},{4,5},{5,4},{6,7},{7,6},{8,9},{9,8},{10,11... | collective-permute-start | bytes 2383880 | tf_op jit(solution)/shard_map/ppermute | solution.py:459
  42.4 18.3 %collective-permute-start.3 = (bf16[2,1552,128]{2,1,0:T(8,128)(2,1)S(1)}, bf16[2,1552,128]{2,1,0:T(8,128)(2,1)S(1)}, u32[]{:S(2)}, u32[]{:S(2)}) collective-permute-start(bf16[2,1552,128]{2,1,0:T(8,128)(2,1)S(1)} %collective-permute-done.2.third_ref), channel_id=1, source_target_pairs={{0,1},{1,0},{2,3},{3,2},{4,5},{5,4},{6,7},{7,6},{8,9},{9,8},{10,11... | collective-permute-start | bytes 2383880 | tf_op jit(solution)/shard_map/ppermute | solution.py:459
  60.7 5.7 %copy-start.2 = (bf16[1,256,256]{2,1,0:T(8,128)(2,1)S(1)}, bf16[1,256,256]{2,1,0:T(8,128)(2,1)}, u32[]{:S(2)}) copy-start(bf16[1,256,256]{2,1,0:T(8,128)(2,1)} %transfer_ref.1) | copy-start | bytes 393220
  60.7 5.7 %copy-start.4 = (bf16[1,256,64]{1,2,0:T(8,128)(2,1)S(1)}, bf16[1,256,64]{1,2,0:T(8,128)(2,1)}, u32[]{:S(2)}) copy-start(bf16[1,256,64]{1,2,0:T(8,128)(2,1)} %param.19) | copy-start | bytes 98308
  60.7 5.7 %copy-start.9 = (s32[1,8]{1,0:T(1,128)S(1)}, s32[1,8]{1,0:T(1,128)}, u32[]{:S(2)}) copy-start(s32[1,8]{1,0:T(1,128)} %far_ref.3) | copy-start | bytes 100
  63.7 4.8 %copy-start = (bf16[2048,256]{1,0:T(8,128)(2,1)S(1)}, bf16[2048,256]{1,0:T(8,128)(2,1)}, u32[]{:S(2)}) copy-start(bf16[2048,256]{1,0:T(8,128)(2,1)} %basis_ref.1) | copy-start | bytes 3145732
  63.7 4.7 %collective-permute-start.7 = (bf16[2048,128]{1,0:T(8,128)(2,1)S(1)}, bf16[2048,128]{1,0:T(8,128)(2,1)S(1)}, u32[]{:S(2)}, u32[]{:S(2)}) collective-permute-start(bf16[2048,128]{1,0:T(8,128)(2,1)S(1)} %get-tuple-element.21), channel_id=1, source_target_pairs={{0,1},{1,0},{2,3},{3,2},{4,5},{5,4},{6,7},{7,6},{8,9},{9,8},{10,11... | collective-permute-start | bytes 1572872 | tf_op jit(solution)/shard_map/ppermute | solution.py:459
  64.2 2.2 %collective-permute-start.13 = (bf16[1792,128]{1,0:T(8,128)(2,1)S(1)}, bf16[1792,128]{1,0:T(8,128)(2,1)S(1)}, u32[]{:S(2)}, u32[]{:S(2)}) collective-permute-start(bf16[1792,128]{1,0:T(8,128)(2,1)S(1)} %shard_map.126.mine_ref), channel_id=1, source_target_pairs={{0,1},{1,0},{2,3},{3,2},{4,5},{5,4},{6,7},{7,6},{8,9},{9,8},{10,11... | collective-permute-start | bytes 1376264 | tf_op jit(solution)/shard_map/ppermute | solution.py:459
